TPU v7x, 1024 devices: a whole 8x8x8 slice. The times are simulated.
1024 devices in a mesh: ctx: 32 (over z, x_lo), head: 32 (over x_hi, y, core).
Axes of the slice: x: 8 (x_hi: 2, x_lo: 4; x = x_hi * 4 + x_lo), y: 8, z: 8, core: 2. Of those that a mesh axis runs over, the one named last changes fastest.
Arguments:
- compressed: bfloat16 [8192, 576], P('ctx'), may hold values from -6 to 6
- query: bfloat16 [8192, 24576], P('ctx', 'head'), may hold values from -6 to 6
- out_grad: bfloat16 [8192, 16384], P('ctx', 'head'), may hold values from -6 to 6
- up_weight: bfloat16 [512, 32768], P(None, 'head'), may hold values from -0.25 to 0.25
- lengths: int32 [96], replicated, may hold values from 1 to 256, 8192 in all
Outputs:
- grad_query: bfloat16 [8192, 24576], P('ctx', 'head')
- grad_compressed: float32 [8192, 576], P(('ctx', 'head'))
- grad_up_weight: float32 [512, 32768], P('ctx', 'head')
Inputs may be any that keep to these rules, and one draw needn't show every extreme that they name: The lengths sum to 8192; the longest document has exactly 256 tokens.
All inputs are finite; a program needn't handle non-finite values.
Results may differ from a plain program's by a relative error of at most 0.025.
Values may be sent and summed in bfloat16 or wider, within the bound.
No kernel may reach another device: no remote copies, remote signals or barrier semaphores. Data moves between devices by JAX's collectives and lax.ppermute only.
A program may use at most 32 MiB of HBM per device.

v0:
```python
import math

import jax
import jax.numpy as jnp
from jax import lax
from jax.sharding import PartitionSpec as P

LATENT = 512
ROPE = 64
NOPE = 128
VDIM = 128


def from_behind(x, axis, by):
    devices = lax.axis_size(axis)
    pairs = [(i, i + by) for i in range(devices) if 0 <= i + by < devices]
    return lax.ppermute(x, axis, pairs)


def project_back(grads, up_weight):
    return jnp.einsum("sk,lk->sl", grads, up_weight, preferred_element_type=jnp.float32)


def head_reduce(total):
    return lax.psum_scatter(
        total.astype(jnp.bfloat16), "head", scatter_dimension=0, tiled=True
    ).astype(jnp.float32)


def body(compressed, query, out_grad, up_weight, lengths):
    tok_rows = compressed.shape[0]
    head_width = NOPE + ROPE
    pair_width = NOPE + VDIM
    heads_here = query.shape[1] // head_width
    scaling = 1.0 / math.sqrt(head_width)
    ctx_rank = lax.axis_index("ctx")
    first_pos = ctx_rank * tok_rows
    ends = jnp.cumsum(lengths)
    query_pos = first_pos + jnp.arange(tok_rows, dtype=jnp.int32)
    key_pos = first_pos - tok_rows + jnp.arange(2 * tok_rows, dtype=jnp.int32)
    query_start = jnp.sum(
        jnp.where(ends[None, :] <= query_pos[:, None], lengths[None, :], 0), axis=1
    )
    visible = (key_pos[None, :] >= query_start[:, None]) & (key_pos[None, :] <= query_pos[:, None])
    own_latent = compressed[:, :LATENT]
    own_rope = compressed[:, LATENT:]
    own_kv = jnp.dot(own_latent, up_weight, preferred_element_type=jnp.float32).astype(jnp.bfloat16)
    prev_kv, prev_rope = from_behind((own_kv, own_rope), "ctx", 1)
    keys_values = jnp.concatenate([prev_kv, own_kv], axis=0).reshape(
        2 * tok_rows, heads_here, pair_width
    )
    key_rope = jnp.concatenate([prev_rope, own_rope], axis=0)
    key_nope = keys_values[:, :, :NOPE]
    values = keys_values[:, :, NOPE:]
    queries = query.reshape(tok_rows, heads_here, head_width)
    query_nope = queries[:, :, :NOPE]
    query_rope = queries[:, :, NOPE:]
    grads_out = out_grad.reshape(tok_rows, heads_here, VDIM)
    scores = (
        jnp.einsum("thd,shd->hts", query_nope, key_nope, preferred_element_type=jnp.float32)
        + jnp.einsum("thd,sd->hts", query_rope, key_rope, preferred_element_type=jnp.float32)
    ) * scaling
    weights = jnp.where(visible[None], jnp.exp(scores), 0.0)
    probs = weights / jnp.sum(weights, axis=-1, keepdims=True)
    probs_b = probs.astype(jnp.bfloat16)
    attended = jnp.einsum(
        "hts,shd->thd", probs_b, values, preferred_element_type=jnp.float32
    ).astype(jnp.bfloat16)
    delta = jnp.sum(grads_out.astype(jnp.float32) * attended.astype(jnp.float32), axis=-1)
    prob_grad = jnp.einsum("thd,shd->hts", grads_out, values, preferred_element_type=jnp.float32)
    score_grad = (probs * (prob_grad - jnp.transpose(delta)[:, :, None]) * scaling).astype(
        jnp.bfloat16
    )
    grad_nope = jnp.einsum("hts,shd->thd", score_grad, key_nope, preferred_element_type=jnp.float32)
    grad_rope = jnp.einsum("hts,sd->thd", score_grad, key_rope, preferred_element_type=jnp.float32)
    grad_query = (
        jnp.concatenate([grad_nope, grad_rope], axis=-1)
        .reshape(tok_rows, heads_here * head_width)
        .astype(jnp.bfloat16)
    )
    key_grad = jnp.einsum(
        "hts,thd->shd", score_grad, query_nope, preferred_element_type=jnp.float32
    )
    rope_grad = jnp.einsum(
        "hts,thd->sd", score_grad, query_rope, preferred_element_type=jnp.float32
    )
    value_grad = jnp.einsum("hts,thd->shd", probs_b, grads_out, preferred_element_type=jnp.float32)
    kv_grads = (
        jnp.concatenate([key_grad, value_grad], axis=-1)
        .reshape(2 * tok_rows, heads_here * pair_width)
        .astype(jnp.bfloat16)
    )
    back_kv = from_behind(kv_grads[:tok_rows], "ctx", -1)
    back_rope = from_behind(rope_grad[:tok_rows].astype(jnp.bfloat16), "ctx", -1).astype(
        jnp.float32
    )
    keys_latent = jnp.concatenate([own_latent, own_latent], axis=0)
    key_grads_all = jnp.concatenate([kv_grads[tok_rows:], back_kv], axis=0)
    latent_grad = project_back(kv_grads[tok_rows:], up_weight) + project_back(back_kv, up_weight)
    total = jnp.concatenate([latent_grad, rope_grad[tok_rows:] + back_rope], axis=1)
    reduced = head_reduce(total)
    grad_weight = lax.psum_scatter(
        jnp.einsum(
            "sl,sk->lk", keys_latent, key_grads_all, preferred_element_type=jnp.float32
        ).astype(jnp.bfloat16),
        "ctx",
        scatter_dimension=0,
        tiled=True,
    ).astype(jnp.float32)
    return (grad_query, reduced, grad_weight)


def solution(mesh):
    placed = (P("ctx", None), P("ctx", "head"), P("ctx", "head"), P(None, "head"), P())
    return jax.shard_map(
        body,
        mesh=mesh,
        in_specs=placed,
        out_specs=(P("ctx", "head"), P(("ctx", "head"), None), P("ctx", "head")),
        check_vma=False,
    )
```

profile of v0, /device:TPU:2, one launch (start us, length us, event | category | flops | bytes accessed | tf_op | source)
XLA Modules:
  0.0 413.9 jit_solution(16838097383341894438)
XLA Ops:
  8.1 1.1 copy-done
  9.2 1.4 convolution_convert_fusion.3
  10.6 3.4 collective-permute-start
  14.8 3.4 collective-permute-start.1
  18.2 0.9 copy.86
  19.8 0.8 compare_and_fusion
  20.6 11.6 %collective-permute-done = bf16[256,1024]{1,0:T(8,128)(2,1)S(1)} collective-permute-done((bf16[256,1024]{1,0:T(8,128)(2,1)S(1)}, bf16[256,1024]{1,0:T(8,128)(2,1)S(1)}, u32[]{:S(2)}, u32[]{:S(2)}) %collective-permute-start) | collective-permute-done | bytes 524320 | tf_op jit(solution)/shard_map/ppermute | solution.py:17
  32.3 0.8 reshape.110
  33.1 1.2 fusion.39
  34.3 1.8 fusion.28
  36.1 2.5 fusion.18
  39.1 0.9 copy-done.4
  40.4 2.1 fusion.1
  43.0 0.9 pad_maximum_fusion.1
  43.9 1.9 collective-permute-start.2
  46.2 1.9 collective-permute-start.3
  48.7 6.8 %collective-permute-done.3 = bf16[256,64]{0,1:T(8,128)(2,1)S(1)} collective-permute-done((bf16[256,64]{0,1:T(8,128)(2,1)S(1)}, bf16[256,64]{0,1:T(8,128)(2,1)S(1)}, u32[]{:S(2)}, u32[]{:S(2)}) %collective-permute-start.3) | collective-permute-done | bytes 32800 | tf_op jit(solution)/shard_map/ppermute | solution.py:17
  55.6 1.5 fusion.7
  58.0 2.8 convolution_convert_fusion
  60.8 1.3 dynamic-slice
  63.5 0.9 copy.101
  64.4 339.4 %all-reduce.3.cloned.1.call-done = bf16[256,576]{1,0:T(8,128)(2,1)} async-done(((bf16[256,576]{1,0:T(8,128)(2,1)}), bf16[256,576]{1,0:T(8,128)(2,1)}) %all-reduce.3.cloned.1.call-update) | async-done | bytes 294928
  403.8 1.3 dynamic-slice_convert_fusion
  405.1 1.4 convert_element_type.53
  (52 shorter events, 5.4 us)
Async XLA Ops:
  8.0 1.2 copy-start
  8.0 10.2 %copy-start.7 = (bf16[256,768]{1,0:T(8,128)(2,1)S(1)}, bf16[256,768]{1,0:T(8,128)(2,1)}, u32[]{:S(2)}) copy-start(bf16[256,768]{1,0:T(8,128)(2,1)} %param.6) | copy-start | bytes 1179652
  8.0 11.1 %copy-start.11 = (s32[96]{0:T(128)S(1)}, s32[96]{0:T(128)}, u32[]{:S(2)}) copy-start(s32[96]{0:T(128)} %param.9) | copy-start | bytes 1156
  8.0 11.5 %copy-start.8 = (bf16[256,512]{1,0:T(8,128)(2,1)S(1)}, bf16[256,512]{1,0:T(8,128)(2,1)}, u32[]{:S(2)}) copy-start(bf16[256,512]{1,0:T(8,128)(2,1)} %param.7) | copy-start | bytes 786436
  8.0 395.8 %all-reduce.3.cloned.1.call-start = ((), (), s32[]{:S(2)}) async-start(), calls=%async_computation.2 | async-start | bytes 655360
  10.6 21.6 %collective-permute-start = (bf16[256,1024]{1,0:T(8,128)(2,1)S(1)}, bf16[256,1024]{1,0:T(8,128)(2,1)S(1)}, u32[]{:S(2)}, u32[]{:S(2)}) collective-permute-start(bf16[256,1024]{1,0:T(8,128)(2,1)S(1)} %convolution_convert_fusion.3), channel_id=1, source_target_pairs={{0,32},{32,64},{64,96},{96,128},{128,160},{160,192},{192,224},{224... | collective-permute-start | bytes 1572872 | tf_op jit(solution)/shard_map/ppermute | solution.py:17
  14.8 21.2 %collective-permute-start.1 = (bf16[256,64]{0,1:T(8,128)(2,1)S(1)}, bf16[256,64]{0,1:T(8,128)(2,1)S(1)}, u32[]{:S(2)}, u32[]{:S(2)}) collective-permute-start(bf16[256,64]{0,1:T(8,128)(2,1)S(1)} %slice.41), channel_id=1, source_target_pairs={{0,32},{32,64},{64,96},{96,128},{128,160},{160,192},{192,224},{224... | collective-permute-start | bytes 98312 | tf_op jit(solution)/shard_map/ppermute | solution.py:17
  33.1 1.2 copy-start.5
  34.3 1.8 copy-start.2
  36.1 2.5 copy-start.9
  38.6 1.8 copy-start.1
  38.6 1.4 copy-start.4
  40.4 2.1 copy-start.6
  43.9 11.8 %collective-permute-start.2 = (bf16[256,1024]{0,1:T(8,128)(2,1)}, bf16[256,1024]{0,1:T(8,128)(2,1)}, u32[]{:S(2)}, u32[]{:S(2)}) collective-permute-start(bf16[256,1024]{0,1:T(8,128)(2,1)} %bitcast.15), channel_id=1, source_target_pairs={{32,0},{64,32},{96,64},{128,96},{160,128},{192,160},{224,192},{256... | collective-permute-start | bytes 1572872 | tf_op jit(solution)/shard_map/ppermute | solution.py:17
  46.2 9.3 %collective-permute-start.3 = (bf16[256,64]{0,1:T(8,128)(2,1)S(1)}, bf16[256,64]{0,1:T(8,128)(2,1)S(1)}, u32[]{:S(2)}, u32[]{:S(2)}) collective-permute-start(bf16[256,64]{0,1:T(8,128)(2,1)S(1)} %slice.78), channel_id=1, source_target_pairs={{32,0},{64,32},{96,64},{128,96},{160,128},{192,160},{224,192},{256... | collective-permute-start | bytes 98312 | tf_op jit(solution)/shard_map/ppermute | solution.py:17
  48.7 9.4 %slice-start = ((bf16[256,576]{0,1:T(8,128)(2,1)}), bf16[256,512]{0,1:T(8,128)(2,1)S(1)}, s32[]{:S(2)}) async-start(bf16[256,576]{0,1:T(8,128)(2,1)} %param.5), calls=%async_computation.3 | async-start | bytes 524288 | tf_op jit(solution)/shard_map/slice | solution.py:45
  58.0 347.1 %reduce-scatter.2.cloned.1.call-start = ((), (), s32[]{:S(2)}) async-start(), calls=%async_computation.1 | async-start | bytes 1081344 | tf_op jit(solution)/shard_map/reduce_scatter | solution.py:102
  58.0 4.8 %copy-start.10 = (bf16[256,64]{0,1:T(8,128)(2,1)S(1)}, bf16[256,64]{0,1:T(8,128)(2,1)}, u32[]{:S(2)}) copy-start(bf16[256,64]{0,1:T(8,128)(2,1)} %copy-done.9) | copy-start | bytes 98308
  60.8 2.3 copy-start.3
Sparse Core Ops, SparseCore 0:
  58.1 345.6 all-reduce.2
Sparse Core Ops, SparseCore 1:
  61.8 176.1 reduce-scatter.1
where the time goes:
time: 415 us; the launch traced here: 414 us
  waiting for transfers between devices  358 us (86%)
  between operations  16.5 us (4%)
  matrix products  14.9 us (4%)
  starting transfers between devices  10.7 us (3%)
  local copies, waits for them, and re-layouts  8.38 us (2%)
  other arithmetic  5.61 us (1%)
    unnamed x3, waiting for transfers between devices  339 us
    ppermute x4, waiting for transfers between devices, from_behind(): return lax.ppermute(x, axis, pairs)  18.5 us
    ppermute x4, starting transfers between devices, from_behind(): return lax.ppermute(x, axis, pairs)  10.6 us
  transfers between devices with their start and end apart: 6, of which 3 were waited for; matrix products, arithmetic and copies ran while one was open for 4% of the time, Pallas kernels for 0%

commit v1 on v0

v1 whole, which is shorter than its diff:
```python
import math

import jax
import jax.numpy as jnp
from jax import lax
from jax.sharding import Mesh
from jax.sharding import PartitionSpec as P

LATENT = 512
ROPE = 64
NOPE = 128
VDIM = 128
CTX = ("zh", "z0", "x1", "x0")
HEAD = ("xh", "y", "core")
F32 = jnp.float32
BF16 = jnp.bfloat16


def ctx_shift(x, by):
    pairs = [(i, i + by) for i in range(32) if 0 <= i + by < 32]
    return lax.ppermute(x, CTX, pairs)


def quad_partner(x, dz, dx):
    pairs = [(i, i ^ (4 * dz) ^ dx) for i in range(32)]
    return lax.ppermute(x, CTX, pairs)


def attention_grads(own, prev, query, out_grad, up_weight, lengths, ctx_rank):
    tok = own.shape[0]
    width = NOPE + ROPE
    heads = query.shape[1] // width
    scaling = 1.0 / math.sqrt(width)
    first_pos = ctx_rank * tok
    ends = jnp.cumsum(lengths)
    query_pos = first_pos + jnp.arange(tok, dtype=jnp.int32)
    key_pos = first_pos - tok + jnp.arange(2 * tok, dtype=jnp.int32)
    start = jnp.sum(jnp.where(ends[None, :] <= query_pos[:, None], lengths[None, :], 0), axis=1)
    visible = (key_pos[None, :] >= start[:, None]) & (key_pos[None, :] <= query_pos[:, None])
    window = jnp.concatenate([prev, own], axis=0)
    kv = jnp.dot(window[:, :LATENT], up_weight, preferred_element_type=F32).astype(BF16)
    kv = kv.reshape(2 * tok, heads, NOPE + VDIM)
    k, v = kv[:, :, :NOPE], kv[:, :, NOPE:]
    kr = window[:, LATENT:]
    q = query.reshape(tok, heads, width)
    qn, qr = q[:, :, :NOPE], q[:, :, NOPE:]
    do = out_grad.reshape(tok, heads, VDIM)
    scores = (
        jnp.einsum("thd,shd->hts", qn, k, preferred_element_type=F32)
        + jnp.einsum("thd,sd->hts", qr, kr, preferred_element_type=F32)
    ) * scaling
    weights = jnp.where(visible[None], jnp.exp(scores), 0.0)
    probs = weights / jnp.sum(weights, axis=-1, keepdims=True)
    probs_b = probs.astype(BF16)
    attended = jnp.einsum("hts,shd->thd", probs_b, v, preferred_element_type=F32).astype(BF16)
    delta = jnp.sum(do.astype(F32) * attended.astype(F32), axis=-1)
    dp = jnp.einsum("thd,shd->hts", do, v, preferred_element_type=F32)
    ds = (probs * (dp - jnp.transpose(delta)[:, :, None]) * scaling).astype(BF16)
    dqn = jnp.einsum("hts,shd->thd", ds, k, preferred_element_type=F32)
    dqr = jnp.einsum("hts,sd->thd", ds, kr, preferred_element_type=F32)
    dq = jnp.concatenate([dqn, dqr], axis=-1).reshape(tok, heads * width).astype(BF16)
    dk = jnp.einsum("hts,thd->shd", ds, qn, preferred_element_type=F32)
    dr = jnp.einsum("hts,thd->sd", ds, qr, preferred_element_type=F32)
    dv = jnp.einsum("hts,thd->shd", probs_b, do, preferred_element_type=F32)
    dkv = jnp.concatenate([dk, dv], axis=-1).reshape(2 * tok, heads * (NOPE + VDIM)).astype(BF16)
    return dq, dkv, dr, window


def body(compressed, query, out_grad, up_weight, lengths):
    ctx_rank = lax.axis_index(CTX)
    core = lax.axis_index("core")
    z0, x0 = lax.axis_index("z0"), lax.axis_index("x0")
    prev = ctx_shift(compressed, 1)
    dq, dkv, dr, window = attention_grads(
        compressed, prev, query, out_grad, up_weight, lengths, ctx_rank
    )

    latent = jnp.einsum("sk,lk->sl", dkv, up_weight, preferred_element_type=F32)
    total = jnp.concatenate([latent, dr], axis=1).reshape(2, 16, 2, 8, LATENT + ROPE)
    mine = lax.dynamic_index_in_dim(total, core, 2, keepdims=False)
    theirs = lax.dynamic_index_in_dim(total, 1 - core, 2, keepdims=False).astype(BF16)
    got = lax.ppermute(theirs, "core", [(0, 1), (1, 0)])
    pair = mine + got.astype(F32)
    back = ctx_shift(pair[0].astype(BF16), -1)
    part = (pair[1] + back.astype(F32)).astype(BF16)

    cols = window[:, :LATENT].reshape(512, 4, 2, 2, 2, 16)

    def piece(a, b):
        sel = lax.dynamic_index_in_dim(cols, a, 2, keepdims=False)
        sel = lax.dynamic_index_in_dim(sel, b, 3, keepdims=False).reshape(512, 128)
        return jnp.einsum("sl,sk->lk", sel, dkv, preferred_element_type=F32)

    got_x = quad_partner(piece(z0, 1 - x0).astype(BF16), 0, 1)
    got_z = quad_partner(piece(1 - z0, x0).astype(BF16), 1, 0)
    got_d = quad_partner(piece(1 - z0, 1 - x0).astype(BF16), 1, 1)
    quad = piece(z0, x0) + got_x.astype(F32) + got_z.astype(F32) + got_d.astype(F32)

    parts = lax.all_to_all(part, ("xh", "y"), 0, 0)
    grad_compressed = jnp.sum(parts.astype(F32), axis=0)
    eighths = lax.all_to_all(quad.astype(BF16).reshape(8, 16, -1), ("zh", "x1"), 0, 0)
    grad_weight = jnp.sum(eighths.astype(F32), axis=0)
    return dq, grad_compressed, grad_weight


def solution(mesh):
    fine = Mesh(
        mesh.devices.reshape(4, 2, 2, 2, 2, 8, 2), ("zh", "z0", "x1", "x0", "xh", "y", "core")
    )
    placed = (P(CTX, None), P(CTX, HEAD), P(CTX, HEAD), P(None, HEAD), P())
    return jax.shard_map(
        body,
        mesh=fine,
        in_specs=placed,
        out_specs=(P(CTX, HEAD), P(CTX + HEAD, None), P(CTX, HEAD)),
        check_vma=False,
    )
```

time: 415 us -> 119 us (0.29)
  waiting for transfers between devices: 358 us -> 35.9 us
  starting transfers between devices: 10.7 us -> 43.7 us
  between operations: 16.5 us -> 1.05 us
  local copies, waits for them, and re-layouts: 8.38 us -> 14.1 us
    unnamed x3 -> x0, waiting for transfers between devices: 339 us -> none
    all_to_all x0 -> x2, starting transfers between devices: none -> 27.1 us  [the longest x1 19.7 us: body(): lax.all_to_all(quad.astype(BF16).reshape(8, 16, -1), ('zh', 'x1'), 0, 0)]
    all_to_all x0 -> x2, waiting for transfers between devices: none -> 17.1 us  [the longest x1 10.2 us: body(): parts = lax.all_to_all(part, ('xh', 'y'), 0, 0)]
    ppermute x4 -> x6, starting transfers between devices: 10.6 us -> 16.5 us  [the longest x3 9.18 us: quad_partner(): return lax.ppermute(x, CTX, pairs)]
    dot_general x12 -> x14, matrix products: 12.4 us -> 15.4 us  [the longest x4 5.91 us: piece(): return jnp.einsum('sl,sk->lk', sel, dkv, preferred_element_type=F32)]
    ppermute x4 -> x6, waiting for transfers between devices: 18.5 us -> 18.8 us  [the longest x2 18.8 us: ctx_shift(): return lax.ppermute(x, CTX, pairs)]
  transfers between devices with their start and end apart: 6 -> 8, of which waited for: 3 -> 4; matrix products, arithmetic and copies ran while one was open for 4% -> 16% of each run, Pallas kernels for 0% -> 0%
where the time goes in v1:
time: 119 us; the launch traced here: 118 us
  starting transfers between devices  43.7 us (37%)
  waiting for transfers between devices  35.9 us (30%)
  matrix products  17.9 us (15%)
  local copies, waits for them, and re-layouts  14.1 us (12%)
  other arithmetic  5.4 us (5%)
    all_to_all x1, starting transfers between devices, body(): lax.all_to_all(quad.astype(BF16).reshape(8, 16, -1), ('zh', 'x1'), 0, 0)  19.7 us
    ppermute x2, waiting for transfers between devices, ctx_shift(): return lax.ppermute(x, CTX, pairs)  18.8 us
    all_to_all x1, waiting for transfers between devices, body(): parts = lax.all_to_all(part, ('xh', 'y'), 0, 0)  10.2 us
    ppermute x3, starting transfers between devices, quad_partner(): return lax.ppermute(x, CTX, pairs)  9.18 us
    all_to_all x1, starting transfers between devices, body(): parts = lax.all_to_all(part, ('xh', 'y'), 0, 0)  7.44 us
    all_to_all x1, waiting for transfers between devices, body(): lax.all_to_all(quad.astype(BF16).reshape(8, 16, -1), ('zh', 'x1'), 0, 0)  6.88 us
    dot_general x4, matrix products, piece(): return jnp.einsum('sl,sk->lk', sel, dkv, preferred_element_type=F32)  5.91 us
    ppermute x2, starting transfers between devices, ctx_shift(): return lax.ppermute(x, CTX, pairs)  5.45 us
  transfers between devices with their start and end apart: 8, of which 4 were waited for; matrix products, arithmetic and copies ran while one was open for 16% of the time, Pallas kernels for 0%

profile of v1, /device:TPU:2, one launch (start us, length us, event | category | flops | bytes accessed | tf_op | source)
XLA Modules:
  0.0 118.1 jit_solution(10578758752471327948)
XLA Ops:
  0.7 3.5 %collective-permute-start = (bf16[256,576]{0,1:T(8,128)(2,1)}, bf16[256,576]{0,1:T(8,128)(2,1)S(1)}, u32[]{:S(2)}, u32[]{:S(2)}) collective-permute-start(bf16[256,576]{0,1:T(8,128)(2,1)} %param.5), channel_id=1, source_target_pairs={{0,32},{32,64},{64,96},{96,128},{128,160},{160,192},{192,224},{224... | collective-permute-start | bytes 884744 | tf_op jit(solution)/shard_map/ppermute | solution.py:21
  6.4 1.2 %copy.49 = bf16[256,512]{0,1:T(8,128)(2,1)S(1)} copy(bf16[256,512]{1,0:T(8,128)(2,1)} %param.7) | data formatting | bytes 524288 | tf_op args[2]
  8.6 11.5 %collective-permute-done = bf16[256,576]{0,1:T(8,128)(2,1)S(1)} collective-permute-done((bf16[256,576]{0,1:T(8,128)(2,1)}, bf16[256,576]{0,1:T(8,128)(2,1)S(1)}, u32[]{:S(2)}, u32[]{:S(2)}) %collective-permute-start) | collective-permute-done | bytes 294944 | tf_op jit(solution)/shard_map/ppermute | solution.py:21
  21.1 1.7 %convolution_convert_fusion = bf16[512,1024]{1,0:T(8,128)(2,1)} fusion(bf16[512,1024]{1,0:T(8,128)(2,1)S(1)} %copy-done, bf16[512,576]{0,1:T(8,128)(2,1)S(1)} %constant_dynamic-update-slice_fusion), kind=kOutput, calls=%fused_computation.8 | convolution fusion | flops 537395200 | bytes 2621440 | tf_op jit(solution)/shard_map/dot_general | solution.py:41
  22.8 1.9 %reshape.162 = bf16[512,4,256]{2,1,0:T(4,128)(2,1)S(1)} reshape(bf16[512,1024]{1,0:T(8,128)(2,1)} %convolution_convert_fusion) | data formatting | bytes 2097152 | tf_op jit(solution)/shard_map/reshape | solution.py:42
  26.6 1.8 %fusion.18 = f32[4,512,256]{2,1,0:T(8,128)} fusion(bf16[512,4,128]{2,1,0:T(4,128)(2,1)S(1)} %get-tuple-element.13, bf16[256,4,192]{0,2,1:T(8,128)(2,1)S(1)} %bitcast.94), kind=kOutput, calls=%fused_computation.37 | convolution fusion | flops 134217728 | bytes 2883584 | tf_op jit(solution)/shard_map/thd,shd->hts/dot_general | solution.py:49
  28.4 2.6 %fusion.12 = f32[4,256,512]{1,2,0:T(8,128)S(1)} fusion(f32[4,512,256]{2,1,0:T(8,128)} %fusion.18, pred[256,512]{0,1:T(8,128)(4,1)S(1)} %compare_and_fusion, bf16[256,4,192]{0,2,1:T(8,128)(2,1)} %bitcast.95, bf16[512,576]{0,1:T(8,128)(2,1)} %copy-done.9), kind=kOutput, calls=%fused_computation.26 | convolution fusion | flops 69207552 | bytes 4521984 | tf_op jit(solution)/shard_map/div | solution.py:53
  32.8 2.1 %fusion.1 = bf16[4,256,512]{1,2,0:T(8,128)(2,1)S(1)} fusion(f32[4,256,512]{1,2,0:T(8,128)} %copy-done.1, bf16[256,4,128]{0,2,1:T(8,128)(2,1)S(1)} %bitcast.91, f32[4,256]{1,0:T(4,128)S(1)} %bitcast.105, bf16[512,4,128]{2,1,0:T(4,128)(2,1)S(1)} %copy-done.4), kind=kOutput, calls=%fused_computation.3 | convolution fusion | flops 136314880 | bytes 3936256 | tf_op jit(solution)/shard_map/thd,shd->hts/dot_general | solution.py:57
  37.0 1.2 %convolution_convert_fusion.3 = bf16[128,1024]{1,0:T(8,128)(2,1)} fusion(bf16[512,128]{0,1:T(8,128)(2,1)S(1)} %bitcast.104, bf16[512,1024]{0,1:T(8,128)(2,1)S(1)} %bitcast.85), kind=kOutput, calls=%fused_computation.13 | convolution fusion | flops 134348800 | bytes 1441792 | tf_op jit(solution)/shard_map/sl,sk->lk/dot_general | solution.py:92
  38.2 1.9 %collective-permute-start.3 = (bf16[128,1024]{1,0:T(8,128)(2,1)}, bf16[128,1024]{1,0:T(8,128)(2,1)}, u32[]{:S(2)}, u32[]{:S(2)}) collective-permute-start(bf16[128,1024]{1,0:T(8,128)(2,1)} %convolution_convert_fusion.3), channel_id=1, source_target_pairs={{0,32},{32,0},{64,96},{96,64},{128,160},{160,128},{192,224},{224,1... | collective-permute-start | bytes 786440 | tf_op jit(solution)/shard_map/ppermute | solution.py:26
  41.2 2.7 %copy.60 = f32[512,576]{1,0:T(8,128)} copy(f32[512,576]{0,1:T(8,128)} %pad_maximum_fusion) | data formatting | bytes 2359296 | tf_op jit(solution)/shard_map/concatenate | solution.py:79
  44.0 1.2 %fusion.20 = bf16[2,16,8,576]{3,2,1,0:T(8,128)(2,1)S(1)} fusion(f32[2,16,2,8,576]{4,3,2,1,0:T(8,128)} %bitcast.92, s32[]{:T(128)S(6)} %select_n.44), kind=kLoop, calls=%fused_computation.40 | loop fusion | bytes 589828 | tf_op jit(solution)/shard_map/convert_element_type | solution.py:81
  45.2 1.9 %collective-permute-start.1 = (bf16[2,16,8,576]{3,2,1,0:T(8,128)(2,1)S(1)}, bf16[2,16,8,576]{3,2,1,0:T(8,128)(2,1)S(1)}, u32[]{:S(2)}, u32[]{:S(2)}) collective-permute-start(bf16[2,16,8,576]{3,2,1,0:T(8,128)(2,1)S(1)} %fusion.20), channel_id=1, source_target_pairs={{0,1},{1,0},{2,3},{3,2},{4,5},{5,4},{6,7},{7,6},{8,9},{9,8},{10,11... | collective-permute-start | bytes 884744 | tf_op jit(solution)/shard_map/ppermute | solution.py:82
  48.3 1.9 %collective-permute-start.4 = (bf16[128,1024]{1,0:T(8,128)(2,1)}, bf16[128,1024]{1,0:T(8,128)(2,1)}, u32[]{:S(2)}, u32[]{:S(2)}) collective-permute-start(bf16[128,1024]{1,0:T(8,128)(2,1)} %convolution_convert_fusion.2), channel_id=1, source_target_pairs={{0,128},{32,160},{64,192},{96,224},{128,0},{160,32},{192,64},{224,... | collective-permute-start | bytes 786440 | tf_op jit(solution)/shard_map/ppermute | solution.py:26
  50.2 1.2 %convolution_convert_fusion.1 = bf16[128,1024]{1,0:T(8,128)(2,1)} fusion(bf16[512,128]{0,1:T(8,128)(2,1)S(1)} %bitcast.102, bf16[512,1024]{0,1:T(8,128)(2,1)S(1)} %bitcast.87), kind=kOutput, calls=%fused_computation.11 | convolution fusion | flops 134348800 | bytes 1441792 | tf_op jit(solution)/shard_map/sl,sk->lk/dot_general | solution.py:92
  51.4 5.4 %collective-permute-start.5 = (bf16[128,1024]{1,0:T(8,128)(2,1)}, bf16[128,1024]{1,0:T(8,128)(2,1)}, u32[]{:S(2)}, u32[]{:S(2)}) collective-permute-start(bf16[128,1024]{1,0:T(8,128)(2,1)} %convolution_convert_fusion.1), channel_id=1, source_target_pairs={{0,160},{32,128},{64,224},{96,192},{128,32},{160,0},{192,96},{224,... | collective-permute-start | bytes 786440 | tf_op jit(solution)/shard_map/ppermute | solution.py:26
  56.9 1.9 %collective-permute-start.2 = (bf16[16,8,576]{2,1,0:T(8,128)(2,1)S(1)}, bf16[16,8,576]{2,1,0:T(8,128)(2,1)S(1)}, u32[]{:S(2)}, u32[]{:S(2)}) collective-permute-start(bf16[16,8,576]{2,1,0:T(8,128)(2,1)S(1)} %fusion.25), channel_id=1, source_target_pairs={{32,0},{64,32},{96,64},{128,96},{160,128},{192,160},{224,192},{256... | collective-permute-start | bytes 442376 | tf_op jit(solution)/shard_map/ppermute | solution.py:21
  59.2 7.3 %collective-permute-done.2 = bf16[16,8,576]{2,1,0:T(8,128)(2,1)S(1)} collective-permute-done((bf16[16,8,576]{2,1,0:T(8,128)(2,1)S(1)}, bf16[16,8,576]{2,1,0:T(8,128)(2,1)S(1)}, u32[]{:S(2)}, u32[]{:S(2)}) %collective-permute-start.2) | collective-permute-done | bytes 147488 | tf_op jit(solution)/shard_map/ppermute | solution.py:21
  67.2 7.4 %all-to-all-start = ((bf16[16,8,576]{2,1,0:T(8,128)(2,1)}), bf16[16,8,576]{2,1,0:T(8,128)(2,1)}, u32[]{:S(2)}, u32[]{:S(2)}) async-start(bf16[16,8,576]{2,1,0:T(8,128)(2,1)} %fusion.22), calls=%async_computation | async-start | bytes 327680 | tf_op jit(solution)/shard_map/all_to_all | solution.py:99
  74.6 2.3 %add_convert_fusion = bf16[128,1024]{1,0:T(8,128)(2,1)} fusion(bf16[128,1024]{1,0:T(8,128)(2,1)} %collective-permute-done.5, bf16[128,1024]{1,0:T(8,128)(2,1)} %collective-permute-done.4, bf16[128,1024]{1,0:T(8,128)(2,1)} %collective-permute-done.3, bf16[512,128]{0,1:T(8,128)(2,1)S(1)} %bitcast.101, bf16[512,1024]{0,1:T(8,128)(2,1)S(1)} %bitcast.88), kind=kOutput, calls=%fused_computation.30 | convolution fusion | flops 135135232 | bytes 2228224 | tf_op jit(solution)/shard_map/sl,sk->lk/dot_general | solution.py:92
  77.0 10.2 %all-to-all-done = bf16[16,8,576]{2,1,0:T(8,128)(2,1)} async-done(((bf16[16,8,576]{2,1,0:T(8,128)(2,1)}), bf16[16,8,576]{2,1,0:T(8,128)(2,1)}, u32[]{:S(2)}, u32[]{:S(2)}) %all-to-all-start) | async-done | bytes 147488 | tf_op jit(solution)/shard_map/all_to_all | solution.py:99
  87.2 19.7 %all-to-all-start.1 = ((bf16[8,16,1024]{2,1,0:T(8,128)(2,1)}), bf16[8,16,1024]{2,1,0:T(8,128)(2,1)S(1)}, u32[]{:S(2)}, u32[]{:S(2)}) async-start(bf16[8,16,1024]{2,1,0:T(8,128)(2,1)} %bitcast.100), calls=%async_computation.1 | async-start | bytes 524288 | tf_op jit(solution)/shard_map/all_to_all | solution.py:101
  109.0 1.6 %convert_reduce_fusion.1 = f32[8,576]{1,0:T(8,128)} fusion(bf16[16,8,576]{2,1,0:T(8,128)(2,1)} %all-to-all-done), kind=kLoop, calls=%fused_computation.45 | loop fusion | flops 142848 | bytes 165888 | tf_op jit(solution)/shard_map/reduce_sum | solution.py:100
  110.6 6.9 %all-to-all-done.1 = bf16[8,16,1024]{2,1,0:T(8,128)(2,1)S(1)} async-done(((bf16[8,16,1024]{2,1,0:T(8,128)(2,1)}), bf16[8,16,1024]{2,1,0:T(8,128)(2,1)S(1)}, u32[]{:S(2)}, u32[]{:S(2)}) %all-to-all-start.1) | async-done | bytes 262176 | tf_op jit(solution)/shard_map/all_to_all | solution.py:101
  (55 shorter events, 16.1 us)
Async XLA Ops:
  0.6 20.5 %copy-start = (bf16[512,1024]{1,0:T(8,128)(2,1)S(1)}, bf16[512,1024]{1,0:T(8,128)(2,1)}, u32[]{:S(2)}) copy-start(bf16[512,1024]{1,0:T(8,128)(2,1)} %param.8) | copy-start | bytes 3145732
  0.6 19.5 %copy-start.10 = (bf16[256,576]{0,1:T(8,128)(2,1)S(1)}, bf16[256,576]{0,1:T(8,128)(2,1)}, u32[]{:S(2)}) copy-start(bf16[256,576]{0,1:T(8,128)(2,1)} %param.5) | copy-start | bytes 884740
  0.7 19.5 %collective-permute-start = (bf16[256,576]{0,1:T(8,128)(2,1)}, bf16[256,576]{0,1:T(8,128)(2,1)S(1)}, u32[]{:S(2)}, u32[]{:S(2)}) collective-permute-start(bf16[256,576]{0,1:T(8,128)(2,1)} %param.5), channel_id=1, source_target_pairs={{0,32},{32,64},{64,96},{96,128},{128,160},{160,192},{192,224},{224... | collective-permute-start | bytes 884744 | tf_op jit(solution)/shard_map/ppermute | solution.py:21
  6.4 19.4 %copy-start.6 = (bf16[256,768]{0,1:T(8,128)(2,1)}, bf16[256,768]{0,1:T(8,128)(2,1)S(1)}, u32[]{:S(2)}) copy-start(bf16[256,768]{0,1:T(8,128)(2,1)S(1)} %copy.46) | copy-start | bytes 1179652
  20.2 4.5 %copy-start.9 = (bf16[512,576]{0,1:T(8,128)(2,1)}, bf16[512,576]{0,1:T(8,128)(2,1)S(1)}, u32[]{:S(2)}) copy-start(bf16[512,576]{0,1:T(8,128)(2,1)S(1)} %constant_dynamic-update-slice_fusion) | copy-start | bytes 1769476
  25.8 0.8 copy-start.2
  31.0 1.8 %copy-start.1 = (f32[4,256,512]{1,2,0:T(8,128)}, f32[4,256,512]{1,2,0:T(8,128)S(1)}, u32[]{:S(2)}) copy-start(f32[4,256,512]{1,2,0:T(8,128)S(1)} %fusion.12) | copy-start | bytes 6291460
  31.0 1.4 %copy-start.4 = (bf16[512,4,128]{2,1,0:T(4,128)(2,1)S(1)}, bf16[512,4,128]{2,1,0:T(4,128)(2,1)}, u32[]{:S(2)}) copy-start(bf16[512,4,128]{2,1,0:T(4,128)(2,1)} %get-tuple-element.12) | copy-start | bytes 1572868
  32.8 2.1 %copy-start.7 = (bf16[256,768]{0,1:T(8,128)(2,1)S(1)}, bf16[256,768]{0,1:T(8,128)(2,1)}, u32[]{:S(2)}) copy-start(bf16[256,768]{0,1:T(8,128)(2,1)} %copy-done.6) | copy-start | bytes 1179652
  35.9 1.0 copy-start.8
  38.2 36.4 %collective-permute-start.3 = (bf16[128,1024]{1,0:T(8,128)(2,1)}, bf16[128,1024]{1,0:T(8,128)(2,1)}, u32[]{:S(2)}, u32[]{:S(2)}) collective-permute-start(bf16[128,1024]{1,0:T(8,128)(2,1)} %convolution_convert_fusion.3), channel_id=1, source_target_pairs={{0,32},{32,0},{64,96},{96,64},{128,160},{160,128},{192,224},{224,1... | collective-permute-start | bytes 786440 | tf_op jit(solution)/shard_map/ppermute | solution.py:26
  44.0 12.8 %copy-start.5 = (f32[512,576]{1,0:T(8,128)S(1)}, f32[512,576]{1,0:T(8,128)}, u32[]{:S(2)}) copy-start(f32[512,576]{1,0:T(8,128)} %copy.60) | copy-start | bytes 3538948
  45.2 11.6 %collective-permute-start.1 = (bf16[2,16,8,576]{3,2,1,0:T(8,128)(2,1)S(1)}, bf16[2,16,8,576]{3,2,1,0:T(8,128)(2,1)S(1)}, u32[]{:S(2)}, u32[]{:S(2)}) collective-permute-start(bf16[2,16,8,576]{3,2,1,0:T(8,128)(2,1)S(1)} %fusion.20), channel_id=1, source_target_pairs={{0,1},{1,0},{2,3},{3,2},{4,5},{5,4},{6,7},{7,6},{8,9},{9,8},{10,11... | collective-permute-start | bytes 884744 | tf_op jit(solution)/shard_map/ppermute | solution.py:82
  47.1 11.7 %copy-start.3 = (bf16[512,4,128]{2,1,0:T(4,128)(2,1)S(1)}, bf16[512,4,128]{2,1,0:T(4,128)(2,1)}, u32[]{:S(2)}) copy-start(bf16[512,4,128]{2,1,0:T(4,128)(2,1)} %copy-done.2) | copy-start | bytes 1572868
  48.3 26.3 %collective-permute-start.4 = (bf16[128,1024]{1,0:T(8,128)(2,1)}, bf16[128,1024]{1,0:T(8,128)(2,1)}, u32[]{:S(2)}, u32[]{:S(2)}) collective-permute-start(bf16[128,1024]{1,0:T(8,128)(2,1)} %convolution_convert_fusion.2), channel_id=1, source_target_pairs={{0,128},{32,160},{64,192},{96,224},{128,0},{160,32},{192,64},{224,... | collective-permute-start | bytes 786440 | tf_op jit(solution)/shard_map/ppermute | solution.py:26
  51.4 23.2 %collective-permute-start.5 = (bf16[128,1024]{1,0:T(8,128)(2,1)}, bf16[128,1024]{1,0:T(8,128)(2,1)}, u32[]{:S(2)}, u32[]{:S(2)}) collective-permute-start(bf16[128,1024]{1,0:T(8,128)(2,1)} %convolution_convert_fusion.1), channel_id=1, source_target_pairs={{0,160},{32,128},{64,224},{96,192},{128,32},{160,0},{192,96},{224,... | collective-permute-start | bytes 786440 | tf_op jit(solution)/shard_map/ppermute | solution.py:26
  56.9 9.6 %collective-permute-start.2 = (bf16[16,8,576]{2,1,0:T(8,128)(2,1)S(1)}, bf16[16,8,576]{2,1,0:T(8,128)(2,1)S(1)}, u32[]{:S(2)}, u32[]{:S(2)}) collective-permute-start(bf16[16,8,576]{2,1,0:T(8,128)(2,1)S(1)} %fusion.25), channel_id=1, source_target_pairs={{32,0},{64,32},{96,64},{128,96},{160,128},{192,160},{224,192},{256... | collective-permute-start | bytes 442376 | tf_op jit(solution)/shard_map/ppermute | solution.py:21
  67.2 20.1 %all-to-all-start = ((bf16[16,8,576]{2,1,0:T(8,128)(2,1)}), bf16[16,8,576]{2,1,0:T(8,128)(2,1)}, u32[]{:S(2)}, u32[]{:S(2)}) async-start(bf16[16,8,576]{2,1,0:T(8,128)(2,1)} %fusion.22), calls=%async_computation | async-start | bytes 327680 | tf_op jit(solution)/shard_map/all_to_all | solution.py:99
  87.2 30.2 %all-to-all-start.1 = ((bf16[8,16,1024]{2,1,0:T(8,128)(2,1)}), bf16[8,16,1024]{2,1,0:T(8,128)(2,1)S(1)}, u32[]{:S(2)}, u32[]{:S(2)}) async-start(bf16[8,16,1024]{2,1,0:T(8,128)(2,1)} %bitcast.100), calls=%async_computation.1 | async-start | bytes 524288 | tf_op jit(solution)/shard_map/all_to_all | solution.py:101

commit v2 on v1

v2 whole, which is shorter than its diff:
```python
import math

import jax
import jax.numpy as jnp
from jax import lax
from jax.experimental import pallas as pl
from jax.experimental.pallas import tpu as pltpu
from jax.sharding import Mesh
from jax.sharding import PartitionSpec as P


LATENT = 512
ROPE = 64
NOPE = 128
VDIM = 128
HEADS = 4
TOK = 256
PAIR = NOPE + VDIM
WIDTH = NOPE + ROPE
SCALING = 1.0 / math.sqrt(WIDTH)
CTX = ("zh", "z0", "x1", "x0")
HEAD = ("xh", "y", "core")
F32 = jnp.float32
BF16 = jnp.bfloat16
NT = (((1,), (1,)), ((), ()))
TN = (((0,), (0,)), ((), ()))
VMEM = pl.BlockSpec(memory_space=pltpu.VMEM)
SMEM = pl.BlockSpec(memory_space=pltpu.SMEM)


def dot(a, b, dims=(((1,), (0,)), ((), ()))):
    return lax.dot_general(a, b, dims, preferred_element_type=F32)


def ctx_shift(x, by):
    pairs = [(i, i + by) for i in range(32) if 0 <= i + by < 32]
    return lax.ppermute(x, CTX, pairs)


def iota(shape, dim):
    return lax.broadcasted_iota(jnp.int32, shape, dim)


def keys_and_values(xt_ref, w_ref, ke_ref):
    kv = dot(xt_ref[:LATENT, :], w_ref[...], TN).astype(BF16)
    rope = jnp.concatenate([xt_ref[LATENT:, :].astype(F32), jnp.zeros((ROPE, TOK), F32)], axis=0)
    rope = jnp.transpose(rope).astype(BF16)
    values = []
    for h in range(HEADS):
        ke_ref[h, :, :NOPE] = kv[:, h * PAIR : h * PAIR + NOPE]
        ke_ref[h, :, NOPE:] = rope
        values.append(kv[:, h * PAIR + NOPE : (h + 1) * PAIR])
    return values


def own_kernel(start_ref, xt_ref, q_ref, do_ref, w_ref, ke_ref, qe_ref, e_ref, dp_ref, lg_ref):
    lane = iota((TOK, 256), 1)
    for h in range(HEADS):
        base = (h // 2) * 2 * WIDTH
        if h % 2 == 0:
            rows = q_ref[:, base : base + 256].astype(F32)
        else:
            rows = pltpu.roll(q_ref[:, base + 128 : base + 384].astype(F32), 192, 1)
        qe_ref[h] = jnp.where(lane < WIDTH, rows, 0.0).astype(BF16)
    values = keys_and_values(xt_ref, w_ref, ke_ref)
    key = iota((TOK, TOK), 0)
    seen = (key >= start_ref[...]) & (key <= iota((TOK, TOK), 1))
    for h in range(HEADS):
        scores = dot(ke_ref[h], qe_ref[h], NT) * SCALING
        e = jnp.where(seen, jnp.exp(scores), 0.0)
        dp = dot(values[h], do_ref[:, h * VDIM : (h + 1) * VDIM], NT)
        e_ref[h] = e
        dp_ref[h] = dp
        lg_ref[h : h + 1, :] = jnp.sum(e, axis=0, keepdims=True)
        lg_ref[h + 4 : h + 5, :] = jnp.sum(e * dp, axis=0, keepdims=True)


def chosen_rows(xt_ref, bit):
    return jnp.concatenate(
        [xt_ref[pl.ds(pl.multiple_of((2 * i + bit) * 64, 64), 64), :] for i in range(4)], axis=0
    )


def weight_half(own_ref, prev_ref, bit, dkv_ref):
    half = dot(chosen_rows(prev_ref, bit), dkv_ref[0])
    return half + dot(chosen_rows(own_ref, bit), dkv_ref[1])


def window_kernel(
    z0_ref, start_ref, xt_ref, own_ref, qe_ref, do_ref, w_ref, e_ref, dp_ref, lg_ref,
    ke_ref, ds_ref, dkv_ref, lat_ref, theirs_ref,
):
    values = keys_and_values(xt_ref, w_ref, ke_ref)
    seen = iota((TOK, TOK), 0) - TOK >= start_ref[...]
    rope_grads = [jnp.zeros((TOK, 128), F32), jnp.zeros((TOK, 128), F32)]
    for h in range(HEADS):
        qe = qe_ref[h]
        do = do_ref[:, h * VDIM : (h + 1) * VDIM]
        scores = dot(ke_ref[h], qe, NT) * SCALING
        e = jnp.where(seen, jnp.exp(scores), 0.0)
        dp = dot(values[h], do, NT)
        norm = 1.0 / (lg_ref[h : h + 1, :] + jnp.sum(e, axis=0, keepdims=True))
        delta = (lg_ref[h + 4 : h + 5, :] + jnp.sum(e * dp, axis=0, keepdims=True)) * norm
        for half in range(2):
            if half == 1:
                e, dp = e_ref[h], dp_ref[h]
            probs = e * norm
            ds = (probs * (dp - delta) * SCALING).astype(BF16)
            ds_ref[h, half] = ds
            dk = dot(ds, qe)
            dkv_ref[half, :, h * PAIR : h * PAIR + NOPE] = dk[:, :NOPE].astype(BF16)
            rope_grads[half] = rope_grads[half] + dk[:, NOPE:]
            dkv_ref[half, :, h * PAIR + NOPE : (h + 1) * PAIR] = dot(
                probs.astype(BF16), do
            ).astype(BF16)
    theirs_ref[...] = weight_half(own_ref, xt_ref, 1 - z0_ref[0], dkv_ref).astype(BF16)
    lat_ref[:, :LATENT] = dot(dkv_ref[1], w_ref[...], NT).astype(BF16)
    lat_ref[:, LATENT : 2 * LATENT] = dot(dkv_ref[0], w_ref[...], NT).astype(BF16)
    lat_ref[:, 2 * LATENT :] = (rope_grads[1] + pltpu.roll(rope_grads[0], ROPE, 1)).astype(BF16)


def rest_kernel(z0_ref, xt_ref, own_ref, kep_ref, keo_ref, ds_ref, dkv_ref, dq_ref, mine_ref):
    for pair in range(HEADS // 2):
        parts = []
        for h in (2 * pair, 2 * pair + 1):
            parts.append(dot(ds_ref[h, 0], kep_ref[h], TN) + dot(ds_ref[h, 1], keo_ref[h], TN))
        moved = pltpu.roll(parts[1], ROPE, 1)
        base = pair * 2 * WIDTH
        dq_ref[:, base : base + 128] = parts[0][:, :128].astype(BF16)
        dq_ref[:, base + 128 : base + 256] = (parts[0][:, 128:] + moved[:, :128]).astype(BF16)
        dq_ref[:, base + 256 : base + 384] = moved[:, 128:].astype(BF16)
    mine_ref[...] = weight_half(own_ref, xt_ref, z0_ref[0], dkv_ref)


def call(kernel, outs, scalars, flops, *args):
    specs = [SMEM] * scalars + [VMEM] * (len(args) - scalars)
    return pl.pallas_call(
        kernel,
        out_shape=[jax.ShapeDtypeStruct(s, d) for s, d in outs],
        in_specs=specs,
        out_specs=[VMEM] * len(outs),
        compiler_params=pltpu.CompilerParams(vmem_limit_bytes=20 << 20),
        cost_estimate=pl.CostEstimate(flops=flops, bytes_accessed=4 << 20, transcendentals=0),
    )(*args)


def attend(own, prev, query, out_grad, up_weight, start, z0):
    square = (HEADS, TOK, 256)
    keo, qe, e, dp, lg = call(
        own_kernel,
        [(square, BF16), (square, BF16), (square, F32), (square, F32), ((8, TOK), F32)],
        0, 470_000_000, start, own, query, out_grad, up_weight,
    )
    kep, ds, dkv, latent, theirs = call(
        window_kernel,
        [
            (square, BF16),
            ((HEADS, 2, TOK, TOK), BF16),
            ((2, TOK, HEADS * PAIR), BF16),
            ((TOK, 2 * LATENT + 2 * ROPE), BF16),
            ((TOK, HEADS * PAIR), BF16),
        ],
        1, 1_700_000_000, z0, start, prev, own, qe, out_grad, up_weight, e, dp, lg,
    )
    return latent, theirs, (prev, own, kep, keo, ds, dkv)


def finish(z0, saved):
    return call(
        rest_kernel,
        [((TOK, HEADS * WIDTH), BF16), ((TOK, HEADS * PAIR), F32)],
        1, 540_000_000, z0, *saved,
    )


def body(compressed, query, out_grad, up_weight, lengths):
    ctx_rank = lax.axis_index(CTX)
    z0 = lax.axis_index("z0").reshape(1)
    own = compressed.T
    prev = ctx_shift(own, 1)

    first_pos = ctx_rank * TOK
    ends = jnp.cumsum(lengths)
    query_pos = first_pos + jnp.arange(TOK, dtype=jnp.int32)
    start = jnp.sum(jnp.where(ends[:, None] <= query_pos[None, :], lengths[:, None], 0), axis=0)
    start = (start - first_pos)[None, :]

    latent, theirs, saved = attend(own, prev, query, out_grad, up_weight, start, z0)
    got = lax.ppermute(theirs, CTX, [(i, i ^ 4) for i in range(32)])
    parts = lax.all_to_all(latent.reshape(32, 8, -1), HEAD, 0, 0)
    dq, mine = finish(z0, saved)
    both = (mine + got.astype(F32)).astype(BF16).reshape(16, 16, -1)
    sixteenths = lax.all_to_all(both, ("zh", "x1", "x0"), 0, 0)
    summed = jnp.sum(parts.astype(F32), axis=0)
    kept = jnp.concatenate([summed[:, :LATENT], summed[:, 2 * LATENT : 2 * LATENT + ROPE]], axis=1)
    sent = jnp.concatenate([summed[:, LATENT : 2 * LATENT], summed[:, 2 * LATENT + ROPE :]], axis=1)
    grad_compressed = kept + ctx_shift(sent, -1)
    grad_weight = jnp.sum(sixteenths.astype(F32), axis=0)
    return dq, grad_compressed, grad_weight


def solution(mesh):
    fine = Mesh(
        mesh.devices.reshape(4, 2, 2, 2, 2, 8, 2), ("zh", "z0", "x1", "x0", "xh", "y", "core")
    )
    placed = (P(CTX, None), P(CTX, HEAD), P(CTX, HEAD), P(None, HEAD), P())
    return jax.shard_map(
        body,
        mesh=fine,
        in_specs=placed,
        out_specs=(P(CTX, HEAD), P(CTX + HEAD, None), P(CTX, HEAD)),
        check_vma=False,
    )
```

time: 119 us -> 88.7 us (0.75)
  the two profiles are of different devices: /device:TPU:2 before, /device:TPU:14 now
where the time goes in v2:
time: 88.7 us; the launch traced here: 88 us
  starting transfers between devices  46.9 us (53%)
  waiting for transfers between devices  22.2 us (25%)
  local copies, waits for them, and re-layouts  7.72 us (9%)
  Pallas kernels  5.93 us (7%)
  other arithmetic  4.5 us (5%)
    all_to_all x1, starting transfers between devices, body(): sixteenths = lax.all_to_all(both, ('zh', 'x1', 'x0'), 0, 0)  18.1 us
    all_to_all x1, starting transfers between devices, body(): parts = lax.all_to_all(latent.reshape(32, 8, -1), HEAD, 0, 0)  13.3 us
    ppermute x2, starting transfers between devices, ctx_shift(): return lax.ppermute(x, CTX, pairs)  10.3 us
    ppermute x1, waiting for transfers between devices, body(): got = lax.ppermute(theirs, CTX, [(i, i ^ 4) for i in range(32)])  10.1 us
    ppermute x2, waiting for transfers between devices, ctx_shift(): return lax.ppermute(x, CTX, pairs)  7.24 us
    unnamed x18, local copies, waits for them, and re-layouts  6.89 us
    pallas_call x3, Pallas kernels, call(): pl.pallas_call(kernel, out_shape=[jax.ShapeDtypeStruct(s, d) for s, d in...  5.93 us
    ppermute x1, starting transfers between devices, body(): got = lax.ppermute(theirs, CTX, [(i, i ^ 4) for i in range(32)])  5.19 us
  transfers between devices with their start and end apart: 5, of which 5 were waited for; matrix products, arithmetic and copies ran while one was open for 5% of the time, Pallas kernels for 2%

profile of v2, /device:TPU:14, one launch (start us, length us, event | category | flops | bytes accessed | tf_op | source)
XLA Modules:
  0.0 88.0 jit_solution(13048337461569209726)
XLA Ops:
  0.6 7.8 %collective-permute-start = (bf16[576,256]{1,0:T(8,128)(2,1)}, bf16[576,256]{1,0:T(8,128)(2,1)S(1)}, u32[]{:S(2)}, u32[]{:S(2)}) collective-permute-start(bf16[576,256]{1,0:T(8,128)(2,1)} %bitcast.6), channel_id=1, source_target_pairs={{0,32},{32,64},{64,96},{96,128},{128,160},{160,192},{192,224},{224... | collective-permute-start | bytes 884744 | tf_op jit(solution)/shard_map/ppermute | solution.py:37
  8.5 0.8 copy.10
  9.5 0.8 select_reduce_fusion
  10.3 1.0 %copy-done = bf16[256,576]{0,1:T(8,128)(2,1)S(1)} copy-done((bf16[256,576]{0,1:T(8,128)(2,1)S(1)}, bf16[256,576]{0,1:T(8,128)(2,1)}, u32[]{:S(2)}) %copy-start) | copy-done | bytes 294936
  11.2 1.2 %copy-done.2 = bf16[512,1024]{1,0:T(8,128)(2,1)S(1)} copy-done((bf16[512,1024]{1,0:T(8,128)(2,1)S(1)}, bf16[512,1024]{1,0:T(8,128)(2,1)}, u32[]{:S(2)}) %copy-start.2) | copy-done | bytes 1048600
  12.4 1.0 %copy-done.4 = bf16[256,768]{1,0:T(8,128)(2,1)S(1)} copy-done((bf16[256,768]{1,0:T(8,128)(2,1)S(1)}, bf16[256,768]{1,0:T(8,128)(2,1)}, u32[]{:S(2)}) %copy-start.4) | copy-done | bytes 393240
  13.4 0.9 %copy-done.7 = bf16[256,512]{1,0:T(8,128)(2,1)S(1)} copy-done((bf16[256,512]{1,0:T(8,128)(2,1)S(1)}, bf16[256,512]{1,0:T(8,128)(2,1)}, u32[]{:S(2)}) %copy-start.7) | copy-done | bytes 262168
  14.4 0.8 shard_map.76
  15.6 3.8 %shard_map.77 = (bf16[4,256,256]{2,1,0:T(8,128)(2,1)S(1)}, bf16[4,2,256,256]{3,2,1,0:T(8,128)(2,1)S(1)}, bf16[2,256,1024]{2,1,0:T(8,128)(2,1)S(1)}, bf16[256,1152]{1,0:T(8,128)(2,1)}, bf16[256,1024]{1,0:T(8,128)(2,1)S(1)}) custom-call(s32[1]{0:T(128)} %bitcast.z0_ref, s32[1,256]{1,0:T(1,128)S(1)} %bitcast.11, ...), custom_call_target="tpu_custom_call" | custom-call | flops 1700000000 | bytes 4194304 | tf_op jit(solution)/shard_map/pallas_call | solution.py:137
  19.4 0.7 copy-done.5
  20.1 0.8 copy-done.8
  20.9 13.3 %all-to-all-start = ((bf16[32,8,1152]{2,1,0:T(8,128)(2,1)}), bf16[32,8,1152]{2,1,0:T(8,128)(2,1)}, u32[]{:S(2)}, u32[]{:S(2)}) async-start(bf16[32,8,1152]{2,1,0:T(8,128)(2,1)} %bitcast.4), calls=%async_computation | async-start | bytes 1179648 | tf_op jit(solution)/shard_map/all_to_all | solution.py:190
  34.2 5.2 %collective-permute-start.2 = (bf16[256,1024]{1,0:T(8,128)(2,1)}, bf16[256,1024]{1,0:T(8,128)(2,1)S(1)}, u32[]{:S(2)}, u32[]{:S(2)}) collective-permute-start(bf16[256,1024]{1,0:T(8,128)(2,1)} %copy-done.8), channel_id=1, source_target_pairs={{0,128},{32,160},{64,192},{96,224},{128,0},{160,32},{192,64},{224,... | collective-permute-start | bytes 1572872 | tf_op jit(solution)/shard_map/ppermute | solution.py:189
  39.4 1.0 %copy-done.6 = bf16[576,256]{1,0:T(8,128)(2,1)S(1)} copy-done((bf16[576,256]{1,0:T(8,128)(2,1)S(1)}, bf16[576,256]{1,0:T(8,128)(2,1)}, u32[]{:S(2)}) %copy-start.6) | copy-done | bytes 294936
  40.4 1.3 %shard_map.78 = (bf16[256,768]{1,0:T(8,128)(2,1)}, f32[256,1024]{1,0:T(8,128)S(1)}) custom-call(s32[1]{0:T(128)} %bitcast.z0_ref, bf16[576,256]{1,0:T(8,128)(2,1)S(1)} %copy-done.6, bf16[576,256]{1,0:T(8,128)(2,1)S(1)} %bitcast.9, bf16[4,256,256]{2,1,0:T(8,128)(2,1)S(1)} %get-tuple-element.19.kep_ref, bf16[4,256,256]{2,1,0:T(8,128)(2,1)S(1)} %get-tuple-element.20.keo_ref, ...), custom_call_target="tpu_custom_call" | custom-call | flops 540000000 | bytes 4194304 | tf_op jit(solution)/shard_map/pallas_call | solution.py:137
  41.7 10.1 %collective-permute-done.2 = bf16[256,1024]{1,0:T(8,128)(2,1)S(1)} collective-permute-done((bf16[256,1024]{1,0:T(8,128)(2,1)}, bf16[256,1024]{1,0:T(8,128)(2,1)S(1)}, u32[]{:S(2)}, u32[]{:S(2)}) %collective-permute-start.2) | collective-permute-done | bytes 524320 | tf_op jit(solution)/shard_map/ppermute | solution.py:189
  51.8 1.0 %add_convert_fusion = bf16[256,1024]{1,0:T(8,128)(2,1)} fusion(f32[256,1024]{1,0:T(8,128)S(1)} %get-tuple-element.25, bf16[256,1024]{1,0:T(8,128)(2,1)S(1)} %collective-permute-done.2), kind=kLoop, calls=%fused_computation.2 | loop fusion | flops 786432 | bytes 2097152 | tf_op jit(solution)/shard_map/convert_element_type | solution.py:192
  53.4 18.1 %all-to-all-start.1 = ((bf16[16,16,1024]{2,1,0:T(8,128)(2,1)}), bf16[16,16,1024]{2,1,0:T(8,128)(2,1)S(1)}, u32[]{:S(2)}, u32[]{:S(2)}) async-start(bf16[16,16,1024]{2,1,0:T(8,128)(2,1)} %bitcast.5), calls=%async_computation.1 | async-start | bytes 1048576 | tf_op jit(solution)/shard_map/all_to_all | solution.py:193
  71.5 1.2 %convert_reduce_fusion = f32[8,1152]{1,0:T(8,128)S(1)} fusion(bf16[32,8,1152]{2,1,0:T(8,128)(2,1)} %all-to-all-done), kind=kLoop, calls=%fused_computation | loop fusion | flops 580608 | bytes 626688 | tf_op jit(solution)/shard_map/reduce_sum | solution.py:194
  72.8 2.5 %collective-permute-start.1 = (f32[8,576]{1,0:T(8,128)S(1)}, f32[8,576]{1,0:T(8,128)S(1)}, u32[]{:S(2)}, u32[]{:S(2)}) collective-permute-start(f32[8,576]{1,0:T(8,128)S(1)} %pad_maximum_fusion), channel_id=1, source_target_pairs={{32,0},{64,32},{96,64},{128,96},{160,128},{192,160},{224,192},{256... | collective-permute-start | bytes 55304 | tf_op jit(solution)/shard_map/ppermute | solution.py:37
  75.3 7.1 %collective-permute-done.1 = f32[8,576]{1,0:T(8,128)S(1)} collective-permute-done((f32[8,576]{1,0:T(8,128)S(1)}, f32[8,576]{1,0:T(8,128)S(1)}, u32[]{:S(2)}, u32[]{:S(2)}) %collective-permute-start.1) | collective-permute-done | bytes 18464 | tf_op jit(solution)/shard_map/ppermute | solution.py:37
  82.4 0.6 maximum_add_fusion
  83.0 4.3 %all-to-all-done.1 = bf16[16,16,1024]{2,1,0:T(8,128)(2,1)S(1)} async-done(((bf16[16,16,1024]{2,1,0:T(8,128)(2,1)}), bf16[16,16,1024]{2,1,0:T(8,128)(2,1)S(1)}, u32[]{:S(2)}, u32[]{:S(2)}) %all-to-all-start.1) | async-done | bytes 524320 | tf_op jit(solution)/shard_map/all_to_all | solution.py:193
  87.3 0.7 convert_reduce_fusion.1
  (20 shorter events, 1.3 us)
Async XLA Ops:
  0.6 14.7 %collective-permute-start = (bf16[576,256]{1,0:T(8,128)(2,1)}, bf16[576,256]{1,0:T(8,128)(2,1)S(1)}, u32[]{:S(2)}, u32[]{:S(2)}) collective-permute-start(bf16[576,256]{1,0:T(8,128)(2,1)} %bitcast.6), channel_id=1, source_target_pairs={{0,32},{32,64},{64,96},{96,128},{128,160},{160,192},{192,224},{224... | collective-permute-start | bytes 884744 | tf_op jit(solution)/shard_map/ppermute | solution.py:37
  10.2 1.0 %copy-start = (bf16[256,576]{0,1:T(8,128)(2,1)S(1)}, bf16[256,576]{0,1:T(8,128)(2,1)}, u32[]{:S(2)}) copy-start(bf16[256,576]{0,1:T(8,128)(2,1)} %param.5) | copy-start | bytes 884740
  11.2 1.2 %copy-start.2 = (bf16[512,1024]{1,0:T(8,128)(2,1)S(1)}, bf16[512,1024]{1,0:T(8,128)(2,1)}, u32[]{:S(2)}) copy-start(bf16[512,1024]{1,0:T(8,128)(2,1)} %w_ref.3) | copy-start | bytes 3145732
  12.4 1.0 %copy-start.4 = (bf16[256,768]{1,0:T(8,128)(2,1)S(1)}, bf16[256,768]{1,0:T(8,128)(2,1)}, u32[]{:S(2)}) copy-start(bf16[256,768]{1,0:T(8,128)(2,1)} %q_ref.1) | copy-start | bytes 1179652
  13.4 0.9 %copy-start.7 = (bf16[256,512]{1,0:T(8,128)(2,1)S(1)}, bf16[256,512]{1,0:T(8,128)(2,1)}, u32[]{:S(2)}) copy-start(bf16[256,512]{1,0:T(8,128)(2,1)} %do_ref.3) | copy-start | bytes 786436
  14.4 1.2 %copy-start.3 = (bf16[512,1024]{1,0:T(8,128)(2,1)S(1)}, bf16[512,1024]{1,0:T(8,128)(2,1)}, u32[]{:S(2)}) copy-start(bf16[512,1024]{1,0:T(8,128)(2,1)} %w_ref.3) | copy-start | bytes 3145732
  19.4 0.7 copy-start.5
  20.1 0.8 copy-start.8
  20.9 18.5 %copy-start.1 = (bf16[256,576]{0,1:T(8,128)(2,1)S(1)}, bf16[256,576]{0,1:T(8,128)(2,1)}, u32[]{:S(2)}) copy-start(bf16[256,576]{0,1:T(8,128)(2,1)} %param.5) | copy-start | bytes 884740
  20.9 32.4 %all-to-all-start = ((bf16[32,8,1152]{2,1,0:T(8,128)(2,1)}), bf16[32,8,1152]{2,1,0:T(8,128)(2,1)}, u32[]{:S(2)}, u32[]{:S(2)}) async-start(bf16[32,8,1152]{2,1,0:T(8,128)(2,1)} %bitcast.4), calls=%async_computation | async-start | bytes 1179648 | tf_op jit(solution)/shard_map/all_to_all | solution.py:190
  34.2 17.6 %collective-permute-start.2 = (bf16[256,1024]{1,0:T(8,128)(2,1)}, bf16[256,1024]{1,0:T(8,128)(2,1)S(1)}, u32[]{:S(2)}, u32[]{:S(2)}) collective-permute-start(bf16[256,1024]{1,0:T(8,128)(2,1)} %copy-done.8), channel_id=1, source_target_pairs={{0,128},{32,160},{64,192},{96,224},{128,0},{160,32},{192,64},{224,... | collective-permute-start | bytes 1572872 | tf_op jit(solution)/shard_map/ppermute | solution.py:189
  39.4 1.0 %copy-start.6 = (bf16[576,256]{1,0:T(8,128)(2,1)S(1)}, bf16[576,256]{1,0:T(8,128)(2,1)}, u32[]{:S(2)}) copy-start(bf16[576,256]{1,0:T(8,128)(2,1)} %copy-done.5) | copy-start | bytes 884740
  53.4 33.9 %all-to-all-start.1 = ((bf16[16,16,1024]{2,1,0:T(8,128)(2,1)}), bf16[16,16,1024]{2,1,0:T(8,128)(2,1)S(1)}, u32[]{:S(2)}, u32[]{:S(2)}) async-start(bf16[16,16,1024]{2,1,0:T(8,128)(2,1)} %bitcast.5), calls=%async_computation.1 | async-start | bytes 1048576 | tf_op jit(solution)/shard_map/all_to_all | solution.py:193
  72.8 9.6 %collective-permute-start.1 = (f32[8,576]{1,0:T(8,128)S(1)}, f32[8,576]{1,0:T(8,128)S(1)}, u32[]{:S(2)}, u32[]{:S(2)}) collective-permute-start(f32[8,576]{1,0:T(8,128)S(1)} %pad_maximum_fusion), channel_id=1, source_target_pairs={{32,0},{64,32},{96,64},{128,96},{160,128},{192,160},{224,192},{256... | collective-permute-start | bytes 55304 | tf_op jit(solution)/shard_map/ppermute | solution.py:37

commit v3 on v2

--- a/solution.py
+++ b/solution.py
@@ -18,7 +18,7 @@
 PAIR = NOPE + VDIM
 WIDTH = NOPE + ROPE
 SCALING = 1.0 / math.sqrt(WIDTH)
-CTX = ("zh", "z0", "x1", "x0")
+CTX = ("z2", "z1", "z0", "x1", "x0")
 HEAD = ("xh", "y", "core")
 F32 = jnp.float32
 BF16 = jnp.bfloat16
@@ -75,20 +75,22 @@
         lg_ref[h + 4 : h + 5, :] = jnp.sum(e * dp, axis=0, keepdims=True)
 
 
-def chosen_rows(xt_ref, bit):
-    return jnp.concatenate(
-        [xt_ref[pl.ds(pl.multiple_of((2 * i + bit) * 64, 64), 64), :] for i in range(4)], axis=0
-    )
-
-
-def weight_half(own_ref, prev_ref, bit, dkv_ref):
-    half = dot(chosen_rows(prev_ref, bit), dkv_ref[0])
-    return half + dot(chosen_rows(own_ref, bit), dkv_ref[1])
+def piece_rows(xt_ref, z0, x0):
+    rows = []
+    for i in range(8):
+        chunk = (((i // 2) * 2 + z0) * 2 + i % 2) * 2 + x0
+        rows.append(xt_ref[pl.ds(pl.multiple_of(chunk * 16, 16), 16), :])
+    return jnp.concatenate(rows, axis=0)
+
+
+def weight_piece(own_ref, prev_ref, z0, x0, dkv_ref):
+    part = dot(piece_rows(prev_ref, z0, x0), dkv_ref[0])
+    return part + dot(piece_rows(own_ref, z0, x0), dkv_ref[1])
 
 
 def window_kernel(
-    z0_ref, start_ref, xt_ref, own_ref, qe_ref, do_ref, w_ref, e_ref, dp_ref, lg_ref,
-    ke_ref, ds_ref, dkv_ref, lat_ref, theirs_ref,
+    bits_ref, start_ref, xt_ref, own_ref, qe_ref, do_ref, w_ref, e_ref, dp_ref, lg_ref,
+    ke_ref, ds_ref, lat_ref, mine_ref, px_ref, pz_ref, pd_ref, dkv_ref,
 ):
     values = keys_and_values(xt_ref, w_ref, ke_ref)
     seen = iota((TOK, TOK), 0) - TOK >= start_ref[...]
@@ -113,13 +115,17 @@
             dkv_ref[half, :, h * PAIR + NOPE : (h + 1) * PAIR] = dot(
                 probs.astype(BF16), do
             ).astype(BF16)
-    theirs_ref[...] = weight_half(own_ref, xt_ref, 1 - z0_ref[0], dkv_ref).astype(BF16)
+    z0, x0 = bits_ref[2], bits_ref[4]
+    px_ref[...] = weight_piece(own_ref, xt_ref, z0, 1 - x0, dkv_ref).astype(BF16)
+    pz_ref[...] = weight_piece(own_ref, xt_ref, 1 - z0, x0, dkv_ref).astype(BF16)
+    pd_ref[...] = weight_piece(own_ref, xt_ref, 1 - z0, 1 - x0, dkv_ref).astype(BF16)
+    mine_ref[...] = weight_piece(own_ref, xt_ref, z0, x0, dkv_ref)
     lat_ref[:, :LATENT] = dot(dkv_ref[1], w_ref[...], NT).astype(BF16)
     lat_ref[:, LATENT : 2 * LATENT] = dot(dkv_ref[0], w_ref[...], NT).astype(BF16)
     lat_ref[:, 2 * LATENT :] = (rope_grads[1] + pltpu.roll(rope_grads[0], ROPE, 1)).astype(BF16)
 
 
-def rest_kernel(z0_ref, xt_ref, own_ref, kep_ref, keo_ref, ds_ref, dkv_ref, dq_ref, mine_ref):
+def query_kernel(kep_ref, keo_ref, ds_ref, dq_ref):
     for pair in range(HEADS // 2):
         parts = []
         for h in (2 * pair, 2 * pair + 1):
@@ -129,53 +135,79 @@
         dq_ref[:, base : base + 128] = parts[0][:, :128].astype(BF16)
         dq_ref[:, base + 128 : base + 256] = (parts[0][:, 128:] + moved[:, :128]).astype(BF16)
         dq_ref[:, base + 256 : base + 384] = moved[:, 128:].astype(BF16)
-    mine_ref[...] = weight_half(own_ref, xt_ref, z0_ref[0], dkv_ref)
-
-
-def call(kernel, outs, scalars, flops, *args):
+
+
+def quad_sum_kernel(bits_ref, mine_ref, gx_ref, gz_ref, gd_ref, kept_ref, px_ref, pz_ref, pd_ref, sum_ref):
+    sum_ref[...] = (
+        mine_ref[...] + gx_ref[...].astype(F32) + gz_ref[...].astype(F32) + gd_ref[...].astype(F32)
+    )
+    z1, x1 = bits_ref[1], bits_ref[3]
+    for out_ref, z, x in (
+        (kept_ref, z1, x1), (px_ref, z1, 1 - x1), (pz_ref, 1 - z1, x1), (pd_ref, 1 - z1, 1 - x1)
+    ):
+        for z2 in range(2):
+            row = pl.multiple_of(((z2 * 2 + z) * 2 + x) * 16, 16)
+            out_ref[z2 * 16 : z2 * 16 + 16, :] = sum_ref[pl.ds(row, 16), :].astype(out_ref.dtype)
+
+
+def last_sum_kernel(bits_ref, mine_ref, gx_ref, gz_ref, gd_ref, kept_ref, sent_ref, sum_ref):
+    sum_ref[...] = (
+        mine_ref[...] + gx_ref[...].astype(F32) + gz_ref[...].astype(F32) + gd_ref[...].astype(F32)
+    )
+    z2 = bits_ref[0]
+    kept_ref[...] = sum_ref[pl.ds(pl.multiple_of(z2 * 16, 16), 16), :]
+    sent_ref[...] = sum_ref[pl.ds(pl.multiple_of((1 - z2) * 16, 16), 16), :].astype(BF16)
+
+
+def call(kernel, outs, scalars, flops, *args, scratch=()):
     specs = [SMEM] * scalars + [VMEM] * (len(args) - scalars)
     return pl.pallas_call(
         kernel,
         out_shape=[jax.ShapeDtypeStruct(s, d) for s, d in outs],
         in_specs=specs,
         out_specs=[VMEM] * len(outs),
+        scratch_shapes=list(scratch),
         compiler_params=pltpu.CompilerParams(vmem_limit_bytes=20 << 20),
         cost_estimate=pl.CostEstimate(flops=flops, bytes_accessed=4 << 20, transcendentals=0),
     )(*args)
 
 
-def attend(own, prev, query, out_grad, up_weight, start, z0):
+def attend(own, prev, query, out_grad, up_weight, start, bits):
     square = (HEADS, TOK, 256)
+    columns = HEADS * PAIR
     keo, qe, e, dp, lg = call(
         own_kernel,
         [(square, BF16), (square, BF16), (square, F32), (square, F32), ((8, TOK), F32)],
         0, 470_000_000, start, own, query, out_grad, up_weight,
     )
-    kep, ds, dkv, latent, theirs = call(
+    kep, ds, latent, mine, *pieces = call(
         window_kernel,
         [
             (square, BF16),
             ((HEADS, 2, TOK, TOK), BF16),
-            ((2, TOK, HEADS * PAIR), BF16),
             ((TOK, 2 * LATENT + 2 * ROPE), BF16),
-            ((TOK, HEADS * PAIR), BF16),
+            ((128, columns), F32),
+            ((128, columns), BF16),
+            ((128, columns), BF16),
+            ((128, columns), BF16),
         ],
-        1, 1_700_000_000, z0, start, prev, own, qe, out_grad, up_weight, e, dp, lg,
-    )
-    return latent, theirs, (prev, own, kep, keo, ds, dkv)
-
-
-def finish(z0, saved):
-    return call(
-        rest_kernel,
-        [((TOK, HEADS * WIDTH), BF16), ((TOK, HEADS * PAIR), F32)],
-        1, 540_000_000, z0, *saved,
-    )
+        1, 2_000_000_000, bits, start, prev, own, qe, out_grad, up_weight, e, dp, lg,
+        scratch=[pltpu.VMEM((2, TOK, columns), BF16)],
+    )
+    return latent, mine, pieces, (kep, keo, ds)
+
+
+def query_grad(saved):
+    return call(query_kernel, [((TOK, HEADS * WIDTH), BF16)], 0, 270_000_000, *saved)[0]
+
+
+def flip(x, mask):
+    return lax.ppermute(x, CTX, [(i, i ^ mask) for i in range(32)])
 
 
 def body(compressed, query, out_grad, up_weight, lengths):
     ctx_rank = lax.axis_index(CTX)
-    z0 = lax.axis_index("z0").reshape(1)
+    bits = jnp.stack([lax.axis_index(name) for name in CTX]).astype(jnp.int32)
     own = compressed.T
     prev = ctx_shift(own, 1)
 
@@ -185,24 +217,39 @@
     start = jnp.sum(jnp.where(ends[:, None] <= query_pos[None, :], lengths[:, None], 0), axis=0)
     start = (start - first_pos)[None, :]
 
-    latent, theirs, saved = attend(own, prev, query, out_grad, up_weight, start, z0)
-    got = lax.ppermute(theirs, CTX, [(i, i ^ 4) for i in range(32)])
+    columns = HEADS * PAIR
+    latent, mine, pieces, saved = attend(own, prev, query, out_grad, up_weight, start, bits)
+    got_x = flip(pieces[0], 1)
+    got_z = flip(pieces[1], 4)
+    got_d = flip(pieces[2], 5)
     parts = lax.all_to_all(latent.reshape(32, 8, -1), HEAD, 0, 0)
-    dq, mine = finish(z0, saved)
-    both = (mine + got.astype(F32)).astype(BF16).reshape(16, 16, -1)
-    sixteenths = lax.all_to_all(both, ("zh", "x1", "x0"), 0, 0)
+    dq = query_grad(saved)
+    kept, *sends = call(
+        quad_sum_kernel,
+        [((32, columns), F32)] + [((32, columns), BF16)] * 3,
+        1, 1_000_000, bits, mine, got_x, got_z, got_d,
+        scratch=[pltpu.VMEM((128, columns), F32)],
+    )
+    far_x = flip(sends[0], 2)
+    far_z = flip(sends[1], 8)
+    far_d = flip(sends[2], 10)
+    last, sent = call(
+        last_sum_kernel,
+        [((16, columns), F32), ((16, columns), BF16)],
+        1, 1_000_000, bits, kept, far_x, far_z, far_d,
+        scratch=[pltpu.VMEM((32, columns), F32)],
+    )
+    grad_weight = last + flip(sent, 16).astype(F32)
     summed = jnp.sum(parts.astype(F32), axis=0)
-    kept = jnp.concatenate([summed[:, :LATENT], summed[:, 2 * LATENT : 2 * LATENT + ROPE]], axis=1)
-    sent = jnp.concatenate([summed[:, LATENT : 2 * LATENT], summed[:, 2 * LATENT + ROPE :]], axis=1)
-    grad_compressed = kept + ctx_shift(sent, -1)
-    grad_weight = jnp.sum(sixteenths.astype(F32), axis=0)
+    rope = 2 * LATENT + ROPE
+    keep = jnp.concatenate([summed[:, :LATENT], summed[:, 2 * LATENT : rope]], axis=1)
+    give = jnp.concatenate([summed[:, LATENT : 2 * LATENT], summed[:, rope:]], axis=1)
+    grad_compressed = keep + ctx_shift(give, -1)
     return dq, grad_compressed, grad_weight
 
 
 def solution(mesh):
-    fine = Mesh(
-        mesh.devices.reshape(4, 2, 2, 2, 2, 8, 2), ("zh", "z0", "x1", "x0", "xh", "y", "core")
-    )
+    fine = Mesh(mesh.devices.reshape(2, 2, 2, 2, 2, 2, 8, 2), CTX + HEAD)
     placed = (P(CTX, None), P(CTX, HEAD), P(CTX, HEAD), P(None, HEAD), P())
     return jax.shard_map(
         body,

time: 88.7 us -> 105 us (1.18)
  the two profiles are of different devices: /device:TPU:14 before, /device:TPU:6 now
where the time goes in v3:
time: 105 us; the launch traced here: 104 us
  starting transfers between devices  58.9 us (56%)
  waiting for transfers between devices  26.5 us (25%)
  Pallas kernels  8.11 us (8%)
  local copies, waits for them, and re-layouts  6.13 us (6%)
  other arithmetic  3.43 us (3%)
    ppermute x7, starting transfers between devices, flip(): return lax.ppermute(x, CTX, [(i, i ^ mask) for i in range(32)])  38.8 us
    ppermute x7, waiting for transfers between devices, flip(): return lax.ppermute(x, CTX, [(i, i ^ mask) for i in range(32)])  20.7 us
    all_to_all x1, starting transfers between devices, body(): parts = lax.all_to_all(latent.reshape(32, 8, -1), HEAD, 0, 0)  13.1 us
    pallas_call x5, Pallas kernels, call(): pl.pallas_call(kernel, out_shape=[jax.ShapeDtypeStruct(s, d) for s, d in...  8.11 us
    ppermute x2, starting transfers between devices, ctx_shift(): return lax.ppermute(x, CTX, pairs)  7.03 us
    ppermute x2, waiting for transfers between devices, ctx_shift(): return lax.ppermute(x, CTX, pairs)  5.8 us
    unnamed x14, local copies, waits for them, and re-layouts  5.21 us
  transfers between devices with their start and end apart: 10, of which 4 were waited for; matrix products, arithmetic and copies ran while one was open for 4% of the time, Pallas kernels for 3%

profile of v3, /device:TPU:6, one launch (start us, length us, event | category | flops | bytes accessed | tf_op | source)
XLA Modules:
  0.0 103.9 jit_solution(9815747984858716363)
XLA Ops:
  0.6 5.1 %collective-permute-start = (bf16[576,256]{1,0:T(8,128)(2,1)}, bf16[576,256]{1,0:T(8,128)(2,1)S(1)}, u32[]{:S(2)}, u32[]{:S(2)}) collective-permute-start(bf16[576,256]{1,0:T(8,128)(2,1)} %bitcast.9), channel_id=1, source_target_pairs={{0,32},{32,64},{64,96},{96,128},{128,160},{160,192},{192,224},{224... | collective-permute-start | bytes 884744 | tf_op jit(solution)/shard_map/ppermute | solution.py:37
  5.8 0.8 copy.10
  6.8 0.8 select_reduce_fusion
  7.6 1.2 %copy-done = bf16[512,1024]{1,0:T(8,128)(2,1)S(1)} copy-done((bf16[512,1024]{1,0:T(8,128)(2,1)S(1)}, bf16[512,1024]{1,0:T(8,128)(2,1)}, u32[]{:S(2)}) %copy-start) | copy-done | bytes 1048600
  8.9 1.0 copy-done.2
  9.9 1.0 copy-done.3
  10.8 0.9 copy-done.4
  11.8 0.8 shard_map.76
  13.0 4.7 %shard_map.77 = (bf16[4,256,256]{2,1,0:T(8,128)(2,1)S(1)}, bf16[4,2,256,256]{3,2,1,0:T(8,128)(2,1)S(1)}, bf16[256,1152]{1,0:T(8,128)(2,1)}, f32[128,1024]{1,0:T(...) custom-call(s32[5]{0:T(128)S(1)} %stack.23.bits_ref, ...), custom_call_target="tpu_custom_call" | custom-call | flops 2000000000 | bytes 4194304 | tf_op jit(solution)/shard_map/pallas_call | solution.py:164
  18.4 13.1 %all-to-all-start = ((bf16[32,8,1152]{2,1,0:T(8,128)(2,1)}), bf16[32,8,1152]{2,1,0:T(8,128)(2,1)}, u32[]{:S(2)}, u32[]{:S(2)}) async-start(bf16[32,8,1152]{2,1,0:T(8,128)(2,1)} %bitcast.8), calls=%async_computation | async-start | bytes 1179648 | tf_op jit(solution)/shard_map/all_to_all | solution.py:225
  31.5 1.9 %collective-permute-start.2 = (bf16[128,1024]{1,0:T(8,128)(2,1)S(1)}, bf16[128,1024]{1,0:T(8,128)(2,1)S(1)}, u32[]{:S(2)}, u32[]{:S(2)}) collective-permute-start(bf16[128,1024]{1,0:T(8,128)(2,1)S(1)} %copy-done.6), channel_id=1, source_target_pairs={{0,32},{32,0},{64,96},{96,64},{128,160},{160,128},{192,224},{224,1... | collective-permute-start | bytes 786440 | tf_op jit(solution)/shard_map/ppermute | solution.py:205
  33.4 5.2 %collective-permute-start.3 = (bf16[128,1024]{1,0:T(8,128)(2,1)S(1)}, bf16[128,1024]{1,0:T(8,128)(2,1)S(1)}, u32[]{:S(2)}, u32[]{:S(2)}) collective-permute-start(bf16[128,1024]{1,0:T(8,128)(2,1)S(1)} %get-tuple-element.31), channel_id=1, source_target_pairs={{0,128},{32,160},{64,192},{96,224},{128,0},{160,32},{192,64},{224,... | collective-permute-start | bytes 786440 | tf_op jit(solution)/shard_map/ppermute | solution.py:205
  38.6 3.4 %collective-permute-start.4 = (bf16[128,1024]{1,0:T(8,128)(2,1)S(1)}, bf16[128,1024]{1,0:T(8,128)(2,1)S(1)}, u32[]{:S(2)}, u32[]{:S(2)}) collective-permute-start(bf16[128,1024]{1,0:T(8,128)(2,1)S(1)} %get-tuple-element.32), channel_id=1, source_target_pairs={{0,160},{32,128},{64,224},{96,192},{128,32},{160,0},{192,96},{224,... | collective-permute-start | bytes 786440 | tf_op jit(solution)/shard_map/ppermute | solution.py:205
  42.0 8.7 %collective-permute-done.2.gx_ref = bf16[128,1024]{1,0:T(8,128)(2,1)S(1)} collective-permute-done((bf16[128,1024]{1,0:T(8,128)(2,1)S(1)}, bf16[128,1024]{1,0:T(8,128)(2,1)S(1)}, u32[]{:S(2)}, u32[]{:S(2)}) %collective-permute-start.2) | collective-permute-done | bytes 262176 | tf_op jit(solution)/shard_map/ppermute | solution.py:205
  50.7 5.7 %collective-permute-done.4.gd_ref = bf16[128,1024]{1,0:T(8,128)(2,1)S(1)} collective-permute-done((bf16[128,1024]{1,0:T(8,128)(2,1)S(1)}, bf16[128,1024]{1,0:T(8,128)(2,1)S(1)}, u32[]{:S(2)}, u32[]{:S(2)}) %collective-permute-start.4) | collective-permute-done | bytes 262176 | tf_op jit(solution)/shard_map/ppermute | solution.py:205
  57.2 6.9 %collective-permute-start.5 = (bf16[32,1024]{1,0:T(8,128)(2,1)S(1)}, bf16[32,1024]{1,0:T(8,128)(2,1)S(1)}, u32[]{:S(2)}, u32[]{:S(2)}) collective-permute-start(bf16[32,1024]{1,0:T(8,128)(2,1)S(1)} %get-tuple-element.34), channel_id=1, source_target_pairs={{0,64},{32,96},{64,0},{96,32},{128,192},{160,224},{192,128},{224,1... | collective-permute-start | bytes 196616 | tf_op jit(solution)/shard_map/ppermute | solution.py:205
  64.1 7.9 %collective-permute-start.6 = (bf16[32,1024]{1,0:T(8,128)(2,1)S(1)}, bf16[32,1024]{1,0:T(8,128)(2,1)S(1)}, u32[]{:S(2)}, u32[]{:S(2)}) collective-permute-start(bf16[32,1024]{1,0:T(8,128)(2,1)S(1)} %get-tuple-element.35), channel_id=1, source_target_pairs={{0,256},{32,288},{64,320},{96,352},{128,384},{160,416},{192,448},{... | collective-permute-start | bytes 196616 | tf_op jit(solution)/shard_map/ppermute | solution.py:205
  72.0 1.9 %collective-permute-start.7 = (bf16[32,1024]{1,0:T(8,128)(2,1)S(1)}, bf16[32,1024]{1,0:T(8,128)(2,1)S(1)}, u32[]{:S(2)}, u32[]{:S(2)}) collective-permute-start(bf16[32,1024]{1,0:T(8,128)(2,1)S(1)} %get-tuple-element.36), channel_id=1, source_target_pairs={{0,320},{32,352},{64,256},{96,288},{128,448},{160,480},{192,384},{... | collective-permute-start | bytes 196616 | tf_op jit(solution)/shard_map/ppermute | solution.py:205
  73.9 1.3 %shard_map.78 = bf16[256,768]{1,0:T(8,128)(2,1)} custom-call(bf16[4,256,256]{2,1,0:T(8,128)(2,1)S(1)} %get-tuple-element.25.kep_ref, bf16[4,256,256]{2,1,0:T(8,128)(2,1)S(1)} %get-tuple-element.26.keo_ref, bf16[4,2,256,256]{3,2,1,0:T(8,128)(2,1)S(1)} %get-tuple-element.27.ds_ref), custom_call_target="tpu_custom_call" | custom-call | flops 270000000 | bytes 4194304 | tf_op jit(solution)/shard_map/pallas_call | solution.py:164
  75.2 6.3 %collective-permute-done.7.gd_ref = bf16[32,1024]{1,0:T(8,128)(2,1)S(1)} collective-permute-done((bf16[32,1024]{1,0:T(8,128)(2,1)S(1)}, bf16[32,1024]{1,0:T(8,128)(2,1)S(1)}, u32[]{:S(2)}, u32[]{:S(2)}) %collective-permute-start.7) | collective-permute-done | bytes 65568 | tf_op jit(solution)/shard_map/ppermute | solution.py:205
  82.1 11.6 %collective-permute-start.8 = (bf16[16,1024]{1,0:T(8,128)(2,1)S(1)}, bf16[16,1024]{1,0:T(8,128)(2,1)S(1)}, u32[]{:S(2)}, u32[]{:S(2)}) collective-permute-start(bf16[16,1024]{1,0:T(8,128)(2,1)S(1)} %get-tuple-element.38), channel_id=1, source_target_pairs={{0,512},{32,544},{64,576},{96,608},{128,640},{160,672},{192,704},{... | collective-permute-start | bytes 98312 | tf_op jit(solution)/shard_map/ppermute | solution.py:205
  93.7 1.2 %convert_reduce_fusion = f32[8,1152]{1,0:T(8,128)S(1)} fusion(bf16[32,8,1152]{2,1,0:T(8,128)(2,1)} %all-to-all-done), kind=kLoop, calls=%fused_computation | loop fusion | flops 580608 | bytes 626688 | tf_op jit(solution)/shard_map/reduce_sum | solution.py:243
  94.9 1.9 %collective-permute-start.1 = (f32[8,576]{1,0:T(8,128)S(1)}, f32[8,576]{1,0:T(8,128)S(1)}, u32[]{:S(2)}, u32[]{:S(2)}) collective-permute-start(f32[8,576]{1,0:T(8,128)S(1)} %pad_maximum_fusion), channel_id=1, source_target_pairs={{32,0},{64,32},{96,64},{128,96},{160,128},{192,160},{224,192},{256... | collective-permute-start | bytes 55304 | tf_op jit(solution)/shard_map/ppermute | solution.py:37
  97.5 5.8 %collective-permute-done.1 = f32[8,576]{1,0:T(8,128)S(1)} collective-permute-done((f32[8,576]{1,0:T(8,128)S(1)}, f32[8,576]{1,0:T(8,128)S(1)}, u32[]{:S(2)}, u32[]{:S(2)}) %collective-permute-start.1) | collective-permute-done | bytes 18464 | tf_op jit(solution)/shard_map/ppermute | solution.py:37
  (28 shorter events, 4.1 us)
Async XLA Ops:
  0.6 12.0 %collective-permute-start = (bf16[576,256]{1,0:T(8,128)(2,1)}, bf16[576,256]{1,0:T(8,128)(2,1)S(1)}, u32[]{:S(2)}, u32[]{:S(2)}) collective-permute-start(bf16[576,256]{1,0:T(8,128)(2,1)} %bitcast.9), channel_id=1, source_target_pairs={{0,32},{32,64},{64,96},{96,128},{128,160},{160,192},{192,224},{224... | collective-permute-start | bytes 884744 | tf_op jit(solution)/shard_map/ppermute | solution.py:37
  7.6 1.2 %copy-start = (bf16[512,1024]{1,0:T(8,128)(2,1)S(1)}, bf16[512,1024]{1,0:T(8,128)(2,1)}, u32[]{:S(2)}) copy-start(bf16[512,1024]{1,0:T(8,128)(2,1)} %w_ref.3) | copy-start | bytes 3145732
  8.9 1.0 copy-start.2
  9.9 1.0 copy-start.3
  10.8 0.9 copy-start.4
  11.8 1.2 %copy-start.1 = (bf16[512,1024]{1,0:T(8,128)(2,1)S(1)}, bf16[512,1024]{1,0:T(8,128)(2,1)}, u32[]{:S(2)}) copy-start(bf16[512,1024]{1,0:T(8,128)(2,1)} %w_ref.3) | copy-start | bytes 3145732
  17.7 0.7 copy-start.5
  18.4 13.1 %copy-start.6 = (bf16[128,1024]{1,0:T(8,128)(2,1)S(1)}, bf16[128,1024]{1,0:T(8,128)(2,1)}, u32[]{:S(2)}) copy-start(bf16[128,1024]{1,0:T(8,128)(2,1)} %copy-done.5) | copy-start | bytes 786436
  18.4 75.3 %all-to-all-start = ((bf16[32,8,1152]{2,1,0:T(8,128)(2,1)}), bf16[32,8,1152]{2,1,0:T(8,128)(2,1)}, u32[]{:S(2)}, u32[]{:S(2)}) async-start(bf16[32,8,1152]{2,1,0:T(8,128)(2,1)} %bitcast.8), calls=%async_computation | async-start | bytes 1179648 | tf_op jit(solution)/shard_map/all_to_all | solution.py:225
  31.5 19.2 %collective-permute-start.2 = (bf16[128,1024]{1,0:T(8,128)(2,1)S(1)}, bf16[128,1024]{1,0:T(8,128)(2,1)S(1)}, u32[]{:S(2)}, u32[]{:S(2)}) collective-permute-start(bf16[128,1024]{1,0:T(8,128)(2,1)S(1)} %copy-done.6), channel_id=1, source_target_pairs={{0,32},{32,0},{64,96},{96,64},{128,160},{160,128},{192,224},{224,1... | collective-permute-start | bytes 786440 | tf_op jit(solution)/shard_map/ppermute | solution.py:205
  33.4 17.3 %collective-permute-start.3 = (bf16[128,1024]{1,0:T(8,128)(2,1)S(1)}, bf16[128,1024]{1,0:T(8,128)(2,1)S(1)}, u32[]{:S(2)}, u32[]{:S(2)}) collective-permute-start(bf16[128,1024]{1,0:T(8,128)(2,1)S(1)} %get-tuple-element.31), channel_id=1, source_target_pairs={{0,128},{32,160},{64,192},{96,224},{128,0},{160,32},{192,64},{224,... | collective-permute-start | bytes 786440 | tf_op jit(solution)/shard_map/ppermute | solution.py:205
  38.6 17.8 %collective-permute-start.4 = (bf16[128,1024]{1,0:T(8,128)(2,1)S(1)}, bf16[128,1024]{1,0:T(8,128)(2,1)S(1)}, u32[]{:S(2)}, u32[]{:S(2)}) collective-permute-start(bf16[128,1024]{1,0:T(8,128)(2,1)S(1)} %get-tuple-element.32), channel_id=1, source_target_pairs={{0,160},{32,128},{64,224},{96,192},{128,32},{160,0},{192,96},{224,... | collective-permute-start | bytes 786440 | tf_op jit(solution)/shard_map/ppermute | solution.py:205
  57.2 18.0 %collective-permute-start.5 = (bf16[32,1024]{1,0:T(8,128)(2,1)S(1)}, bf16[32,1024]{1,0:T(8,128)(2,1)S(1)}, u32[]{:S(2)}, u32[]{:S(2)}) collective-permute-start(bf16[32,1024]{1,0:T(8,128)(2,1)S(1)} %get-tuple-element.34), channel_id=1, source_target_pairs={{0,64},{32,96},{64,0},{96,32},{128,192},{160,224},{192,128},{224,1... | collective-permute-start | bytes 196616 | tf_op jit(solution)/shard_map/ppermute | solution.py:205
  64.1 11.1 %collective-permute-start.6 = (bf16[32,1024]{1,0:T(8,128)(2,1)S(1)}, bf16[32,1024]{1,0:T(8,128)(2,1)S(1)}, u32[]{:S(2)}, u32[]{:S(2)}) collective-permute-start(bf16[32,1024]{1,0:T(8,128)(2,1)S(1)} %get-tuple-element.35), channel_id=1, source_target_pairs={{0,256},{32,288},{64,320},{96,352},{128,384},{160,416},{192,448},{... | collective-permute-start | bytes 196616 | tf_op jit(solution)/shard_map/ppermute | solution.py:205
  72.0 9.5 %collective-permute-start.7 = (bf16[32,1024]{1,0:T(8,128)(2,1)S(1)}, bf16[32,1024]{1,0:T(8,128)(2,1)S(1)}, u32[]{:S(2)}, u32[]{:S(2)}) collective-permute-start(bf16[32,1024]{1,0:T(8,128)(2,1)S(1)} %get-tuple-element.36), channel_id=1, source_target_pairs={{0,320},{32,352},{64,256},{96,288},{128,448},{160,480},{192,384},{... | collective-permute-start | bytes 196616 | tf_op jit(solution)/shard_map/ppermute | solution.py:205
  82.1 14.8 %collective-permute-start.8 = (bf16[16,1024]{1,0:T(8,128)(2,1)S(1)}, bf16[16,1024]{1,0:T(8,128)(2,1)S(1)}, u32[]{:S(2)}, u32[]{:S(2)}) collective-permute-start(bf16[16,1024]{1,0:T(8,128)(2,1)S(1)} %get-tuple-element.38), channel_id=1, source_target_pairs={{0,512},{32,544},{64,576},{96,608},{128,640},{160,672},{192,704},{... | collective-permute-start | bytes 98312 | tf_op jit(solution)/shard_map/ppermute | solution.py:205
  94.9 8.4 %collective-permute-start.1 = (f32[8,576]{1,0:T(8,128)S(1)}, f32[8,576]{1,0:T(8,128)S(1)}, u32[]{:S(2)}, u32[]{:S(2)}) collective-permute-start(f32[8,576]{1,0:T(8,128)S(1)} %pad_maximum_fusion), channel_id=1, source_target_pairs={{32,0},{64,32},{96,64},{128,96},{160,128},{192,160},{224,192},{256... | collective-permute-start | bytes 55304 | tf_op jit(solution)/shard_map/ppermute | solution.py:37

commit v4 on v2

v4 whole, which is shorter than its diff:
```python
import math

import jax
import jax.numpy as jnp
from jax import lax
from jax.experimental import pallas as pl
from jax.experimental.pallas import tpu as pltpu
from jax.sharding import Mesh
from jax.sharding import PartitionSpec as P


LATENT = 512
ROPE = 64
NOPE = 128
VDIM = 128
HEADS = 4
TOK = 256
PAIR = NOPE + VDIM
WIDTH = NOPE + ROPE
SCALING = 1.0 / math.sqrt(WIDTH)
CTX = ("z2", "z1", "z0", "x1", "x0")
HEAD = ("xh", "y", "core")
F32 = jnp.float32
BF16 = jnp.bfloat16
NT = (((1,), (1,)), ((), ()))
TN = (((0,), (0,)), ((), ()))
VMEM = pl.BlockSpec(memory_space=pltpu.VMEM)


def dot(a, b, dims=(((1,), (0,)), ((), ()))):
    return lax.dot_general(a, b, dims, preferred_element_type=F32)


def ctx_shift(x, by):
    pairs = [(i, i + by) for i in range(32) if 0 <= i + by < 32]
    return lax.ppermute(x, CTX, pairs)


def iota(shape, dim):
    return lax.broadcasted_iota(jnp.int32, shape, dim)


def keys_and_values(xt_ref, w_ref, ke_ref):
    kv = dot(xt_ref[:LATENT, :], w_ref[...], TN).astype(BF16)
    rope = jnp.concatenate([xt_ref[LATENT:, :].astype(F32), jnp.zeros((ROPE, TOK), F32)], axis=0)
    rope = jnp.transpose(rope).astype(BF16)
    values = []
    for h in range(HEADS):
        ke_ref[h, :, :NOPE] = kv[:, h * PAIR : h * PAIR + NOPE]
        ke_ref[h, :, NOPE:] = rope
        values.append(kv[:, h * PAIR + NOPE : (h + 1) * PAIR])
    return values


def first_visible(len_ref):
    docs = len_ref.shape[1]
    lengths = jnp.broadcast_to(len_ref[...].astype(F32), (docs, docs))
    row, col = iota((docs, docs), 0), iota((docs, docs), 1)
    ends = jnp.sum(jnp.where(col <= row, lengths, 0.0), axis=1, keepdims=True)
    each = jnp.sum(jnp.where(col == row, lengths, 0.0), axis=1, keepdims=True)
    first = lax.axis_index(CTX) * TOK
    query = (iota((docs, TOK), 1) + first).astype(F32)
    before = jnp.sum(jnp.where(ends <= query, each, 0.0), axis=0, keepdims=True)
    return before.astype(jnp.int32) - first


def own_kernel(
    len_ref, xt_ref, q_ref, do_ref, w_ref, ke_ref, qe_ref, e_ref, dp_ref, lg_ref, start_ref
):
    start_ref[...] = first_visible(len_ref)
    lane = iota((TOK, 256), 1)
    for h in range(HEADS):
        base = (h // 2) * 2 * WIDTH
        if h % 2 == 0:
            rows = q_ref[:, base : base + 256].astype(F32)
        else:
            rows = pltpu.roll(q_ref[:, base + 128 : base + 384].astype(F32), 192, 1)
        qe_ref[h] = jnp.where(lane < WIDTH, rows, 0.0).astype(BF16)
    values = keys_and_values(xt_ref, w_ref, ke_ref)
    key = iota((TOK, TOK), 0)
    seen = (key >= start_ref[...]) & (key <= iota((TOK, TOK), 1))
    for h in range(HEADS):
        scores = dot(ke_ref[h], qe_ref[h], NT) * SCALING
        e = jnp.where(seen, jnp.exp(scores), 0.0)
        dp = dot(values[h], do_ref[:, h * VDIM : (h + 1) * VDIM], NT)
        e_ref[h] = e
        dp_ref[h] = dp
        lg_ref[h : h + 1, :] = jnp.sum(e, axis=0, keepdims=True)
        lg_ref[h + 4 : h + 5, :] = jnp.sum(e * dp, axis=0, keepdims=True)


def rows_of(xt_ref, z0=None, x0=None):
    if x0 is None:
        starts, size = [(2 * i + z0) * 64 for i in range(4)], 64
    else:
        starts, size = [(2 * i + x0) * 16 for i in range(16)], 16
    rows = [xt_ref[pl.ds(pl.multiple_of(at, size), size), :] for at in starts]
    return jnp.concatenate(rows, axis=0)


def window_kernel(
    xt_ref, start_ref, own_ref, qe_ref, do_ref, w_ref, e_ref, dp_ref, lg_ref,
    ke_ref, ds_ref, dkv_ref, lat_mine_ref, lat_ref, theirs_a_ref, theirs_b_ref, xm_ref,
    total_ref,
):
    values = keys_and_values(xt_ref, w_ref, ke_ref)
    seen = iota((TOK, TOK), 0) - TOK >= start_ref[...]
    rope_grads = [jnp.zeros((TOK, 128), F32), jnp.zeros((TOK, 128), F32)]
    for h in range(HEADS):
        qe = qe_ref[h]
        do = do_ref[:, h * VDIM : (h + 1) * VDIM]
        scores = dot(ke_ref[h], qe, NT) * SCALING
        e = jnp.where(seen, jnp.exp(scores), 0.0)
        dp = dot(values[h], do, NT)
        norm = 1.0 / (lg_ref[h : h + 1, :] + jnp.sum(e, axis=0, keepdims=True))
        delta = (lg_ref[h + 4 : h + 5, :] + jnp.sum(e * dp, axis=0, keepdims=True)) * norm
        for half in range(2):
            if half == 1:
                e, dp = e_ref[h], dp_ref[h]
            probs = e * norm
            ds = (probs * (dp - delta) * SCALING).astype(BF16)
            ds_ref[h, half] = ds
            dk = dot(ds, qe)
            dkv_ref[half, :, h * PAIR : h * PAIR + NOPE] = dk[:, :NOPE].astype(BF16)
            rope_grads[half] = rope_grads[half] + dk[:, NOPE:]
            dkv_ref[half, :, h * PAIR + NOPE : (h + 1) * PAIR] = dot(
                probs.astype(BF16), do
            ).astype(BF16)
    z0, x0, core = (lax.axis_index(name) for name in ("z0", "x0", "core"))
    total_ref[:, :LATENT] = dot(dkv_ref[1], w_ref[...], NT)
    total_ref[:, LATENT : 2 * LATENT] = dot(dkv_ref[0], w_ref[...], NT)
    total_ref[:, 2 * LATENT :] = rope_grads[1] + pltpu.roll(rope_grads[0], ROPE, 1)
    for out_ref, parity in ((lat_mine_ref, core), (lat_ref, 1 - core)):
        for i in range(8):
            pair = [
                total_ref[pl.ds(pl.multiple_of((4 * i + 2 * j + parity) * 8, 8), 8), :]
                for j in range(2)
            ]
            out_ref[16 * i : 16 * i + 16, :] = jnp.concatenate(pair, axis=0).astype(out_ref.dtype)
    cut = HEADS * PAIR // 2
    sources = (xt_ref, own_ref)
    theirs_a_ref[...] = sum(
        dot(rows_of(sources[u], z0=1 - z0), dkv_ref[u, :, :cut]) for u in range(2)
    ).astype(BF16)
    theirs_b_ref[...] = sum(
        dot(rows_of(sources[u], x0=1 - x0), dkv_ref[u, :, cut:]) for u in range(2)
    ).astype(BF16)
    for u in range(2):
        xm_ref[0, u] = rows_of(sources[u], z0=z0)
        xm_ref[1, u] = rows_of(sources[u], x0=x0)


def core_sum_kernel(mine_ref, got_ref, out_ref):
    out_ref[...] = (mine_ref[...] + got_ref[...].astype(F32)).astype(BF16)


def query_kernel(kep_ref, keo_ref, ds_ref, dq_ref):
    for pair in range(HEADS // 2):
        parts = []
        for h in (2 * pair, 2 * pair + 1):
            parts.append(dot(ds_ref[h, 0], kep_ref[h], TN) + dot(ds_ref[h, 1], keo_ref[h], TN))
        moved = pltpu.roll(parts[1], ROPE, 1)
        base = pair * 2 * WIDTH
        dq_ref[:, base : base + 128] = parts[0][:, :128].astype(BF16)
        dq_ref[:, base + 128 : base + 256] = (parts[0][:, 128:] + moved[:, :128]).astype(BF16)
        dq_ref[:, base + 256 : base + 384] = moved[:, 128:].astype(BF16)


def first_sum_kernel(
    xm_ref, dkv_ref, got_a_ref, got_b_ref, kept_ref, send_a_ref, send_b_ref, a_ref, b_ref
):
    cut = HEADS * PAIR // 2
    a_ref[...] = got_a_ref[...].astype(F32) + sum(
        dot(xm_ref[0, u], dkv_ref[u, :, :cut]) for u in range(2)
    )
    b_ref[...] = got_b_ref[...].astype(F32) + sum(
        dot(xm_ref[1, u], dkv_ref[u, :, cut:]) for u in range(2)
    )
    z0, x0 = lax.axis_index("z0"), lax.axis_index("x0")
    for i in range(8):
        rows = slice(16 * i, 16 * i + 16)

        def of_a(x):
            return a_ref[pl.ds(pl.multiple_of((2 * i + x) * 16, 16), 16), :]

        def of_b(z):
            at = (i // 2) * 64 + z * 32 + (i % 2) * 16
            return b_ref[pl.ds(pl.multiple_of(at, 16), 16), :]

        kept_ref[rows, :cut] = of_a(x0)
        kept_ref[rows, cut:] = of_b(z0)
        send_a_ref[rows, :] = of_a(1 - x0).astype(BF16)
        send_b_ref[rows, :] = of_b(1 - z0).astype(BF16)


def second_sum_kernel(kept_ref, got_a_ref, got_b_ref, out_ref):
    cut = HEADS * PAIR // 2
    out_ref[:, :cut] = (kept_ref[:, :cut] + got_a_ref[...].astype(F32)).astype(BF16)
    out_ref[:, cut:] = (kept_ref[:, cut:] + got_b_ref[...].astype(F32)).astype(BF16)


def call(kernel, outs, flops, *args, scratch=()):
    return pl.pallas_call(
        kernel,
        out_shape=[jax.ShapeDtypeStruct(s, d) for s, d in outs],
        in_specs=[VMEM] * len(args),
        out_specs=[VMEM] * len(outs),
        scratch_shapes=list(scratch),
        compiler_params=pltpu.CompilerParams(vmem_limit_bytes=20 << 20),
        cost_estimate=pl.CostEstimate(flops=flops, bytes_accessed=4 << 20, transcendentals=0),
    )(*args)


def attend(own, prev, query, out_grad, up_weight, lengths):
    square = (HEADS, TOK, 256)
    columns = HEADS * PAIR
    keo, qe, e, dp, lg, start = call(
        own_kernel,
        [
            (square, BF16),
            (square, BF16),
            (square, F32),
            (square, F32),
            ((8, TOK), F32),
            ((1, TOK), jnp.int32),
        ],
        470_000_000, lengths.reshape(1, -1), own, query, out_grad, up_weight,
    )
    kep, ds, dkv, lat_mine, lat_theirs, theirs_a, theirs_b, xm = call(
        window_kernel,
        [
            (square, BF16),
            ((HEADS, 2, TOK, TOK), BF16),
            ((2, TOK, columns), BF16),
            ((TOK // 2, 2 * LATENT + 2 * ROPE), F32),
            ((TOK // 2, 2 * LATENT + 2 * ROPE), BF16),
            ((TOK, columns // 2), BF16),
            ((TOK, columns // 2), BF16),
            ((2, 2, TOK, TOK), BF16),
        ],
        1_700_000_000, prev, start, own, qe, out_grad, up_weight, e, dp, lg,
        scratch=[pltpu.VMEM((TOK, 2 * LATENT + 2 * ROPE), F32)],
    )
    return lat_mine, lat_theirs, theirs_a, theirs_b, (xm, dkv), (kep, keo, ds)


def query_grad(saved):
    return call(query_kernel, [((TOK, HEADS * WIDTH), BF16)], 270_000_000, *saved)[0]


def flip(x, mask):
    return lax.ppermute(x, CTX, [(i, i ^ mask) for i in range(32)])


def body(compressed, query, out_grad, up_weight, lengths):
    own = compressed.T
    prev = ctx_shift(own, 1)

    columns = HEADS * PAIR
    lat_mine, lat_theirs, theirs_a, theirs_b, factors, saved = attend(
        own, prev, query, out_grad, up_weight, lengths
    )
    got_core = lax.ppermute(lat_theirs, "core", [(0, 1), (1, 0)])
    got_a = flip(theirs_a, 4)
    got_b = flip(theirs_b, 1)
    (latent,) = call(core_sum_kernel, [(lat_mine.shape, BF16)], 1_000_000, lat_mine, got_core)
    parts = lax.all_to_all(latent.reshape(16, 8, -1), ("xh", "y"), 0, 0)
    kept, send_a, send_b = call(
        first_sum_kernel,
        [((128, columns), F32), ((128, columns // 2), BF16), ((128, columns // 2), BF16)],
        270_000_000, *factors, got_a, got_b,
        scratch=[pltpu.VMEM((TOK, columns // 2), F32)] * 2,
    )
    next_a = flip(send_a, 1)
    next_b = flip(send_b, 4)
    dq = query_grad(saved)
    (eighth,) = call(second_sum_kernel, [((128, columns), BF16)], 1_000_000, kept, next_a, next_b)
    eighths = lax.all_to_all(eighth.reshape(8, 16, -1), ("z2", "z1", "x1"), 0, 0)
    summed = jnp.sum(parts.astype(F32), axis=0)
    grad_weight = jnp.sum(eighths.astype(F32), axis=0)
    rope = 2 * LATENT + ROPE
    keep = jnp.concatenate([summed[:, :LATENT], summed[:, 2 * LATENT : rope]], axis=1)
    give = jnp.concatenate([summed[:, LATENT : 2 * LATENT], summed[:, rope:]], axis=1)
    grad_compressed = keep + ctx_shift(give, -1)
    return dq, grad_compressed, grad_weight


def solution(mesh):
    fine = Mesh(mesh.devices.reshape(2, 2, 2, 2, 2, 2, 8, 2), CTX + HEAD)
    placed = (P(CTX, None), P(CTX, HEAD), P(CTX, HEAD), P(None, HEAD), P())
    return jax.shard_map(
        body,
        mesh=fine,
        in_specs=placed,
        out_specs=(P(CTX, HEAD), P(CTX + HEAD, None), P(CTX, HEAD)),
        check_vma=False,
    )
```

time: 88.7 us -> 90.9 us (1.025)
  the two profiles are of different devices: /device:TPU:14 before, /device:TPU:16 now
where the time goes in v4:
time: 90.9 us; the launch traced here: 90.2 us
  starting transfers between devices  52.1 us (57%)
  waiting for transfers between devices  22.3 us (25%)
  Pallas kernels  7.41 us (8%)
  local copies, waits for them, and re-layouts  5.26 us (6%)
  other arithmetic  2.3 us (3%)
    ppermute x4, starting transfers between devices, flip(): return lax.ppermute(x, CTX, [(i, i ^ mask) for i in range(32)])  17 us
    all_to_all x1, starting transfers between devices, body(): lax.all_to_all(eighth.reshape(8, 16, -1), ('z2', 'z1', 'x1'), 0, 0)  14.9 us
    all_to_all x1, starting transfers between devices, body(): parts = lax.all_to_all(latent.reshape(16, 8, -1), ('xh', 'y'), 0, 0)  13.7 us
    all_to_all x1, waiting for transfers between devices, body(): lax.all_to_all(eighth.reshape(8, 16, -1), ('z2', 'z1', 'x1'), 0, 0)  9.97 us
    ppermute x4, waiting for transfers between devices, flip(): return lax.ppermute(x, CTX, [(i, i ^ mask) for i in range(32)])  9.22 us
    pallas_call x6, Pallas kernels, call(): pl.pallas_call(kernel, out_shape=[jax.ShapeDtypeStruct(s, d) for s, d in...  7.41 us
    unnamed x20, local copies, waits for them, and re-layouts  5.19 us
    ppermute x2, starting transfers between devices, ctx_shift(): return lax.ppermute(x, CTX, pairs)  4.7 us
  transfers between devices with their start and end apart: 9, of which 6 were waited for; matrix products, arithmetic and copies ran while one was open for 2% of the time, Pallas kernels for 4%

profile of v4, /device:TPU:16, one launch (start us, length us, event | category | flops | bytes accessed | tf_op | source)
XLA Modules:
  0.0 90.2 jit_solution(14953978792953714539)
XLA Ops:
  0.6 3.4 %collective-permute-start = (bf16[576,256]{1,0:T(8,128)(2,1)}, bf16[576,256]{1,0:T(8,128)(2,1)S(1)}, u32[]{:S(2)}, u32[]{:S(2)}) collective-permute-start(bf16[576,256]{1,0:T(8,128)(2,1)} %bitcast.4), channel_id=1, source_target_pairs={{0,32},{32,64},{64,96},{96,128},{128,160},{160,192},{192,224},{224... | collective-permute-start | bytes 884744 | tf_op jit(solution)/shard_map/ppermute | solution.py:36
  4.1 1.2 %copy-done = bf16[512,1024]{1,0:T(8,128)(2,1)S(1)} copy-done((bf16[512,1024]{1,0:T(8,128)(2,1)S(1)}, bf16[512,1024]{1,0:T(8,128)(2,1)}, u32[]{:S(2)}) %copy-start) | copy-done | bytes 1048600
  5.3 1.0 %copy-done.4 = bf16[256,768]{1,0:T(8,128)(2,1)S(1)} copy-done((bf16[256,768]{1,0:T(8,128)(2,1)S(1)}, bf16[256,768]{1,0:T(8,128)(2,1)}, u32[]{:S(2)}) %copy-start.4) | copy-done | bytes 393240
  6.3 1.0 %copy-done.5 = bf16[256,576]{0,1:T(8,128)(2,1)S(1)} copy-done((bf16[256,576]{0,1:T(8,128)(2,1)S(1)}, bf16[256,576]{0,1:T(8,128)(2,1)}, u32[]{:S(2)}) %copy-start.5) | copy-done | bytes 294936
  7.3 0.9 %copy-done.7 = bf16[256,512]{1,0:T(8,128)(2,1)S(1)} copy-done((bf16[256,512]{1,0:T(8,128)(2,1)S(1)}, bf16[256,512]{1,0:T(8,128)(2,1)}, u32[]{:S(2)}) %copy-start.7) | copy-done | bytes 262168
  8.2 0.8 shard_map.76
  9.0 1.6 %collective-permute-done.xt_ref = bf16[576,256]{1,0:T(8,128)(2,1)S(1)} collective-permute-done((bf16[576,256]{1,0:T(8,128)(2,1)}, bf16[576,256]{1,0:T(8,128)(2,1)S(1)}, u32[]{:S(2)}, u32[]{:S(2)}) %collective-permute-start) | collective-permute-done | bytes 294944 | tf_op jit(solution)/shard_map/ppermute | solution.py:36
  10.6 3.2 %shard_map.77 = (bf16[4,256,256]{2,1,0:T(8,128)(2,1)S(1)}, bf16[4,2,256,256]{3,2,1,0:T(8,128)(2,1)S(1)}, bf16[2,256,1024]{2,1,0:T(8,128)(2,1)S(1)}, f32[128,1152...) custom-call(bf16[576,256]{1,0:T(8,128)(2,1)S(1)} %collective-permute, ...), custom_call_target="tpu_custom_call" | custom-call | flops 1700000000 | bytes 4194304 | tf_op jit(solution)/shard_map/pallas_call | solution.py:203
  13.9 1.9 %collective-permute-start.1 = (bf16[128,1152]{1,0:T(8,128)(2,1)S(1)}, bf16[128,1152]{1,0:T(8,128)(2,1)S(1)}, u32[]{:S(2)}, u32[]{:S(2)}) collective-permute-start(bf16[128,1152]{1,0:T(8,128)(2,1)S(1)} %get-tuple-element.29), channel_id=1, source_target_pairs={{0,1},{1,0},{2,3},{3,2},{4,5},{5,4},{6,7},{7,6},{8,9},{9,8},{10,11... | collective-permute-start | bytes 884744 | tf_op jit(solution)/shard_map/ppermute | solution.py:263
  15.8 1.5 %collective-permute-done.1.got_ref = bf16[128,1152]{1,0:T(8,128)(2,1)S(1)} collective-permute-done((bf16[128,1152]{1,0:T(8,128)(2,1)S(1)}, bf16[128,1152]{1,0:T(8,128)(2,1)S(1)}, u32[]{:S(2)}, u32[]{:S(2)}) %collective-permute-start.1) | collective-permute-done | bytes 294944 | tf_op jit(solution)/shard_map/ppermute | solution.py:263
  18.1 13.7 %all-to-all-start = ((bf16[16,8,1152]{2,1,0:T(8,128)(2,1)}), bf16[16,8,1152]{2,1,0:T(8,128)(2,1)}, u32[]{:S(2)}, u32[]{:S(2)}) async-start(bf16[16,8,1152]{2,1,0:T(8,128)(2,1)} %bitcast.2), calls=%async_computation | async-start | bytes 589824 | tf_op jit(solution)/shard_map/all_to_all | solution.py:267
  31.8 7.9 %collective-permute-start.3 = (bf16[256,512]{1,0:T(8,128)(2,1)}, bf16[256,512]{1,0:T(8,128)(2,1)S(1)}, u32[]{:S(2)}, u32[]{:S(2)}) collective-permute-start(bf16[256,512]{1,0:T(8,128)(2,1)} %copy-done.9), channel_id=1, source_target_pairs={{0,128},{32,160},{64,192},{96,224},{128,0},{160,32},{192,64},{224,... | collective-permute-start | bytes 786440 | tf_op jit(solution)/shard_map/ppermute | solution.py:252
  39.7 1.9 %collective-permute-start.4 = (bf16[256,512]{1,0:T(8,128)(2,1)S(1)}, bf16[256,512]{1,0:T(8,128)(2,1)S(1)}, u32[]{:S(2)}, u32[]{:S(2)}) collective-permute-start(bf16[256,512]{1,0:T(8,128)(2,1)S(1)} %get-tuple-element.33), channel_id=1, source_target_pairs={{0,32},{32,0},{64,96},{96,64},{128,160},{160,128},{192,224},{224,1... | collective-permute-start | bytes 786440 | tf_op jit(solution)/shard_map/ppermute | solution.py:252
  41.7 4.3 %collective-permute-done.3.got_a_ref = bf16[256,512]{1,0:T(8,128)(2,1)S(1)} collective-permute-done((bf16[256,512]{1,0:T(8,128)(2,1)}, bf16[256,512]{1,0:T(8,128)(2,1)S(1)}, u32[]{:S(2)}, u32[]{:S(2)}) %collective-permute-start.3) | collective-permute-done | bytes 262176 | tf_op jit(solution)/shard_map/ppermute | solution.py:252
  46.0 3.2 %collective-permute-done.4.got_b_ref = bf16[256,512]{1,0:T(8,128)(2,1)S(1)} collective-permute-done((bf16[256,512]{1,0:T(8,128)(2,1)S(1)}, bf16[256,512]{1,0:T(8,128)(2,1)S(1)}, u32[]{:S(2)}, u32[]{:S(2)}) %collective-permute-start.4) | collective-permute-done | bytes 262176 | tf_op jit(solution)/shard_map/ppermute | solution.py:252
  49.1 1.0 %copy-done.3 = bf16[2,2,256,256]{3,2,1,0:T(8,128)(2,1)S(1)} copy-done((bf16[2,2,256,256]{3,2,1,0:T(8,128)(2,1)S(1)}, bf16[2,2,256,256]{3,2,1,0:T(8,128)(2,1)}, u32[]{:S(2)}) %copy-start.3) | copy-done | bytes 524312
  50.8 2.2 %collective-permute-start.5 = (bf16[128,512]{1,0:T(8,128)(2,1)S(1)}, bf16[128,512]{1,0:T(8,128)(2,1)S(1)}, u32[]{:S(2)}, u32[]{:S(2)}) collective-permute-start(bf16[128,512]{1,0:T(8,128)(2,1)S(1)} %get-tuple-element.35), channel_id=1, source_target_pairs={{0,32},{32,0},{64,96},{96,64},{128,160},{160,128},{192,224},{224,1... | collective-permute-start | bytes 393224 | tf_op jit(solution)/shard_map/ppermute | solution.py:252
  53.0 4.9 %collective-permute-start.6 = (bf16[128,512]{1,0:T(8,128)(2,1)S(1)}, bf16[128,512]{1,0:T(8,128)(2,1)S(1)}, u32[]{:S(2)}, u32[]{:S(2)}) collective-permute-start(bf16[128,512]{1,0:T(8,128)(2,1)S(1)} %get-tuple-element.36), channel_id=1, source_target_pairs={{0,128},{32,160},{64,192},{96,224},{128,0},{160,32},{192,64},{224,... | collective-permute-start | bytes 393224 | tf_op jit(solution)/shard_map/ppermute | solution.py:252
  57.9 1.3 %shard_map.78 = bf16[256,768]{1,0:T(8,128)(2,1)} custom-call(bf16[4,256,256]{2,1,0:T(8,128)(2,1)S(1)} %get-tuple-element.25.kep_ref, bf16[4,256,256]{2,1,0:T(8,128)(2,1)S(1)} %get-tuple-element.26.keo_ref, bf16[4,2,256,256]{3,2,1,0:T(8,128)(2,1)S(1)} %get-tuple-element.27.ds_ref), custom_call_target="tpu_custom_call" | custom-call | flops 270000000 | bytes 4194304 | tf_op jit(solution)/shard_map/pallas_call | solution.py:203
  59.2 1.7 %collective-permute-done.6.got_b_ref = bf16[128,512]{1,0:T(8,128)(2,1)S(1)} collective-permute-done((bf16[128,512]{1,0:T(8,128)(2,1)S(1)}, bf16[128,512]{1,0:T(8,128)(2,1)S(1)}, u32[]{:S(2)}, u32[]{:S(2)}) %collective-permute-start.6) | collective-permute-done | bytes 131104 | tf_op jit(solution)/shard_map/ppermute | solution.py:252
  61.6 14.9 %all-to-all-start.1 = ((bf16[8,16,1024]{2,1,0:T(8,128)(2,1)}), bf16[8,16,1024]{2,1,0:T(8,128)(2,1)S(1)}, u32[]{:S(2)}, u32[]{:S(2)}) async-start(bf16[8,16,1024]{2,1,0:T(8,128)(2,1)} %bitcast.3), calls=%async_computation.1 | async-start | bytes 524288 | tf_op jit(solution)/shard_map/all_to_all | solution.py:278
  76.5 1.0 %convert_reduce_fusion = f32[8,1152]{1,0:T(8,128)S(1)} fusion(bf16[16,8,1152]{2,1,0:T(8,128)(2,1)} %all-to-all-done), kind=kLoop, calls=%fused_computation | loop fusion | flops 285696 | bytes 331776 | tf_op jit(solution)/shard_map/reduce_sum | solution.py:279
  77.6 1.3 %collective-permute-start.2 = (f32[8,576]{1,0:T(8,128)S(1)}, f32[8,576]{1,0:T(8,128)S(1)}, u32[]{:S(2)}, u32[]{:S(2)}) collective-permute-start(f32[8,576]{1,0:T(8,128)S(1)} %pad_maximum_fusion), channel_id=1, source_target_pairs={{32,0},{64,32},{96,64},{128,96},{160,128},{192,160},{224,192},{256... | collective-permute-start | bytes 55304 | tf_op jit(solution)/shard_map/ppermute | solution.py:36
  78.9 10.0 %all-to-all-done.1 = bf16[8,16,1024]{2,1,0:T(8,128)(2,1)S(1)} async-done(((bf16[8,16,1024]{2,1,0:T(8,128)(2,1)}), bf16[8,16,1024]{2,1,0:T(8,128)(2,1)S(1)}, u32[]{:S(2)}, u32[]{:S(2)}) %all-to-all-start.1) | async-done | bytes 262176 | tf_op jit(solution)/shard_map/all_to_all | solution.py:278
  (26 shorter events, 3.5 us)
Async XLA Ops:
  0.6 3.4 %copy-start.8 = (s32[96]{0:T(128)S(1)}, s32[96]{0:T(128)}, u32[]{:S(2)}) copy-start(s32[96]{0:T(128)} %param.9) | copy-start | bytes 1156
  0.6 10.0 %collective-permute-start = (bf16[576,256]{1,0:T(8,128)(2,1)}, bf16[576,256]{1,0:T(8,128)(2,1)S(1)}, u32[]{:S(2)}, u32[]{:S(2)}) collective-permute-start(bf16[576,256]{1,0:T(8,128)(2,1)} %bitcast.4), channel_id=1, source_target_pairs={{0,32},{32,64},{64,96},{96,128},{128,160},{160,192},{192,224},{224... | collective-permute-start | bytes 884744 | tf_op jit(solution)/shard_map/ppermute | solution.py:36
  4.1 1.2 %copy-start = (bf16[512,1024]{1,0:T(8,128)(2,1)S(1)}, bf16[512,1024]{1,0:T(8,128)(2,1)}, u32[]{:S(2)}) copy-start(bf16[512,1024]{1,0:T(8,128)(2,1)} %w_ref.3) | copy-start | bytes 3145732
  5.3 1.0 %copy-start.4 = (bf16[256,768]{1,0:T(8,128)(2,1)S(1)}, bf16[256,768]{1,0:T(8,128)(2,1)}, u32[]{:S(2)}) copy-start(bf16[256,768]{1,0:T(8,128)(2,1)} %q_ref.1) | copy-start | bytes 1179652
  6.3 1.0 %copy-start.5 = (bf16[256,576]{0,1:T(8,128)(2,1)S(1)}, bf16[256,576]{0,1:T(8,128)(2,1)}, u32[]{:S(2)}) copy-start(bf16[256,576]{0,1:T(8,128)(2,1)} %param.5) | copy-start | bytes 884740
  7.3 0.9 %copy-start.7 = (bf16[256,512]{1,0:T(8,128)(2,1)S(1)}, bf16[256,512]{1,0:T(8,128)(2,1)}, u32[]{:S(2)}) copy-start(bf16[256,512]{1,0:T(8,128)(2,1)} %do_ref.3) | copy-start | bytes 786436
  8.2 2.4 %copy-start.1 = (bf16[512,1024]{1,0:T(8,128)(2,1)S(1)}, bf16[512,1024]{1,0:T(8,128)(2,1)}, u32[]{:S(2)}) copy-start(bf16[512,1024]{1,0:T(8,128)(2,1)} %w_ref.3) | copy-start | bytes 3145732
  8.2 2.4 %copy-start.6 = (bf16[256,576]{0,1:T(8,128)(2,1)S(1)}, bf16[256,576]{0,1:T(8,128)(2,1)}, u32[]{:S(2)}) copy-start(bf16[256,576]{0,1:T(8,128)(2,1)} %param.5) | copy-start | bytes 884740
  13.8 4.3 %copy-start.2 = (bf16[2,2,256,256]{3,2,1,0:T(8,128)(2,1)}, bf16[2,2,256,256]{3,2,1,0:T(8,128)(2,1)S(1)}, u32[]{:S(2)}) copy-start(bf16[2,2,256,256]{3,2,1,0:T(8,128)(2,1)S(1)} %get-tuple-element.30.xm_ref) | copy-start | bytes 1572868
  13.8 4.3 %copy-start.9 = (bf16[256,512]{1,0:T(8,128)(2,1)}, bf16[256,512]{1,0:T(8,128)(2,1)S(1)}, u32[]{:S(2)}) copy-start(bf16[256,512]{1,0:T(8,128)(2,1)S(1)} %get-tuple-element.32) | copy-start | bytes 786436
  13.9 3.5 %collective-permute-start.1 = (bf16[128,1152]{1,0:T(8,128)(2,1)S(1)}, bf16[128,1152]{1,0:T(8,128)(2,1)S(1)}, u32[]{:S(2)}, u32[]{:S(2)}) collective-permute-start(bf16[128,1152]{1,0:T(8,128)(2,1)S(1)} %get-tuple-element.29), channel_id=1, source_target_pairs={{0,1},{1,0},{2,3},{3,2},{4,5},{5,4},{6,7},{7,6},{8,9},{9,8},{10,11... | collective-permute-start | bytes 884744 | tf_op jit(solution)/shard_map/ppermute | solution.py:263
  18.1 43.5 %all-to-all-start = ((bf16[16,8,1152]{2,1,0:T(8,128)(2,1)}), bf16[16,8,1152]{2,1,0:T(8,128)(2,1)}, u32[]{:S(2)}, u32[]{:S(2)}) async-start(bf16[16,8,1152]{2,1,0:T(8,128)(2,1)} %bitcast.2), calls=%async_computation | async-start | bytes 589824 | tf_op jit(solution)/shard_map/all_to_all | solution.py:267
  31.8 14.2 %collective-permute-start.3 = (bf16[256,512]{1,0:T(8,128)(2,1)}, bf16[256,512]{1,0:T(8,128)(2,1)S(1)}, u32[]{:S(2)}, u32[]{:S(2)}) collective-permute-start(bf16[256,512]{1,0:T(8,128)(2,1)} %copy-done.9), channel_id=1, source_target_pairs={{0,128},{32,160},{64,192},{96,224},{128,0},{160,32},{192,64},{224,... | collective-permute-start | bytes 786440 | tf_op jit(solution)/shard_map/ppermute | solution.py:252
  39.7 9.4 %collective-permute-start.4 = (bf16[256,512]{1,0:T(8,128)(2,1)S(1)}, bf16[256,512]{1,0:T(8,128)(2,1)S(1)}, u32[]{:S(2)}, u32[]{:S(2)}) collective-permute-start(bf16[256,512]{1,0:T(8,128)(2,1)S(1)} %get-tuple-element.33), channel_id=1, source_target_pairs={{0,32},{32,0},{64,96},{96,64},{128,160},{160,128},{192,224},{224,1... | collective-permute-start | bytes 786440 | tf_op jit(solution)/shard_map/ppermute | solution.py:252
  49.1 1.0 %copy-start.3 = (bf16[2,2,256,256]{3,2,1,0:T(8,128)(2,1)S(1)}, bf16[2,2,256,256]{3,2,1,0:T(8,128)(2,1)}, u32[]{:S(2)}) copy-start(bf16[2,2,256,256]{3,2,1,0:T(8,128)(2,1)} %copy-done.2) | copy-start | bytes 1572868
  50.8 8.4 %collective-permute-start.5 = (bf16[128,512]{1,0:T(8,128)(2,1)S(1)}, bf16[128,512]{1,0:T(8,128)(2,1)S(1)}, u32[]{:S(2)}, u32[]{:S(2)}) collective-permute-start(bf16[128,512]{1,0:T(8,128)(2,1)S(1)} %get-tuple-element.35), channel_id=1, source_target_pairs={{0,32},{32,0},{64,96},{96,64},{128,160},{160,128},{192,224},{224,1... | collective-permute-start | bytes 393224 | tf_op jit(solution)/shard_map/ppermute | solution.py:252
  53.0 7.9 %collective-permute-start.6 = (bf16[128,512]{1,0:T(8,128)(2,1)S(1)}, bf16[128,512]{1,0:T(8,128)(2,1)S(1)}, u32[]{:S(2)}, u32[]{:S(2)}) collective-permute-start(bf16[128,512]{1,0:T(8,128)(2,1)S(1)} %get-tuple-element.36), channel_id=1, source_target_pairs={{0,128},{32,160},{64,192},{96,224},{128,0},{160,32},{192,64},{224,... | collective-permute-start | bytes 393224 | tf_op jit(solution)/shard_map/ppermute | solution.py:252
  61.6 27.3 %all-to-all-start.1 = ((bf16[8,16,1024]{2,1,0:T(8,128)(2,1)}), bf16[8,16,1024]{2,1,0:T(8,128)(2,1)S(1)}, u32[]{:S(2)}, u32[]{:S(2)}) async-start(bf16[8,16,1024]{2,1,0:T(8,128)(2,1)} %bitcast.3), calls=%async_computation.1 | async-start | bytes 524288 | tf_op jit(solution)/shard_map/all_to_all | solution.py:278
  77.6 11.9 %collective-permute-start.2 = (f32[8,576]{1,0:T(8,128)S(1)}, f32[8,576]{1,0:T(8,128)S(1)}, u32[]{:S(2)}, u32[]{:S(2)}) collective-permute-start(f32[8,576]{1,0:T(8,128)S(1)} %pad_maximum_fusion), channel_id=1, source_target_pairs={{32,0},{64,32},{96,64},{128,96},{160,128},{192,160},{224,192},{256... | collective-permute-start | bytes 55304 | tf_op jit(solution)/shard_map/ppermute | solution.py:36

commit v5 on v4

--- a/solution.py
+++ b/solution.py
@@ -100,8 +100,8 @@
 
 def window_kernel(
     xt_ref, start_ref, own_ref, qe_ref, do_ref, w_ref, e_ref, dp_ref, lg_ref,
-    ke_ref, ds_ref, dkv_ref, lat_mine_ref, lat_ref, theirs_a_ref, theirs_b_ref, xm_ref,
-    total_ref,
+    ke_ref, ds_ref, lat_mine_ref, lat_ref, theirs_a_ref, theirs_b_ref,
+    mine_a_ref, mine_b_ref, total_ref, dkv_ref,
 ):
     values = keys_and_values(xt_ref, w_ref, ke_ref)
     seen = iota((TOK, TOK), 0) - TOK >= start_ref[...]
@@ -133,7 +133,7 @@
     for out_ref, parity in ((lat_mine_ref, core), (lat_ref, 1 - core)):
         for i in range(8):
             pair = [
-                total_ref[pl.ds(pl.multiple_of((4 * i + 2 * j + parity) * 8, 8), 8), :]
+                total_ref[pl.ds(pl.multiple_of((16 * j + 2 * i + parity) * 8, 8), 8), :]
                 for j in range(2)
             ]
             out_ref[16 * i : 16 * i + 16, :] = jnp.concatenate(pair, axis=0).astype(out_ref.dtype)
@@ -145,9 +145,8 @@
     theirs_b_ref[...] = sum(
         dot(rows_of(sources[u], x0=1 - x0), dkv_ref[u, :, cut:]) for u in range(2)
     ).astype(BF16)
-    for u in range(2):
-        xm_ref[0, u] = rows_of(sources[u], z0=z0)
-        xm_ref[1, u] = rows_of(sources[u], x0=x0)
+    mine_a_ref[...] = sum(dot(rows_of(sources[u], z0=z0), dkv_ref[u, :, :cut]) for u in range(2))
+    mine_b_ref[...] = sum(dot(rows_of(sources[u], x0=x0), dkv_ref[u, :, cut:]) for u in range(2))
 
 
 def core_sum_kernel(mine_ref, got_ref, out_ref):
@@ -167,15 +166,11 @@
 
 
 def first_sum_kernel(
-    xm_ref, dkv_ref, got_a_ref, got_b_ref, kept_ref, send_a_ref, send_b_ref, a_ref, b_ref
+    mine_a_ref, mine_b_ref, got_a_ref, got_b_ref, kept_ref, send_a_ref, send_b_ref, a_ref, b_ref
 ):
     cut = HEADS * PAIR // 2
-    a_ref[...] = got_a_ref[...].astype(F32) + sum(
-        dot(xm_ref[0, u], dkv_ref[u, :, :cut]) for u in range(2)
-    )
-    b_ref[...] = got_b_ref[...].astype(F32) + sum(
-        dot(xm_ref[1, u], dkv_ref[u, :, cut:]) for u in range(2)
-    )
+    a_ref[...] = mine_a_ref[...] + got_a_ref[...].astype(F32)
+    b_ref[...] = mine_b_ref[...] + got_b_ref[...].astype(F32)
     z0, x0 = lax.axis_index("z0"), lax.axis_index("x0")
     for i in range(8):
         rows = slice(16 * i, 16 * i + 16)
@@ -197,6 +192,25 @@
     cut = HEADS * PAIR // 2
     out_ref[:, :cut] = (kept_ref[:, :cut] + got_a_ref[...].astype(F32)).astype(BF16)
     out_ref[:, cut:] = (kept_ref[:, cut:] + got_b_ref[...].astype(F32)).astype(BF16)
+
+
+def head_sum_kernel(parts_ref, mine_ref, send_ref, sum_ref):
+    total = parts_ref[0].astype(F32)
+    for i in range(1, 8):
+        total = total + parts_ref[i].astype(F32)
+    sum_ref[...] = total
+    xh = lax.axis_index("xh")
+    mine_ref[...] = sum_ref[pl.ds(pl.multiple_of(xh * 8, 8), 8), :]
+    send_ref[...] = sum_ref[pl.ds(pl.multiple_of((1 - xh) * 8, 8), 8), :].astype(BF16)
+
+
+def part_kernel(mine_ref, got_ref, keep_ref, give_ref):
+    total = mine_ref[...] + got_ref[...].astype(F32)
+    keep_ref[:, :LATENT] = total[:, :LATENT]
+    give_ref[:, :LATENT] = total[:, LATENT : 2 * LATENT]
+    rope = total[:, 2 * LATENT :]
+    keep_ref[:, LATENT:] = rope[:, :ROPE]
+    give_ref[:, LATENT:] = pltpu.roll(rope, ROPE, 1)[:, :ROPE]
 
 
 def call(kernel, outs, flops, *args, scratch=()):
@@ -226,22 +240,25 @@
         ],
         470_000_000, lengths.reshape(1, -1), own, query, out_grad, up_weight,
     )
-    kep, ds, dkv, lat_mine, lat_theirs, theirs_a, theirs_b, xm = call(
+    kep, ds, lat_mine, lat_theirs, theirs_a, theirs_b, *mine = call(
         window_kernel,
         [
             (square, BF16),
             ((HEADS, 2, TOK, TOK), BF16),
-            ((2, TOK, columns), BF16),
             ((TOK // 2, 2 * LATENT + 2 * ROPE), F32),
             ((TOK // 2, 2 * LATENT + 2 * ROPE), BF16),
             ((TOK, columns // 2), BF16),
             ((TOK, columns // 2), BF16),
-            ((2, 2, TOK, TOK), BF16),
+            ((TOK, columns // 2), F32),
+            ((TOK, columns // 2), F32),
         ],
         1_700_000_000, prev, start, own, qe, out_grad, up_weight, e, dp, lg,
-        scratch=[pltpu.VMEM((TOK, 2 * LATENT + 2 * ROPE), F32)],
-    )
-    return lat_mine, lat_theirs, theirs_a, theirs_b, (xm, dkv), (kep, keo, ds)
+        scratch=[
+            pltpu.VMEM((TOK, 2 * LATENT + 2 * ROPE), F32),
+            pltpu.VMEM((2, TOK, columns), BF16),
+        ],
+    )
+    return lat_mine, lat_theirs, theirs_a, theirs_b, mine, (kep, keo, ds)
 
 
 def query_grad(saved):
@@ -257,18 +274,18 @@
     prev = ctx_shift(own, 1)
 
     columns = HEADS * PAIR
-    lat_mine, lat_theirs, theirs_a, theirs_b, factors, saved = attend(
+    lat_mine, lat_theirs, theirs_a, theirs_b, mine, saved = attend(
         own, prev, query, out_grad, up_weight, lengths
     )
     got_core = lax.ppermute(lat_theirs, "core", [(0, 1), (1, 0)])
     got_a = flip(theirs_a, 4)
     got_b = flip(theirs_b, 1)
     (latent,) = call(core_sum_kernel, [(lat_mine.shape, BF16)], 1_000_000, lat_mine, got_core)
-    parts = lax.all_to_all(latent.reshape(16, 8, -1), ("xh", "y"), 0, 0)
+    parts = lax.all_to_all(latent.reshape(8, 16, -1), "y", 0, 0)
     kept, send_a, send_b = call(
         first_sum_kernel,
         [((128, columns), F32), ((128, columns // 2), BF16), ((128, columns // 2), BF16)],
-        270_000_000, *factors, got_a, got_b,
+        1_000_000, *mine, got_a, got_b,
         scratch=[pltpu.VMEM((TOK, columns // 2), F32)] * 2,
     )
     next_a = flip(send_a, 1)
@@ -276,12 +293,18 @@
     dq = query_grad(saved)
     (eighth,) = call(second_sum_kernel, [((128, columns), BF16)], 1_000_000, kept, next_a, next_b)
     eighths = lax.all_to_all(eighth.reshape(8, 16, -1), ("z2", "z1", "x1"), 0, 0)
-    summed = jnp.sum(parts.astype(F32), axis=0)
+    rows = (8, 2 * LATENT + 2 * ROPE)
+    kept_rows, sent_rows = call(
+        head_sum_kernel,
+        [(rows, F32), (rows, BF16)],
+        1_000_000, parts,
+        scratch=[pltpu.VMEM((16, rows[1]), F32)],
+    )
+    pairs = [(0, 1), (1, 0)]
+    got_rows = lax.ppermute(sent_rows, "xh", pairs)
+    keep, give = call(part_kernel, [((8, LATENT + ROPE), F32)] * 2, 1_000_000, kept_rows, got_rows)
+    grad_compressed = keep + ctx_shift(give, -1)
     grad_weight = jnp.sum(eighths.astype(F32), axis=0)
-    rope = 2 * LATENT + ROPE
-    keep = jnp.concatenate([summed[:, :LATENT], summed[:, 2 * LATENT : rope]], axis=1)
-    give = jnp.concatenate([summed[:, LATENT : 2 * LATENT], summed[:, rope:]], axis=1)
-    grad_compressed = keep + ctx_shift(give, -1)
     return dq, grad_compressed, grad_weight
 
 

time: 90.9 us -> 93 us (1.023)
  the two profiles are of different devices: /device:TPU:16 before, /device:TPU:30 now
where the time goes in v5:
time: 93 us; the launch traced here: 92.3 us
  starting transfers between devices  51.1 us (55%)
  waiting for transfers between devices  27.7 us (30%)
  Pallas kernels  7.34 us (8%)
  local copies, waits for them, and re-layouts  4.14 us (4%)
  other arithmetic  1.28 us (1%)
    all_to_all x1, starting transfers between devices, body(): lax.all_to_all(eighth.reshape(8, 16, -1), ('z2', 'z1', 'x1'), 0, 0)  17.5 us
    ppermute x4, waiting for transfers between devices, flip(): return lax.ppermute(x, CTX, [(i, i ^ mask) for i in range(32)])  12.3 us
    ppermute x4, starting transfers between devices, flip(): return lax.ppermute(x, CTX, [(i, i ^ mask) for i in range(32)])  11.5 us
    ppermute x2, starting transfers between devices, ctx_shift(): return lax.ppermute(x, CTX, pairs)  9.95 us
    all_to_all x1, starting transfers between devices, body(): parts = lax.all_to_all(latent.reshape(8, 16, -1), 'y', 0, 0)  7.89 us
    pallas_call x8, Pallas kernels, call(): pl.pallas_call(kernel, out_shape=[jax.ShapeDtypeStruct(s, d) for s, d in...  7.34 us
    ppermute x1, waiting for transfers between devices, body(): got_rows = lax.ppermute(sent_rows, 'xh', pairs)  7.25 us
    ppermute x2, waiting for transfers between devices, ctx_shift(): return lax.ppermute(x, CTX, pairs)  6.53 us
  transfers between devices with their start and end apart: 10, of which 8 were waited for; matrix products, arithmetic and copies ran while one was open for 1% of the time, Pallas kernels for 3%

profile of v5, /device:TPU:30, one launch (start us, length us, event | category | flops | bytes accessed | tf_op | source)
XLA Modules:
  0.0 92.3 jit_solution(4405383544487661952)
XLA Ops:
  0.6 7.8 %collective-permute-start = (bf16[576,256]{1,0:T(8,128)(2,1)}, bf16[576,256]{1,0:T(8,128)(2,1)S(1)}, u32[]{:S(2)}, u32[]{:S(2)}) collective-permute-start(bf16[576,256]{1,0:T(8,128)(2,1)} %bitcast.4), channel_id=1, source_target_pairs={{0,32},{32,64},{64,96},{96,128},{128,160},{160,192},{192,224},{224... | collective-permute-start | bytes 884744 | tf_op jit(solution)/shard_map/ppermute | solution.py:36
  8.5 1.2 %copy-done = bf16[512,1024]{1,0:T(8,128)(2,1)S(1)} copy-done((bf16[512,1024]{1,0:T(8,128)(2,1)S(1)}, bf16[512,1024]{1,0:T(8,128)(2,1)}, u32[]{:S(2)}) %copy-start) | copy-done | bytes 1048600
  9.7 1.0 %copy-done.2 = bf16[256,768]{1,0:T(8,128)(2,1)S(1)} copy-done((bf16[256,768]{1,0:T(8,128)(2,1)S(1)}, bf16[256,768]{1,0:T(8,128)(2,1)}, u32[]{:S(2)}) %copy-start.2) | copy-done | bytes 393240
  10.7 1.0 %copy-done.3 = bf16[256,576]{0,1:T(8,128)(2,1)S(1)} copy-done((bf16[256,576]{0,1:T(8,128)(2,1)S(1)}, bf16[256,576]{0,1:T(8,128)(2,1)}, u32[]{:S(2)}) %copy-start.3) | copy-done | bytes 294936
  11.6 0.9 %copy-done.5 = bf16[256,512]{1,0:T(8,128)(2,1)S(1)} copy-done((bf16[256,512]{1,0:T(8,128)(2,1)S(1)}, bf16[256,512]{1,0:T(8,128)(2,1)}, u32[]{:S(2)}) %copy-start.5) | copy-done | bytes 262168
  13.4 1.6 %collective-permute-done.xt_ref = bf16[576,256]{1,0:T(8,128)(2,1)S(1)} collective-permute-done((bf16[576,256]{1,0:T(8,128)(2,1)}, bf16[576,256]{1,0:T(8,128)(2,1)S(1)}, u32[]{:S(2)}, u32[]{:S(2)}) %collective-permute-start) | collective-permute-done | bytes 294944 | tf_op jit(solution)/shard_map/ppermute | solution.py:36
  15.0 3.4 %shard_map.77 = (bf16[4,256,256]{2,1,0:T(8,128)(2,1)S(1)}, bf16[4,2,256,256]{3,2,1,0:T(8,128)(2,1)S(1)}, f32[128,1152]{1,0:T(8,128)S(1)}, bf16[128,1152]{1,0:T(8...) custom-call(bf16[576,256]{1,0:T(8,128)(2,1)S(1)} %collective-permute, ...), custom_call_target="tpu_custom_call" | custom-call | flops 1700000000 | bytes 4194304 | tf_op jit(solution)/shard_map/pallas_call | solution.py:217
  18.5 1.9 %collective-permute-start.1 = (bf16[128,1152]{1,0:T(8,128)(2,1)S(1)}, bf16[128,1152]{1,0:T(8,128)(2,1)S(1)}, u32[]{:S(2)}, u32[]{:S(2)}) collective-permute-start(bf16[128,1152]{1,0:T(8,128)(2,1)S(1)} %get-tuple-element.33), channel_id=1, source_target_pairs={{0,1},{1,0},{2,3},{3,2},{4,5},{5,4},{6,7},{7,6},{8,9},{9,8},{10,11... | collective-permute-start | bytes 884744 | tf_op jit(solution)/shard_map/ppermute | solution.py:280
  20.4 1.5 %collective-permute-done.1.got_ref = bf16[128,1152]{1,0:T(8,128)(2,1)S(1)} collective-permute-done((bf16[128,1152]{1,0:T(8,128)(2,1)S(1)}, bf16[128,1152]{1,0:T(8,128)(2,1)S(1)}, u32[]{:S(2)}, u32[]{:S(2)}) %collective-permute-start.1) | collective-permute-done | bytes 294944 | tf_op jit(solution)/shard_map/ppermute | solution.py:280
  22.7 7.9 %all-to-all-start = ((bf16[8,16,1152]{2,1,0:T(8,128)(2,1)}), bf16[8,16,1152]{2,1,0:T(8,128)(2,1)S(1)}, u32[]{:S(2)}, u32[]{:S(2)}) async-start(bf16[8,16,1152]{2,1,0:T(8,128)(2,1)} %bitcast.2), calls=%async_computation | async-start | bytes 589824 | tf_op jit(solution)/shard_map/all_to_all | solution.py:284
  30.6 5.2 %collective-permute-start.4 = (bf16[256,512]{1,0:T(8,128)(2,1)}, bf16[256,512]{1,0:T(8,128)(2,1)S(1)}, u32[]{:S(2)}, u32[]{:S(2)}) collective-permute-start(bf16[256,512]{1,0:T(8,128)(2,1)} %copy-done.8), channel_id=1, source_target_pairs={{0,128},{32,160},{64,192},{96,224},{128,0},{160,32},{192,64},{224,... | collective-permute-start | bytes 786440 | tf_op jit(solution)/shard_map/ppermute | solution.py:269
  35.8 1.9 %collective-permute-start.5 = (bf16[256,512]{1,0:T(8,128)(2,1)}, bf16[256,512]{1,0:T(8,128)(2,1)S(1)}, u32[]{:S(2)}, u32[]{:S(2)}) collective-permute-start(bf16[256,512]{1,0:T(8,128)(2,1)} %copy-done.7), channel_id=1, source_target_pairs={{0,32},{32,0},{64,96},{96,64},{128,160},{160,128},{192,224},{224,1... | collective-permute-start | bytes 786440 | tf_op jit(solution)/shard_map/ppermute | solution.py:269
  37.7 4.3 %collective-permute-done.4.got_a_ref = bf16[256,512]{1,0:T(8,128)(2,1)S(1)} collective-permute-done((bf16[256,512]{1,0:T(8,128)(2,1)}, bf16[256,512]{1,0:T(8,128)(2,1)S(1)}, u32[]{:S(2)}, u32[]{:S(2)}) %collective-permute-start.4) | collective-permute-done | bytes 262176 | tf_op jit(solution)/shard_map/ppermute | solution.py:269
  42.0 3.4 %collective-permute-done.5.got_b_ref = bf16[256,512]{1,0:T(8,128)(2,1)S(1)} collective-permute-done((bf16[256,512]{1,0:T(8,128)(2,1)}, bf16[256,512]{1,0:T(8,128)(2,1)S(1)}, u32[]{:S(2)}, u32[]{:S(2)}) %collective-permute-start.5) | collective-permute-done | bytes 262176 | tf_op jit(solution)/shard_map/ppermute | solution.py:269
  45.6 2.2 %collective-permute-start.6 = (bf16[128,512]{1,0:T(8,128)(2,1)S(1)}, bf16[128,512]{1,0:T(8,128)(2,1)S(1)}, u32[]{:S(2)}, u32[]{:S(2)}) collective-permute-start(bf16[128,512]{1,0:T(8,128)(2,1)S(1)} %get-tuple-element.43), channel_id=1, source_target_pairs={{0,32},{32,0},{64,96},{96,64},{128,160},{160,128},{192,224},{224,1... | collective-permute-start | bytes 393224 | tf_op jit(solution)/shard_map/ppermute | solution.py:269
  47.8 2.2 %collective-permute-start.7 = (bf16[128,512]{1,0:T(8,128)(2,1)S(1)}, bf16[128,512]{1,0:T(8,128)(2,1)S(1)}, u32[]{:S(2)}, u32[]{:S(2)}) collective-permute-start(bf16[128,512]{1,0:T(8,128)(2,1)S(1)} %get-tuple-element.44), channel_id=1, source_target_pairs={{0,128},{32,160},{64,192},{96,224},{128,0},{160,32},{192,64},{224,... | collective-permute-start | bytes 393224 | tf_op jit(solution)/shard_map/ppermute | solution.py:269
  50.0 2.4 %collective-permute-done.6.got_a_ref = bf16[128,512]{1,0:T(8,128)(2,1)S(1)} collective-permute-done((bf16[128,512]{1,0:T(8,128)(2,1)S(1)}, bf16[128,512]{1,0:T(8,128)(2,1)S(1)}, u32[]{:S(2)}, u32[]{:S(2)}) %collective-permute-start.6) | collective-permute-done | bytes 131104 | tf_op jit(solution)/shard_map/ppermute | solution.py:269
  52.4 2.2 %collective-permute-done.7.got_b_ref = bf16[128,512]{1,0:T(8,128)(2,1)S(1)} collective-permute-done((bf16[128,512]{1,0:T(8,128)(2,1)S(1)}, bf16[128,512]{1,0:T(8,128)(2,1)S(1)}, u32[]{:S(2)}, u32[]{:S(2)}) %collective-permute-start.7) | collective-permute-done | bytes 131104 | tf_op jit(solution)/shard_map/ppermute | solution.py:269
  55.4 17.5 %all-to-all-start.1 = ((bf16[8,16,1024]{2,1,0:T(8,128)(2,1)}), bf16[8,16,1024]{2,1,0:T(8,128)(2,1)S(1)}, u32[]{:S(2)}, u32[]{:S(2)}) async-start(bf16[8,16,1024]{2,1,0:T(8,128)(2,1)} %bitcast.3), calls=%async_computation.1 | async-start | bytes 524288 | tf_op jit(solution)/shard_map/all_to_all | solution.py:295
  72.9 2.3 %collective-permute-start.2 = (bf16[8,1152]{1,0:T(8,128)(2,1)S(1)}, bf16[8,1152]{1,0:T(8,128)(2,1)S(1)}, u32[]{:S(2)}, u32[]{:S(2)}) collective-permute-start(bf16[8,1152]{1,0:T(8,128)(2,1)S(1)} %get-tuple-element.35), channel_id=1, source_target_pairs={{0,16},{16,0},{1,17},{17,1},{2,18},{18,2},{3,19},{19,3},{4,20},{20... | collective-permute-start | bytes 55304 | tf_op jit(solution)/shard_map/ppermute | solution.py:304
  75.3 7.2 %collective-permute-done.2.got_ref = bf16[8,1152]{1,0:T(8,128)(2,1)S(1)} collective-permute-done((bf16[8,1152]{1,0:T(8,128)(2,1)S(1)}, bf16[8,1152]{1,0:T(8,128)(2,1)S(1)}, u32[]{:S(2)}, u32[]{:S(2)}) %collective-permute-start.2) | collective-permute-done | bytes 18464 | tf_op jit(solution)/shard_map/ppermute | solution.py:304
  82.6 2.1 %collective-permute-start.3 = (f32[8,576]{1,0:T(8,128)S(1)}, f32[8,576]{1,0:T(8,128)S(1)}, u32[]{:S(2)}, u32[]{:S(2)}) collective-permute-start(f32[8,576]{1,0:T(8,128)S(1)} %get-tuple-element.37), channel_id=1, source_target_pairs={{32,0},{64,32},{96,64},{128,96},{160,128},{192,160},{224,192},{256... | collective-permute-start | bytes 55304 | tf_op jit(solution)/shard_map/ppermute | solution.py:36
  84.8 1.3 %shard_map.78 = bf16[256,768]{1,0:T(8,128)(2,1)} custom-call(bf16[4,256,256]{2,1,0:T(8,128)(2,1)S(1)} %get-tuple-element.29.kep_ref, bf16[4,256,256]{2,1,0:T(8,128)(2,1)S(1)} %get-tuple-element.30.keo_ref, bf16[4,2,256,256]{3,2,1,0:T(8,128)(2,1)S(1)} %get-tuple-element.31.ds_ref), custom_call_target="tpu_custom_call" | custom-call | flops 270000000 | bytes 4194304 | tf_op jit(solution)/shard_map/pallas_call | solution.py:217
  86.0 4.9 %collective-permute-done.3 = f32[8,576]{1,0:T(8,128)S(1)} collective-permute-done((f32[8,576]{1,0:T(8,128)S(1)}, f32[8,576]{1,0:T(8,128)S(1)}, u32[]{:S(2)}, u32[]{:S(2)}) %collective-permute-start.3) | collective-permute-done | bytes 18464 | tf_op jit(solution)/shard_map/ppermute | solution.py:36
  (24 shorter events, 4.0 us)
Async XLA Ops:
  0.6 7.8 %copy-start.6 = (s32[96]{0:T(128)S(1)}, s32[96]{0:T(128)}, u32[]{:S(2)}) copy-start(s32[96]{0:T(128)} %param.9) | copy-start | bytes 1156
  0.6 14.4 %collective-permute-start = (bf16[576,256]{1,0:T(8,128)(2,1)}, bf16[576,256]{1,0:T(8,128)(2,1)S(1)}, u32[]{:S(2)}, u32[]{:S(2)}) collective-permute-start(bf16[576,256]{1,0:T(8,128)(2,1)} %bitcast.4), channel_id=1, source_target_pairs={{0,32},{32,64},{64,96},{96,128},{128,160},{160,192},{192,224},{224... | collective-permute-start | bytes 884744 | tf_op jit(solution)/shard_map/ppermute | solution.py:36
  8.5 1.2 %copy-start = (bf16[512,1024]{1,0:T(8,128)(2,1)S(1)}, bf16[512,1024]{1,0:T(8,128)(2,1)}, u32[]{:S(2)}) copy-start(bf16[512,1024]{1,0:T(8,128)(2,1)} %w_ref.3) | copy-start | bytes 3145732
  9.7 1.0 %copy-start.2 = (bf16[256,768]{1,0:T(8,128)(2,1)S(1)}, bf16[256,768]{1,0:T(8,128)(2,1)}, u32[]{:S(2)}) copy-start(bf16[256,768]{1,0:T(8,128)(2,1)} %q_ref.1) | copy-start | bytes 1179652
  10.7 1.0 %copy-start.3 = (bf16[256,576]{0,1:T(8,128)(2,1)S(1)}, bf16[256,576]{0,1:T(8,128)(2,1)}, u32[]{:S(2)}) copy-start(bf16[256,576]{0,1:T(8,128)(2,1)} %param.5) | copy-start | bytes 884740
  11.6 0.9 %copy-start.5 = (bf16[256,512]{1,0:T(8,128)(2,1)S(1)}, bf16[256,512]{1,0:T(8,128)(2,1)}, u32[]{:S(2)}) copy-start(bf16[256,512]{1,0:T(8,128)(2,1)} %do_ref.3) | copy-start | bytes 786436
  12.6 2.4 %copy-start.1 = (bf16[512,1024]{1,0:T(8,128)(2,1)S(1)}, bf16[512,1024]{1,0:T(8,128)(2,1)}, u32[]{:S(2)}) copy-start(bf16[512,1024]{1,0:T(8,128)(2,1)} %w_ref.3) | copy-start | bytes 3145732
  12.6 2.4 %copy-start.4 = (bf16[256,576]{0,1:T(8,128)(2,1)S(1)}, bf16[256,576]{0,1:T(8,128)(2,1)}, u32[]{:S(2)}) copy-start(bf16[256,576]{0,1:T(8,128)(2,1)} %param.5) | copy-start | bytes 884740
  18.4 4.3 %copy-start.7 = (bf16[256,512]{1,0:T(8,128)(2,1)}, bf16[256,512]{1,0:T(8,128)(2,1)S(1)}, u32[]{:S(2)}) copy-start(bf16[256,512]{1,0:T(8,128)(2,1)S(1)} %get-tuple-element.41) | copy-start | bytes 786436
  18.5 4.3 %copy-start.8 = (bf16[256,512]{1,0:T(8,128)(2,1)}, bf16[256,512]{1,0:T(8,128)(2,1)S(1)}, u32[]{:S(2)}) copy-start(bf16[256,512]{1,0:T(8,128)(2,1)S(1)} %get-tuple-element.40) | copy-start | bytes 786436
  18.5 3.5 %collective-permute-start.1 = (bf16[128,1152]{1,0:T(8,128)(2,1)S(1)}, bf16[128,1152]{1,0:T(8,128)(2,1)S(1)}, u32[]{:S(2)}, u32[]{:S(2)}) collective-permute-start(bf16[128,1152]{1,0:T(8,128)(2,1)S(1)} %get-tuple-element.33), channel_id=1, source_target_pairs={{0,1},{1,0},{2,3},{3,2},{4,5},{5,4},{6,7},{7,6},{8,9},{9,8},{10,11... | collective-permute-start | bytes 884744 | tf_op jit(solution)/shard_map/ppermute | solution.py:280
  22.7 32.7 %all-to-all-start = ((bf16[8,16,1152]{2,1,0:T(8,128)(2,1)}), bf16[8,16,1152]{2,1,0:T(8,128)(2,1)S(1)}, u32[]{:S(2)}, u32[]{:S(2)}) async-start(bf16[8,16,1152]{2,1,0:T(8,128)(2,1)} %bitcast.2), calls=%async_computation | async-start | bytes 589824 | tf_op jit(solution)/shard_map/all_to_all | solution.py:284
  30.6 11.4 %collective-permute-start.4 = (bf16[256,512]{1,0:T(8,128)(2,1)}, bf16[256,512]{1,0:T(8,128)(2,1)S(1)}, u32[]{:S(2)}, u32[]{:S(2)}) collective-permute-start(bf16[256,512]{1,0:T(8,128)(2,1)} %copy-done.8), channel_id=1, source_target_pairs={{0,128},{32,160},{64,192},{96,224},{128,0},{160,32},{192,64},{224,... | collective-permute-start | bytes 786440 | tf_op jit(solution)/shard_map/ppermute | solution.py:269
  35.8 9.6 %collective-permute-start.5 = (bf16[256,512]{1,0:T(8,128)(2,1)}, bf16[256,512]{1,0:T(8,128)(2,1)S(1)}, u32[]{:S(2)}, u32[]{:S(2)}) collective-permute-start(bf16[256,512]{1,0:T(8,128)(2,1)} %copy-done.7), channel_id=1, source_target_pairs={{0,32},{32,0},{64,96},{96,64},{128,160},{160,128},{192,224},{224,1... | collective-permute-start | bytes 786440 | tf_op jit(solution)/shard_map/ppermute | solution.py:269
  45.6 6.9 %collective-permute-start.6 = (bf16[128,512]{1,0:T(8,128)(2,1)S(1)}, bf16[128,512]{1,0:T(8,128)(2,1)S(1)}, u32[]{:S(2)}, u32[]{:S(2)}) collective-permute-start(bf16[128,512]{1,0:T(8,128)(2,1)S(1)} %get-tuple-element.43), channel_id=1, source_target_pairs={{0,32},{32,0},{64,96},{96,64},{128,160},{160,128},{192,224},{224,1... | collective-permute-start | bytes 393224 | tf_op jit(solution)/shard_map/ppermute | solution.py:269
  47.8 6.9 %collective-permute-start.7 = (bf16[128,512]{1,0:T(8,128)(2,1)S(1)}, bf16[128,512]{1,0:T(8,128)(2,1)S(1)}, u32[]{:S(2)}, u32[]{:S(2)}) collective-permute-start(bf16[128,512]{1,0:T(8,128)(2,1)S(1)} %get-tuple-element.44), channel_id=1, source_target_pairs={{0,128},{32,160},{64,192},{96,224},{128,0},{160,32},{192,64},{224,... | collective-permute-start | bytes 393224 | tf_op jit(solution)/shard_map/ppermute | solution.py:269
  55.4 36.2 %all-to-all-start.1 = ((bf16[8,16,1024]{2,1,0:T(8,128)(2,1)}), bf16[8,16,1024]{2,1,0:T(8,128)(2,1)S(1)}, u32[]{:S(2)}, u32[]{:S(2)}) async-start(bf16[8,16,1024]{2,1,0:T(8,128)(2,1)} %bitcast.3), calls=%async_computation.1 | async-start | bytes 524288 | tf_op jit(solution)/shard_map/all_to_all | solution.py:295
  72.9 9.6 %collective-permute-start.2 = (bf16[8,1152]{1,0:T(8,128)(2,1)S(1)}, bf16[8,1152]{1,0:T(8,128)(2,1)S(1)}, u32[]{:S(2)}, u32[]{:S(2)}) collective-permute-start(bf16[8,1152]{1,0:T(8,128)(2,1)S(1)} %get-tuple-element.35), channel_id=1, source_target_pairs={{0,16},{16,0},{1,17},{17,1},{2,18},{18,2},{3,19},{19,3},{4,20},{20... | collective-permute-start | bytes 55304 | tf_op jit(solution)/shard_map/ppermute | solution.py:304
  82.6 8.4 %collective-permute-start.3 = (f32[8,576]{1,0:T(8,128)S(1)}, f32[8,576]{1,0:T(8,128)S(1)}, u32[]{:S(2)}, u32[]{:S(2)}) collective-permute-start(f32[8,576]{1,0:T(8,128)S(1)} %get-tuple-element.37), channel_id=1, source_target_pairs={{32,0},{64,32},{96,64},{128,96},{160,128},{192,160},{224,192},{256... | collective-permute-start | bytes 55304 | tf_op jit(solution)/shard_map/ppermute | solution.py:36

commit v6 on v5

--- a/solution.py
+++ b/solution.py
@@ -89,19 +89,14 @@
         lg_ref[h + 4 : h + 5, :] = jnp.sum(e * dp, axis=0, keepdims=True)
 
 
-def rows_of(xt_ref, z0=None, x0=None):
-    if x0 is None:
-        starts, size = [(2 * i + z0) * 64 for i in range(4)], 64
-    else:
-        starts, size = [(2 * i + x0) * 16 for i in range(16)], 16
-    rows = [xt_ref[pl.ds(pl.multiple_of(at, size), size), :] for at in starts]
+def rows_of(xt_ref, z0):
+    rows = [xt_ref[pl.ds(pl.multiple_of((2 * i + z0) * 64, 64), 64), :] for i in range(4)]
     return jnp.concatenate(rows, axis=0)
 
 
 def window_kernel(
     xt_ref, start_ref, own_ref, qe_ref, do_ref, w_ref, e_ref, dp_ref, lg_ref,
-    ke_ref, ds_ref, lat_mine_ref, lat_ref, theirs_a_ref, theirs_b_ref,
-    mine_a_ref, mine_b_ref, total_ref, dkv_ref,
+    ke_ref, ds_ref, lat_mine_ref, lat_ref, theirs_ref, mine_ref, total_ref, dkv_ref,
 ):
     values = keys_and_values(xt_ref, w_ref, ke_ref)
     seen = iota((TOK, TOK), 0) - TOK >= start_ref[...]
@@ -126,30 +121,23 @@
             dkv_ref[half, :, h * PAIR + NOPE : (h + 1) * PAIR] = dot(
                 probs.astype(BF16), do
             ).astype(BF16)
-    z0, x0, core = (lax.axis_index(name) for name in ("z0", "x0", "core"))
+    z0, core = lax.axis_index("z0"), lax.axis_index("core")
     total_ref[:, :LATENT] = dot(dkv_ref[1], w_ref[...], NT)
     total_ref[:, LATENT : 2 * LATENT] = dot(dkv_ref[0], w_ref[...], NT)
     total_ref[:, 2 * LATENT :] = rope_grads[1] + pltpu.roll(rope_grads[0], ROPE, 1)
     for out_ref, parity in ((lat_mine_ref, core), (lat_ref, 1 - core)):
         for i in range(8):
             pair = [
-                total_ref[pl.ds(pl.multiple_of((16 * j + 2 * i + parity) * 8, 8), 8), :]
+                total_ref[pl.ds(pl.multiple_of((4 * i + 2 * j + parity) * 8, 8), 8), :]
                 for j in range(2)
             ]
             out_ref[16 * i : 16 * i + 16, :] = jnp.concatenate(pair, axis=0).astype(out_ref.dtype)
-    cut = HEADS * PAIR // 2
     sources = (xt_ref, own_ref)
-    theirs_a_ref[...] = sum(
-        dot(rows_of(sources[u], z0=1 - z0), dkv_ref[u, :, :cut]) for u in range(2)
-    ).astype(BF16)
-    theirs_b_ref[...] = sum(
-        dot(rows_of(sources[u], x0=1 - x0), dkv_ref[u, :, cut:]) for u in range(2)
-    ).astype(BF16)
-    mine_a_ref[...] = sum(dot(rows_of(sources[u], z0=z0), dkv_ref[u, :, :cut]) for u in range(2))
-    mine_b_ref[...] = sum(dot(rows_of(sources[u], x0=x0), dkv_ref[u, :, cut:]) for u in range(2))
-
-
-def core_sum_kernel(mine_ref, got_ref, out_ref):
+    theirs_ref[...] = sum(dot(rows_of(sources[u], 1 - z0), dkv_ref[u]) for u in range(2)).astype(BF16)
+    mine_ref[...] = sum(dot(rows_of(sources[u], z0), dkv_ref[u]) for u in range(2))
+
+
+def pair_sum_kernel(mine_ref, got_ref, out_ref):
     out_ref[...] = (mine_ref[...] + got_ref[...].astype(F32)).astype(BF16)
 
 
@@ -165,47 +153,21 @@
         dq_ref[:, base + 256 : base + 384] = moved[:, 128:].astype(BF16)
 
 
-def first_sum_kernel(
-    mine_a_ref, mine_b_ref, got_a_ref, got_b_ref, kept_ref, send_a_ref, send_b_ref, a_ref, b_ref
-):
-    cut = HEADS * PAIR // 2
-    a_ref[...] = mine_a_ref[...] + got_a_ref[...].astype(F32)
-    b_ref[...] = mine_b_ref[...] + got_b_ref[...].astype(F32)
-    z0, x0 = lax.axis_index("z0"), lax.axis_index("x0")
+def first_sum_kernel(mine_ref, got_ref, kept_ref, send_ref, sum_ref):
+    sum_ref[...] = mine_ref[...] + got_ref[...].astype(F32)
+    x0 = lax.axis_index("x0")
     for i in range(8):
         rows = slice(16 * i, 16 * i + 16)
-
-        def of_a(x):
-            return a_ref[pl.ds(pl.multiple_of((2 * i + x) * 16, 16), 16), :]
-
-        def of_b(z):
-            at = (i // 2) * 64 + z * 32 + (i % 2) * 16
-            return b_ref[pl.ds(pl.multiple_of(at, 16), 16), :]
-
-        kept_ref[rows, :cut] = of_a(x0)
-        kept_ref[rows, cut:] = of_b(z0)
-        send_a_ref[rows, :] = of_a(1 - x0).astype(BF16)
-        send_b_ref[rows, :] = of_b(1 - z0).astype(BF16)
-
-
-def second_sum_kernel(kept_ref, got_a_ref, got_b_ref, out_ref):
-    cut = HEADS * PAIR // 2
-    out_ref[:, :cut] = (kept_ref[:, :cut] + got_a_ref[...].astype(F32)).astype(BF16)
-    out_ref[:, cut:] = (kept_ref[:, cut:] + got_b_ref[...].astype(F32)).astype(BF16)
-
-
-def head_sum_kernel(parts_ref, mine_ref, send_ref, sum_ref):
+        kept_ref[rows, :] = sum_ref[pl.ds(pl.multiple_of((2 * i + x0) * 16, 16), 16), :]
+        send_ref[rows, :] = sum_ref[
+            pl.ds(pl.multiple_of((2 * i + 1 - x0) * 16, 16), 16), :
+        ].astype(BF16)
+
+
+def head_sum_kernel(parts_ref, keep_ref, give_ref):
     total = parts_ref[0].astype(F32)
-    for i in range(1, 8):
+    for i in range(1, 16):
         total = total + parts_ref[i].astype(F32)
-    sum_ref[...] = total
-    xh = lax.axis_index("xh")
-    mine_ref[...] = sum_ref[pl.ds(pl.multiple_of(xh * 8, 8), 8), :]
-    send_ref[...] = sum_ref[pl.ds(pl.multiple_of((1 - xh) * 8, 8), 8), :].astype(BF16)
-
-
-def part_kernel(mine_ref, got_ref, keep_ref, give_ref):
-    total = mine_ref[...] + got_ref[...].astype(F32)
     keep_ref[:, :LATENT] = total[:, :LATENT]
     give_ref[:, :LATENT] = total[:, LATENT : 2 * LATENT]
     rope = total[:, 2 * LATENT :]
@@ -240,17 +202,15 @@
         ],
         470_000_000, lengths.reshape(1, -1), own, query, out_grad, up_weight,
     )
-    kep, ds, lat_mine, lat_theirs, theirs_a, theirs_b, *mine = call(
+    kep, ds, lat_mine, lat_theirs, theirs, mine = call(
         window_kernel,
         [
             (square, BF16),
             ((HEADS, 2, TOK, TOK), BF16),
             ((TOK // 2, 2 * LATENT + 2 * ROPE), F32),
             ((TOK // 2, 2 * LATENT + 2 * ROPE), BF16),
-            ((TOK, columns // 2), BF16),
-            ((TOK, columns // 2), BF16),
-            ((TOK, columns // 2), F32),
-            ((TOK, columns // 2), F32),
+            ((TOK, columns), BF16),
+            ((TOK, columns), F32),
         ],
         1_700_000_000, prev, start, own, qe, out_grad, up_weight, e, dp, lg,
         scratch=[
@@ -258,7 +218,7 @@
             pltpu.VMEM((2, TOK, columns), BF16),
         ],
     )
-    return lat_mine, lat_theirs, theirs_a, theirs_b, mine, (kep, keo, ds)
+    return lat_mine, lat_theirs, theirs, mine, (kep, keo, ds)
 
 
 def query_grad(saved):
@@ -274,35 +234,24 @@
     prev = ctx_shift(own, 1)
 
     columns = HEADS * PAIR
-    lat_mine, lat_theirs, theirs_a, theirs_b, mine, saved = attend(
+    lat_mine, lat_theirs, theirs, mine, saved = attend(
         own, prev, query, out_grad, up_weight, lengths
     )
     got_core = lax.ppermute(lat_theirs, "core", [(0, 1), (1, 0)])
-    got_a = flip(theirs_a, 4)
-    got_b = flip(theirs_b, 1)
-    (latent,) = call(core_sum_kernel, [(lat_mine.shape, BF16)], 1_000_000, lat_mine, got_core)
-    parts = lax.all_to_all(latent.reshape(8, 16, -1), "y", 0, 0)
-    kept, send_a, send_b = call(
+    got_z = flip(theirs, 4)
+    (latent,) = call(pair_sum_kernel, [(lat_mine.shape, BF16)], 1_000_000, lat_mine, got_core)
+    parts = lax.all_to_all(latent.reshape(16, 8, -1), ("xh", "y"), 0, 0)
+    kept, send = call(
         first_sum_kernel,
-        [((128, columns), F32), ((128, columns // 2), BF16), ((128, columns // 2), BF16)],
-        1_000_000, *mine, got_a, got_b,
-        scratch=[pltpu.VMEM((TOK, columns // 2), F32)] * 2,
-    )
-    next_a = flip(send_a, 1)
-    next_b = flip(send_b, 4)
+        [((128, columns), F32), ((128, columns), BF16)],
+        1_000_000, mine, got_z,
+        scratch=[pltpu.VMEM((TOK, columns), F32)],
+    )
+    got_x = flip(send, 1)
     dq = query_grad(saved)
-    (eighth,) = call(second_sum_kernel, [((128, columns), BF16)], 1_000_000, kept, next_a, next_b)
+    (eighth,) = call(pair_sum_kernel, [((128, columns), BF16)], 1_000_000, kept, got_x)
     eighths = lax.all_to_all(eighth.reshape(8, 16, -1), ("z2", "z1", "x1"), 0, 0)
-    rows = (8, 2 * LATENT + 2 * ROPE)
-    kept_rows, sent_rows = call(
-        head_sum_kernel,
-        [(rows, F32), (rows, BF16)],
-        1_000_000, parts,
-        scratch=[pltpu.VMEM((16, rows[1]), F32)],
-    )
-    pairs = [(0, 1), (1, 0)]
-    got_rows = lax.ppermute(sent_rows, "xh", pairs)
-    keep, give = call(part_kernel, [((8, LATENT + ROPE), F32)] * 2, 1_000_000, kept_rows, got_rows)
+    keep, give = call(head_sum_kernel, [((8, LATENT + ROPE), F32)] * 2, 1_000_000, parts)
     grad_compressed = keep + ctx_shift(give, -1)
     grad_weight = jnp.sum(eighths.astype(F32), axis=0)
     return dq, grad_compressed, grad_weight

time: 93 us -> 81.5 us (0.88)
  the two profiles are of different devices: /device:TPU:30 before, /device:TPU:48 now
where the time goes in v6:
time: 81.5 us; the launch traced here: 80.9 us
  starting transfers between devices  44.3 us (54%)
  waiting for transfers between devices  21.4 us (26%)
  Pallas kernels  9.07 us (11%)
  local copies, waits for them, and re-layouts  4.14 us (5%)
  other arithmetic  1.28 us (2%)
    all_to_all x1, starting transfers between devices, body(): lax.all_to_all(eighth.reshape(8, 16, -1), ('z2', 'z1', 'x1'), 0, 0)  14.7 us
    all_to_all x1, starting transfers between devices, body(): parts = lax.all_to_all(latent.reshape(16, 8, -1), ('xh', 'y'), 0, 0)  12.4 us
    ppermute x2, starting transfers between devices, flip(): return lax.ppermute(x, CTX, [(i, i ^ mask) for i in range(32)])  10.7 us
    ppermute x2, waiting for transfers between devices, flip(): return lax.ppermute(x, CTX, [(i, i ^ mask) for i in range(32)])  9.66 us
    pallas_call x7, Pallas kernels, call(): pl.pallas_call(kernel, out_shape=[jax.ShapeDtypeStruct(s, d) for s, d in...  9.07 us
    all_to_all x1, waiting for transfers between devices, body(): lax.all_to_all(eighth.reshape(8, 16, -1), ('z2', 'z1', 'x1'), 0, 0)  7.03 us
    ppermute x2, starting transfers between devices, ctx_shift(): return lax.ppermute(x, CTX, pairs)  4.69 us
    ppermute x2, waiting for transfers between devices, ctx_shift(): return lax.ppermute(x, CTX, pairs)  4.68 us
  transfers between devices with their start and end apart: 7, of which 4 were waited for; matrix products, arithmetic and copies ran while one was open for 1% of the time, Pallas kernels for 6%

profile of v6, /device:TPU:48, one launch (start us, length us, event | category | flops | bytes accessed | tf_op | source)
XLA Modules:
  0.0 80.9 jit_solution(917116403556680913)
XLA Ops:
  0.6 3.4 %collective-permute-start = (bf16[576,256]{1,0:T(8,128)(2,1)}, bf16[576,256]{1,0:T(8,128)(2,1)S(1)}, u32[]{:S(2)}, u32[]{:S(2)}) collective-permute-start(bf16[576,256]{1,0:T(8,128)(2,1)} %bitcast.4), channel_id=1, source_target_pairs={{0,32},{32,64},{64,96},{96,128},{128,160},{160,192},{192,224},{224... | collective-permute-start | bytes 884744 | tf_op jit(solution)/shard_map/ppermute | solution.py:36
  4.1 1.2 %copy-done = bf16[512,1024]{1,0:T(8,128)(2,1)S(1)} copy-done((bf16[512,1024]{1,0:T(8,128)(2,1)S(1)}, bf16[512,1024]{1,0:T(8,128)(2,1)}, u32[]{:S(2)}) %copy-start) | copy-done | bytes 1048600
  5.3 1.0 %copy-done.2 = bf16[256,768]{1,0:T(8,128)(2,1)S(1)} copy-done((bf16[256,768]{1,0:T(8,128)(2,1)S(1)}, bf16[256,768]{1,0:T(8,128)(2,1)}, u32[]{:S(2)}) %copy-start.2) | copy-done | bytes 393240
  6.3 1.0 %copy-done.3 = bf16[256,576]{0,1:T(8,128)(2,1)S(1)} copy-done((bf16[256,576]{0,1:T(8,128)(2,1)S(1)}, bf16[256,576]{0,1:T(8,128)(2,1)}, u32[]{:S(2)}) %copy-start.3) | copy-done | bytes 294936
  7.3 0.9 %copy-done.5 = bf16[256,512]{1,0:T(8,128)(2,1)S(1)} copy-done((bf16[256,512]{1,0:T(8,128)(2,1)S(1)}, bf16[256,512]{1,0:T(8,128)(2,1)}, u32[]{:S(2)}) %copy-start.5) | copy-done | bytes 262168
  8.2 0.8 %shard_map.76 = (bf16[4,256,256]{2,1,0:T(8,128)(2,1)S(1)}, bf16[4,256,256]{2,1,0:T(8,128)(2,1)S(1)}, f32[4,256,256]{2,1,0:T(8,128)S(1)}, f32[4,256,256]{2,1,0:T(...) custom-call(s32[1,96]{1,0:T(1,128)S(1)} %bitcast.7, bf16[576,256]{1,0:T(8,128)(2,1)S(1)} %bitcast.5, ...), custom_call_target="tpu_custom_call" | custom-call | flops 470000000 | bytes 4194304 | tf_op jit(solution)/shard_map/pallas_call | solution.py:179
  9.0 1.6 %collective-permute-done.xt_ref = bf16[576,256]{1,0:T(8,128)(2,1)S(1)} collective-permute-done((bf16[576,256]{1,0:T(8,128)(2,1)}, bf16[576,256]{1,0:T(8,128)(2,1)S(1)}, u32[]{:S(2)}, u32[]{:S(2)}) %collective-permute-start) | collective-permute-done | bytes 294944 | tf_op jit(solution)/shard_map/ppermute | solution.py:36
  10.6 4.1 %shard_map.77 = (bf16[4,256,256]{2,1,0:T(8,128)(2,1)S(1)}, bf16[4,2,256,256]{3,2,1,0:T(8,128)(2,1)S(1)}, f32[128,1152]{1,0:T(8,128)S(1)}, bf16[128,1152]{1,0:T(8...) custom-call(bf16[576,256]{1,0:T(8,128)(2,1)S(1)} %collective-permute-done.xt_ref, ...), custom_call_target="tpu_custom_call" | custom-call | flops 1700000000 | bytes 4194304 | tf_op jit(solution)/shard_map/pallas_call | solution.py:179
  14.7 1.9 %collective-permute-start.1 = (bf16[128,1152]{1,0:T(8,128)(2,1)S(1)}, bf16[128,1152]{1,0:T(8,128)(2,1)S(1)}, u32[]{:S(2)}, u32[]{:S(2)}) collective-permute-start(bf16[128,1152]{1,0:T(8,128)(2,1)S(1)} %get-tuple-element.28), channel_id=1, source_target_pairs={{0,1},{1,0},{2,3},{3,2},{4,5},{5,4},{6,7},{7,6},{8,9},{9,8},{10,11... | collective-permute-start | bytes 884744 | tf_op jit(solution)/shard_map/ppermute | solution.py:240
  16.6 8.8 %collective-permute-start.3 = (bf16[256,1024]{1,0:T(8,128)(2,1)}, bf16[256,1024]{1,0:T(8,128)(2,1)}, u32[]{:S(2)}, u32[]{:S(2)}) collective-permute-start(bf16[256,1024]{1,0:T(8,128)(2,1)} %get-tuple-element.32), channel_id=1, source_target_pairs={{0,128},{32,160},{64,192},{96,224},{128,0},{160,32},{192,64},{224,... | collective-permute-start | bytes 1572872 | tf_op jit(solution)/shard_map/ppermute | solution.py:229
  25.4 0.8 shard_map.79
  26.2 12.4 %all-to-all-start = ((bf16[16,8,1152]{2,1,0:T(8,128)(2,1)}), bf16[16,8,1152]{2,1,0:T(8,128)(2,1)S(1)}, u32[]{:S(2)}, u32[]{:S(2)}) async-start(bf16[16,8,1152]{2,1,0:T(8,128)(2,1)} %bitcast.2), calls=%async_computation | async-start | bytes 589824 | tf_op jit(solution)/shard_map/all_to_all | solution.py:243
  38.5 1.3 %shard_map.81 = (f32[128,1024]{1,0:T(8,128)S(1)}, bf16[128,1024]{1,0:T(8,128)(2,1)S(1)}) custom-call(f32[256,1024]{1,0:T(8,128)S(1)} %get-tuple-element.31.mine_ref, bf16[256,1024]{1,0:T(8,128)(2,1)} %collective-permute-done.3.got_ref), custom_call_target="tpu_custom_call" | custom-call | flops 1000000 | bytes 4194304 | tf_op jit(solution)/shard_map/pallas_call | solution.py:179
  39.8 1.9 %collective-permute-start.4 = (bf16[128,1024]{1,0:T(8,128)(2,1)S(1)}, bf16[128,1024]{1,0:T(8,128)(2,1)S(1)}, u32[]{:S(2)}, u32[]{:S(2)}) collective-permute-start(bf16[128,1024]{1,0:T(8,128)(2,1)S(1)} %get-tuple-element.34), channel_id=1, source_target_pairs={{0,32},{32,0},{64,96},{96,64},{128,160},{160,128},{192,224},{224,1... | collective-permute-start | bytes 786440 | tf_op jit(solution)/shard_map/ppermute | solution.py:229
  41.8 9.7 %collective-permute-done.4.got_ref = bf16[128,1024]{1,0:T(8,128)(2,1)S(1)} collective-permute-done((bf16[128,1024]{1,0:T(8,128)(2,1)S(1)}, bf16[128,1024]{1,0:T(8,128)(2,1)S(1)}, u32[]{:S(2)}, u32[]{:S(2)}) %collective-permute-start.4) | collective-permute-done | bytes 262176 | tf_op jit(solution)/shard_map/ppermute | solution.py:229
  51.4 0.7 shard_map.82
  52.1 14.7 %all-to-all-start.1 = ((bf16[8,16,1024]{2,1,0:T(8,128)(2,1)}), bf16[8,16,1024]{2,1,0:T(8,128)(2,1)S(1)}, u32[]{:S(2)}, u32[]{:S(2)}) async-start(bf16[8,16,1024]{2,1,0:T(8,128)(2,1)} %bitcast.3), calls=%async_computation.1 | async-start | bytes 524288 | tf_op jit(solution)/shard_map/all_to_all | solution.py:253
  66.8 0.1 shard_map.80
  66.9 1.3 %collective-permute-start.2 = (f32[8,576]{1,0:T(8,128)S(1)}, f32[8,576]{1,0:T(8,128)S(1)}, u32[]{:S(2)}, u32[]{:S(2)}) collective-permute-start(f32[8,576]{1,0:T(8,128)S(1)} %get-tuple-element.30), channel_id=1, source_target_pairs={{32,0},{64,32},{96,64},{128,96},{160,128},{192,160},{224,192},{256... | collective-permute-start | bytes 55304 | tf_op jit(solution)/shard_map/ppermute | solution.py:36
  68.2 1.3 %shard_map.78 = bf16[256,768]{1,0:T(8,128)(2,1)} custom-call(bf16[4,256,256]{2,1,0:T(8,128)(2,1)S(1)} %get-tuple-element.24.kep_ref, bf16[4,256,256]{2,1,0:T(8,128)(2,1)S(1)} %get-tuple-element.25.keo_ref, bf16[4,2,256,256]{3,2,1,0:T(8,128)(2,1)S(1)} %get-tuple-element.26.ds_ref), custom_call_target="tpu_custom_call" | custom-call | flops 270000000 | bytes 4194304 | tf_op jit(solution)/shard_map/pallas_call | solution.py:179
  69.5 3.1 %collective-permute-done.2 = f32[8,576]{1,0:T(8,128)S(1)} collective-permute-done((f32[8,576]{1,0:T(8,128)S(1)}, f32[8,576]{1,0:T(8,128)S(1)}, u32[]{:S(2)}, u32[]{:S(2)}) %collective-permute-start.2) | collective-permute-done | bytes 18464 | tf_op jit(solution)/shard_map/ppermute | solution.py:36
  72.6 0.6 add.3
  73.2 7.0 %all-to-all-done.1 = bf16[8,16,1024]{2,1,0:T(8,128)(2,1)S(1)} async-done(((bf16[8,16,1024]{2,1,0:T(8,128)(2,1)}), bf16[8,16,1024]{2,1,0:T(8,128)(2,1)S(1)}, u32[]{:S(2)}, u32[]{:S(2)}) %all-to-all-start.1) | async-done | bytes 262176 | tf_op jit(solution)/shard_map/all_to_all | solution.py:253
  80.2 0.7 convert_reduce_fusion
  (13 shorter events, 0.0 us)
Async XLA Ops:
  0.6 3.4 %copy-start.6 = (s32[96]{0:T(128)S(1)}, s32[96]{0:T(128)}, u32[]{:S(2)}) copy-start(s32[96]{0:T(128)} %param.9) | copy-start | bytes 1156
  0.6 10.0 %collective-permute-start = (bf16[576,256]{1,0:T(8,128)(2,1)}, bf16[576,256]{1,0:T(8,128)(2,1)S(1)}, u32[]{:S(2)}, u32[]{:S(2)}) collective-permute-start(bf16[576,256]{1,0:T(8,128)(2,1)} %bitcast.4), channel_id=1, source_target_pairs={{0,32},{32,64},{64,96},{96,128},{128,160},{160,192},{192,224},{224... | collective-permute-start | bytes 884744 | tf_op jit(solution)/shard_map/ppermute | solution.py:36
  4.1 1.2 %copy-start = (bf16[512,1024]{1,0:T(8,128)(2,1)S(1)}, bf16[512,1024]{1,0:T(8,128)(2,1)}, u32[]{:S(2)}) copy-start(bf16[512,1024]{1,0:T(8,128)(2,1)} %w_ref.3) | copy-start | bytes 3145732
  5.3 1.0 %copy-start.2 = (bf16[256,768]{1,0:T(8,128)(2,1)S(1)}, bf16[256,768]{1,0:T(8,128)(2,1)}, u32[]{:S(2)}) copy-start(bf16[256,768]{1,0:T(8,128)(2,1)} %q_ref.1) | copy-start | bytes 1179652
  6.3 1.0 %copy-start.3 = (bf16[256,576]{0,1:T(8,128)(2,1)S(1)}, bf16[256,576]{0,1:T(8,128)(2,1)}, u32[]{:S(2)}) copy-start(bf16[256,576]{0,1:T(8,128)(2,1)} %param.5) | copy-start | bytes 884740
  7.3 0.9 %copy-start.5 = (bf16[256,512]{1,0:T(8,128)(2,1)S(1)}, bf16[256,512]{1,0:T(8,128)(2,1)}, u32[]{:S(2)}) copy-start(bf16[256,512]{1,0:T(8,128)(2,1)} %do_ref.3) | copy-start | bytes 786436
  8.2 2.4 %copy-start.1 = (bf16[512,1024]{1,0:T(8,128)(2,1)S(1)}, bf16[512,1024]{1,0:T(8,128)(2,1)}, u32[]{:S(2)}) copy-start(bf16[512,1024]{1,0:T(8,128)(2,1)} %w_ref.3) | copy-start | bytes 3145732
  8.2 2.4 %copy-start.4 = (bf16[256,576]{0,1:T(8,128)(2,1)S(1)}, bf16[256,576]{0,1:T(8,128)(2,1)}, u32[]{:S(2)}) copy-start(bf16[256,576]{0,1:T(8,128)(2,1)} %param.5) | copy-start | bytes 884740
  14.7 10.7 %collective-permute-start.1 = (bf16[128,1152]{1,0:T(8,128)(2,1)S(1)}, bf16[128,1152]{1,0:T(8,128)(2,1)S(1)}, u32[]{:S(2)}, u32[]{:S(2)}) collective-permute-start(bf16[128,1152]{1,0:T(8,128)(2,1)S(1)} %get-tuple-element.28), channel_id=1, source_target_pairs={{0,1},{1,0},{2,3},{3,2},{4,5},{5,4},{6,7},{7,6},{8,9},{9,8},{10,11... | collective-permute-start | bytes 884744 | tf_op jit(solution)/shard_map/ppermute | solution.py:240
  16.6 21.9 %collective-permute-start.3 = (bf16[256,1024]{1,0:T(8,128)(2,1)}, bf16[256,1024]{1,0:T(8,128)(2,1)}, u32[]{:S(2)}, u32[]{:S(2)}) collective-permute-start(bf16[256,1024]{1,0:T(8,128)(2,1)} %get-tuple-element.32), channel_id=1, source_target_pairs={{0,128},{32,160},{64,192},{96,224},{128,0},{160,32},{192,64},{224,... | collective-permute-start | bytes 1572872 | tf_op jit(solution)/shard_map/ppermute | solution.py:229
  26.2 26.0 %all-to-all-start = ((bf16[16,8,1152]{2,1,0:T(8,128)(2,1)}), bf16[16,8,1152]{2,1,0:T(8,128)(2,1)S(1)}, u32[]{:S(2)}, u32[]{:S(2)}) async-start(bf16[16,8,1152]{2,1,0:T(8,128)(2,1)} %bitcast.2), calls=%async_computation | async-start | bytes 589824 | tf_op jit(solution)/shard_map/all_to_all | solution.py:243
  39.8 11.6 %collective-permute-start.4 = (bf16[128,1024]{1,0:T(8,128)(2,1)S(1)}, bf16[128,1024]{1,0:T(8,128)(2,1)S(1)}, u32[]{:S(2)}, u32[]{:S(2)}) collective-permute-start(bf16[128,1024]{1,0:T(8,128)(2,1)S(1)} %get-tuple-element.34), channel_id=1, source_target_pairs={{0,32},{32,0},{64,96},{96,64},{128,160},{160,128},{192,224},{224,1... | collective-permute-start | bytes 786440 | tf_op jit(solution)/shard_map/ppermute | solution.py:229
  52.1 28.1 %all-to-all-start.1 = ((bf16[8,16,1024]{2,1,0:T(8,128)(2,1)}), bf16[8,16,1024]{2,1,0:T(8,128)(2,1)S(1)}, u32[]{:S(2)}, u32[]{:S(2)}) async-start(bf16[8,16,1024]{2,1,0:T(8,128)(2,1)} %bitcast.3), calls=%async_computation.1 | async-start | bytes 524288 | tf_op jit(solution)/shard_map/all_to_all | solution.py:253
  66.9 5.7 %collective-permute-start.2 = (f32[8,576]{1,0:T(8,128)S(1)}, f32[8,576]{1,0:T(8,128)S(1)}, u32[]{:S(2)}, u32[]{:S(2)}) collective-permute-start(f32[8,576]{1,0:T(8,128)S(1)} %get-tuple-element.30), channel_id=1, source_target_pairs={{32,0},{64,32},{96,64},{128,96},{160,128},{192,160},{224,192},{256... | collective-permute-start | bytes 55304 | tf_op jit(solution)/shard_map/ppermute | solution.py:36

commit v7 on v6

--- a/solution.py
+++ b/solution.py
@@ -89,8 +89,8 @@
         lg_ref[h + 4 : h + 5, :] = jnp.sum(e * dp, axis=0, keepdims=True)
 
 
-def rows_of(xt_ref, z0):
-    rows = [xt_ref[pl.ds(pl.multiple_of((2 * i + z0) * 64, 64), 64), :] for i in range(4)]
+def rows_of(xt_ref, x0):
+    rows = [xt_ref[pl.ds(pl.multiple_of((2 * i + x0) * 16, 16), 16), :] for i in range(16)]
     return jnp.concatenate(rows, axis=0)
 
 
@@ -121,7 +121,7 @@
             dkv_ref[half, :, h * PAIR + NOPE : (h + 1) * PAIR] = dot(
                 probs.astype(BF16), do
             ).astype(BF16)
-    z0, core = lax.axis_index("z0"), lax.axis_index("core")
+    x0, core = lax.axis_index("x0"), lax.axis_index("core")
     total_ref[:, :LATENT] = dot(dkv_ref[1], w_ref[...], NT)
     total_ref[:, LATENT : 2 * LATENT] = dot(dkv_ref[0], w_ref[...], NT)
     total_ref[:, 2 * LATENT :] = rope_grads[1] + pltpu.roll(rope_grads[0], ROPE, 1)
@@ -133,8 +133,8 @@
             ]
             out_ref[16 * i : 16 * i + 16, :] = jnp.concatenate(pair, axis=0).astype(out_ref.dtype)
     sources = (xt_ref, own_ref)
-    theirs_ref[...] = sum(dot(rows_of(sources[u], 1 - z0), dkv_ref[u]) for u in range(2)).astype(BF16)
-    mine_ref[...] = sum(dot(rows_of(sources[u], z0), dkv_ref[u]) for u in range(2))
+    theirs_ref[...] = sum(dot(rows_of(sources[u], 1 - x0), dkv_ref[u]) for u in range(2)).astype(BF16)
+    mine_ref[...] = sum(dot(rows_of(sources[u], x0), dkv_ref[u]) for u in range(2))
 
 
 def pair_sum_kernel(mine_ref, got_ref, out_ref):
@@ -155,12 +155,13 @@
 
 def first_sum_kernel(mine_ref, got_ref, kept_ref, send_ref, sum_ref):
     sum_ref[...] = mine_ref[...] + got_ref[...].astype(F32)
-    x0 = lax.axis_index("x0")
+    z0 = lax.axis_index("z0")
     for i in range(8):
         rows = slice(16 * i, 16 * i + 16)
-        kept_ref[rows, :] = sum_ref[pl.ds(pl.multiple_of((2 * i + x0) * 16, 16), 16), :]
+        base = (i // 2) * 64 + (i % 2) * 16
+        kept_ref[rows, :] = sum_ref[pl.ds(pl.multiple_of(base + z0 * 32, 16), 16), :]
         send_ref[rows, :] = sum_ref[
-            pl.ds(pl.multiple_of((2 * i + 1 - x0) * 16, 16), 16), :
+            pl.ds(pl.multiple_of(base + (1 - z0) * 32, 16), 16), :
         ].astype(BF16)
 
 
@@ -238,18 +239,18 @@
         own, prev, query, out_grad, up_weight, lengths
     )
     got_core = lax.ppermute(lat_theirs, "core", [(0, 1), (1, 0)])
-    got_z = flip(theirs, 4)
+    got_x = flip(theirs, 1)
     (latent,) = call(pair_sum_kernel, [(lat_mine.shape, BF16)], 1_000_000, lat_mine, got_core)
     parts = lax.all_to_all(latent.reshape(16, 8, -1), ("xh", "y"), 0, 0)
     kept, send = call(
         first_sum_kernel,
         [((128, columns), F32), ((128, columns), BF16)],
-        1_000_000, mine, got_z,
+        1_000_000, mine, got_x,
         scratch=[pltpu.VMEM((TOK, columns), F32)],
     )
-    got_x = flip(send, 1)
+    got_z = flip(send, 4)
     dq = query_grad(saved)
-    (eighth,) = call(pair_sum_kernel, [((128, columns), BF16)], 1_000_000, kept, got_x)
+    (eighth,) = call(pair_sum_kernel, [((128, columns), BF16)], 1_000_000, kept, got_z)
     eighths = lax.all_to_all(eighth.reshape(8, 16, -1), ("z2", "z1", "x1"), 0, 0)
     keep, give = call(head_sum_kernel, [((8, LATENT + ROPE), F32)] * 2, 1_000_000, parts)
     grad_compressed = keep + ctx_shift(give, -1)

time: 81.5 us -> 82.5 us (1.012)
  the two profiles are of different devices: /device:TPU:48 before, /device:TPU:78 now
where the time goes in v7:
time: 82.5 us; the launch traced here: 81.9 us
  starting transfers between devices  48.3 us (59%)
  waiting for transfers between devices  18.4 us (22%)
  Pallas kernels  9.08 us (11%)
  local copies, waits for them, and re-layouts  4.14 us (5%)
  other arithmetic  1.28 us (2%)
    all_to_all x1, starting transfers between devices, body(): lax.all_to_all(eighth.reshape(8, 16, -1), ('z2', 'z1', 'x1'), 0, 0)  19.3 us
    all_to_all x1, starting transfers between devices, body(): parts = lax.all_to_all(latent.reshape(16, 8, -1), ('xh', 'y'), 0, 0)  12 us
    ppermute x2, waiting for transfers between devices, flip(): return lax.ppermute(x, CTX, [(i, i ^ mask) for i in range(32)])  11.3 us
    ppermute x2, starting transfers between devices, ctx_shift(): return lax.ppermute(x, CTX, pairs)  11.2 us
    pallas_call x7, Pallas kernels, call(): pl.pallas_call(kernel, out_shape=[jax.ShapeDtypeStruct(s, d) for s, d in...  9.08 us
    ppermute x2, waiting for transfers between devices, ctx_shift(): return lax.ppermute(x, CTX, pairs)  5.51 us
    unnamed x14, local copies, waits for them, and re-layouts  4.14 us
    ppermute x2, starting transfers between devices, flip(): return lax.ppermute(x, CTX, [(i, i ^ mask) for i in range(32)])  3.9 us
  transfers between devices with their start and end apart: 7, of which 5 were waited for; matrix products, arithmetic and copies ran while one was open for 1% of the time, Pallas kernels for 6%

profile of v7, /device:TPU:78, one launch (start us, length us, event | category | flops | bytes accessed | tf_op | source)
XLA Modules:
  0.0 81.9 jit_solution(6880719494289623839)
XLA Ops:
  0.6 7.8 %collective-permute-start = (bf16[576,256]{1,0:T(8,128)(2,1)}, bf16[576,256]{1,0:T(8,128)(2,1)S(1)}, u32[]{:S(2)}, u32[]{:S(2)}) collective-permute-start(bf16[576,256]{1,0:T(8,128)(2,1)} %bitcast.4), channel_id=1, source_target_pairs={{0,32},{32,64},{64,96},{96,128},{128,160},{160,192},{192,224},{224... | collective-permute-start | bytes 884744 | tf_op jit(solution)/shard_map/ppermute | solution.py:36
  8.5 1.2 %copy-done = bf16[512,1024]{1,0:T(8,128)(2,1)S(1)} copy-done((bf16[512,1024]{1,0:T(8,128)(2,1)S(1)}, bf16[512,1024]{1,0:T(8,128)(2,1)}, u32[]{:S(2)}) %copy-start) | copy-done | bytes 1048600
  9.7 1.0 %copy-done.2 = bf16[256,768]{1,0:T(8,128)(2,1)S(1)} copy-done((bf16[256,768]{1,0:T(8,128)(2,1)S(1)}, bf16[256,768]{1,0:T(8,128)(2,1)}, u32[]{:S(2)}) %copy-start.2) | copy-done | bytes 393240
  10.7 1.0 %copy-done.3 = bf16[256,576]{0,1:T(8,128)(2,1)S(1)} copy-done((bf16[256,576]{0,1:T(8,128)(2,1)S(1)}, bf16[256,576]{0,1:T(8,128)(2,1)}, u32[]{:S(2)}) %copy-start.3) | copy-done | bytes 294936
  11.6 0.9 %copy-done.5 = bf16[256,512]{1,0:T(8,128)(2,1)S(1)} copy-done((bf16[256,512]{1,0:T(8,128)(2,1)S(1)}, bf16[256,512]{1,0:T(8,128)(2,1)}, u32[]{:S(2)}) %copy-start.5) | copy-done | bytes 262168
  12.6 0.8 %shard_map.76 = (bf16[4,256,256]{2,1,0:T(8,128)(2,1)S(1)}, bf16[4,256,256]{2,1,0:T(8,128)(2,1)S(1)}, f32[4,256,256]{2,1,0:T(8,128)S(1)}, f32[4,256,256]{2,1,0:T(...) custom-call(s32[1,96]{1,0:T(1,128)S(1)} %bitcast.7, bf16[576,256]{1,0:T(8,128)(2,1)S(1)} %bitcast.5, ...), custom_call_target="tpu_custom_call" | custom-call | flops 470000000 | bytes 4194304 | tf_op jit(solution)/shard_map/pallas_call | solution.py:180
  13.4 1.6 %collective-permute-done.xt_ref = bf16[576,256]{1,0:T(8,128)(2,1)S(1)} collective-permute-done((bf16[576,256]{1,0:T(8,128)(2,1)}, bf16[576,256]{1,0:T(8,128)(2,1)S(1)}, u32[]{:S(2)}, u32[]{:S(2)}) %collective-permute-start) | collective-permute-done | bytes 294944 | tf_op jit(solution)/shard_map/ppermute | solution.py:36
  15.0 4.1 %shard_map.77 = (bf16[4,256,256]{2,1,0:T(8,128)(2,1)S(1)}, bf16[4,2,256,256]{3,2,1,0:T(8,128)(2,1)S(1)}, f32[128,1152]{1,0:T(8,128)S(1)}, bf16[128,1152]{1,0:T(8...) custom-call(bf16[576,256]{1,0:T(8,128)(2,1)S(1)} %collective-permute-done.xt_ref, ...), custom_call_target="tpu_custom_call" | custom-call | flops 1700000000 | bytes 4194304 | tf_op jit(solution)/shard_map/pallas_call | solution.py:180
  19.1 1.9 %collective-permute-start.1 = (bf16[128,1152]{1,0:T(8,128)(2,1)S(1)}, bf16[128,1152]{1,0:T(8,128)(2,1)S(1)}, u32[]{:S(2)}, u32[]{:S(2)}) collective-permute-start(bf16[128,1152]{1,0:T(8,128)(2,1)S(1)} %get-tuple-element.28), channel_id=1, source_target_pairs={{0,1},{1,0},{2,3},{3,2},{4,5},{5,4},{6,7},{7,6},{8,9},{9,8},{10,11... | collective-permute-start | bytes 884744 | tf_op jit(solution)/shard_map/ppermute | solution.py:241
  21.0 1.9 %collective-permute-start.3 = (bf16[256,1024]{1,0:T(8,128)(2,1)}, bf16[256,1024]{1,0:T(8,128)(2,1)}, u32[]{:S(2)}, u32[]{:S(2)}) collective-permute-start(bf16[256,1024]{1,0:T(8,128)(2,1)} %get-tuple-element.32), channel_id=1, source_target_pairs={{0,32},{32,0},{64,96},{96,64},{128,160},{160,128},{192,224},{224,1... | collective-permute-start | bytes 1572872 | tf_op jit(solution)/shard_map/ppermute | solution.py:230
  23.0 0.8 shard_map.79
  23.7 12.0 %all-to-all-start = ((bf16[16,8,1152]{2,1,0:T(8,128)(2,1)}), bf16[16,8,1152]{2,1,0:T(8,128)(2,1)S(1)}, u32[]{:S(2)}, u32[]{:S(2)}) async-start(bf16[16,8,1152]{2,1,0:T(8,128)(2,1)} %bitcast.2), calls=%async_computation | async-start | bytes 589824 | tf_op jit(solution)/shard_map/all_to_all | solution.py:244
  35.8 5.0 %collective-permute-done.3.got_ref = bf16[256,1024]{1,0:T(8,128)(2,1)} collective-permute-done((bf16[256,1024]{1,0:T(8,128)(2,1)}, bf16[256,1024]{1,0:T(8,128)(2,1)}, u32[]{:S(2)}, u32[]{:S(2)}) %collective-permute-start.3) | collective-permute-done | bytes 524320 | tf_op jit(solution)/shard_map/ppermute | solution.py:230
  40.8 1.3 %shard_map.81 = (f32[128,1024]{1,0:T(8,128)S(1)}, bf16[128,1024]{1,0:T(8,128)(2,1)S(1)}) custom-call(f32[256,1024]{1,0:T(8,128)S(1)} %get-tuple-element.31.mine_ref, bf16[256,1024]{1,0:T(8,128)(2,1)} %collective-permute-done.3.got_ref), custom_call_target="tpu_custom_call" | custom-call | flops 1000000 | bytes 4194304 | tf_op jit(solution)/shard_map/pallas_call | solution.py:180
  42.0 2.0 %collective-permute-start.4 = (bf16[128,1024]{1,0:T(8,128)(2,1)S(1)}, bf16[128,1024]{1,0:T(8,128)(2,1)S(1)}, u32[]{:S(2)}, u32[]{:S(2)}) collective-permute-start(bf16[128,1024]{1,0:T(8,128)(2,1)S(1)} %get-tuple-element.34), channel_id=1, source_target_pairs={{0,128},{32,160},{64,192},{96,224},{128,0},{160,32},{192,64},{224,... | collective-permute-start | bytes 786440 | tf_op jit(solution)/shard_map/ppermute | solution.py:230
  44.0 6.3 %collective-permute-done.4.got_ref = bf16[128,1024]{1,0:T(8,128)(2,1)S(1)} collective-permute-done((bf16[128,1024]{1,0:T(8,128)(2,1)S(1)}, bf16[128,1024]{1,0:T(8,128)(2,1)S(1)}, u32[]{:S(2)}, u32[]{:S(2)}) %collective-permute-start.4) | collective-permute-done | bytes 262176 | tf_op jit(solution)/shard_map/ppermute | solution.py:230
  50.3 0.7 shard_map.82
  51.0 19.3 %all-to-all-start.1 = ((bf16[8,16,1024]{2,1,0:T(8,128)(2,1)}), bf16[8,16,1024]{2,1,0:T(8,128)(2,1)S(1)}, u32[]{:S(2)}, u32[]{:S(2)}) async-start(bf16[8,16,1024]{2,1,0:T(8,128)(2,1)} %bitcast.3), calls=%async_computation.1 | async-start | bytes 524288 | tf_op jit(solution)/shard_map/all_to_all | solution.py:254
  70.4 3.4 %collective-permute-start.2 = (f32[8,576]{1,0:T(8,128)S(1)}, f32[8,576]{1,0:T(8,128)S(1)}, u32[]{:S(2)}, u32[]{:S(2)}) collective-permute-start(f32[8,576]{1,0:T(8,128)S(1)} %get-tuple-element.30), channel_id=1, source_target_pairs={{32,0},{64,32},{96,64},{128,96},{160,128},{192,160},{224,192},{256... | collective-permute-start | bytes 55304 | tf_op jit(solution)/shard_map/ppermute | solution.py:36
  73.8 1.3 %shard_map.78 = bf16[256,768]{1,0:T(8,128)(2,1)} custom-call(bf16[4,256,256]{2,1,0:T(8,128)(2,1)S(1)} %get-tuple-element.24.kep_ref, bf16[4,256,256]{2,1,0:T(8,128)(2,1)S(1)} %get-tuple-element.25.keo_ref, bf16[4,2,256,256]{3,2,1,0:T(8,128)(2,1)S(1)} %get-tuple-element.26.ds_ref), custom_call_target="tpu_custom_call" | custom-call | flops 270000000 | bytes 4194304 | tf_op jit(solution)/shard_map/pallas_call | solution.py:180
  75.1 3.9 %collective-permute-done.2 = f32[8,576]{1,0:T(8,128)S(1)} collective-permute-done((f32[8,576]{1,0:T(8,128)S(1)}, f32[8,576]{1,0:T(8,128)S(1)}, u32[]{:S(2)}, u32[]{:S(2)}) %collective-permute-start.2) | collective-permute-done | bytes 18464 | tf_op jit(solution)/shard_map/ppermute | solution.py:36
  79.0 0.6 add.3
  79.6 1.6 %all-to-all-done.1 = bf16[8,16,1024]{2,1,0:T(8,128)(2,1)S(1)} async-done(((bf16[8,16,1024]{2,1,0:T(8,128)(2,1)}), bf16[8,16,1024]{2,1,0:T(8,128)(2,1)S(1)}, u32[]{:S(2)}, u32[]{:S(2)}) %all-to-all-start.1) | async-done | bytes 262176 | tf_op jit(solution)/shard_map/all_to_all | solution.py:254
  81.2 0.7 convert_reduce_fusion
  (13 shorter events, 0.1 us)
Async XLA Ops:
  0.6 7.8 %copy-start.6 = (s32[96]{0:T(128)S(1)}, s32[96]{0:T(128)}, u32[]{:S(2)}) copy-start(s32[96]{0:T(128)} %param.9) | copy-start | bytes 1156
  0.6 14.4 %collective-permute-start = (bf16[576,256]{1,0:T(8,128)(2,1)}, bf16[576,256]{1,0:T(8,128)(2,1)S(1)}, u32[]{:S(2)}, u32[]{:S(2)}) collective-permute-start(bf16[576,256]{1,0:T(8,128)(2,1)} %bitcast.4), channel_id=1, source_target_pairs={{0,32},{32,64},{64,96},{96,128},{128,160},{160,192},{192,224},{224... | collective-permute-start | bytes 884744 | tf_op jit(solution)/shard_map/ppermute | solution.py:36
  8.5 1.2 %copy-start = (bf16[512,1024]{1,0:T(8,128)(2,1)S(1)}, bf16[512,1024]{1,0:T(8,128)(2,1)}, u32[]{:S(2)}) copy-start(bf16[512,1024]{1,0:T(8,128)(2,1)} %w_ref.3) | copy-start | bytes 3145732
  9.7 1.0 %copy-start.2 = (bf16[256,768]{1,0:T(8,128)(2,1)S(1)}, bf16[256,768]{1,0:T(8,128)(2,1)}, u32[]{:S(2)}) copy-start(bf16[256,768]{1,0:T(8,128)(2,1)} %q_ref.1) | copy-start | bytes 1179652
  10.7 1.0 %copy-start.3 = (bf16[256,576]{0,1:T(8,128)(2,1)S(1)}, bf16[256,576]{0,1:T(8,128)(2,1)}, u32[]{:S(2)}) copy-start(bf16[256,576]{0,1:T(8,128)(2,1)} %param.5) | copy-start | bytes 884740
  11.6 0.9 %copy-start.5 = (bf16[256,512]{1,0:T(8,128)(2,1)S(1)}, bf16[256,512]{1,0:T(8,128)(2,1)}, u32[]{:S(2)}) copy-start(bf16[256,512]{1,0:T(8,128)(2,1)} %do_ref.3) | copy-start | bytes 786436
  12.6 2.4 %copy-start.1 = (bf16[512,1024]{1,0:T(8,128)(2,1)S(1)}, bf16[512,1024]{1,0:T(8,128)(2,1)}, u32[]{:S(2)}) copy-start(bf16[512,1024]{1,0:T(8,128)(2,1)} %w_ref.3) | copy-start | bytes 3145732
  12.6 2.4 %copy-start.4 = (bf16[256,576]{0,1:T(8,128)(2,1)S(1)}, bf16[256,576]{0,1:T(8,128)(2,1)}, u32[]{:S(2)}) copy-start(bf16[256,576]{0,1:T(8,128)(2,1)} %param.5) | copy-start | bytes 884740
  19.1 3.8 %collective-permute-start.1 = (bf16[128,1152]{1,0:T(8,128)(2,1)S(1)}, bf16[128,1152]{1,0:T(8,128)(2,1)S(1)}, u32[]{:S(2)}, u32[]{:S(2)}) collective-permute-start(bf16[128,1152]{1,0:T(8,128)(2,1)S(1)} %get-tuple-element.28), channel_id=1, source_target_pairs={{0,1},{1,0},{2,3},{3,2},{4,5},{5,4},{6,7},{7,6},{8,9},{9,8},{10,11... | collective-permute-start | bytes 884744 | tf_op jit(solution)/shard_map/ppermute | solution.py:241
  21.0 19.7 %collective-permute-start.3 = (bf16[256,1024]{1,0:T(8,128)(2,1)}, bf16[256,1024]{1,0:T(8,128)(2,1)}, u32[]{:S(2)}, u32[]{:S(2)}) collective-permute-start(bf16[256,1024]{1,0:T(8,128)(2,1)} %get-tuple-element.32), channel_id=1, source_target_pairs={{0,32},{32,0},{64,96},{96,64},{128,160},{160,128},{192,224},{224,1... | collective-permute-start | bytes 1572872 | tf_op jit(solution)/shard_map/ppermute | solution.py:230
  23.7 27.3 %all-to-all-start = ((bf16[16,8,1152]{2,1,0:T(8,128)(2,1)}), bf16[16,8,1152]{2,1,0:T(8,128)(2,1)S(1)}, u32[]{:S(2)}, u32[]{:S(2)}) async-start(bf16[16,8,1152]{2,1,0:T(8,128)(2,1)} %bitcast.2), calls=%async_computation | async-start | bytes 589824 | tf_op jit(solution)/shard_map/all_to_all | solution.py:244
  42.0 8.3 %collective-permute-start.4 = (bf16[128,1024]{1,0:T(8,128)(2,1)S(1)}, bf16[128,1024]{1,0:T(8,128)(2,1)S(1)}, u32[]{:S(2)}, u32[]{:S(2)}) collective-permute-start(bf16[128,1024]{1,0:T(8,128)(2,1)S(1)} %get-tuple-element.34), channel_id=1, source_target_pairs={{0,128},{32,160},{64,192},{96,224},{128,0},{160,32},{192,64},{224,... | collective-permute-start | bytes 786440 | tf_op jit(solution)/shard_map/ppermute | solution.py:230
  51.0 30.2 %all-to-all-start.1 = ((bf16[8,16,1024]{2,1,0:T(8,128)(2,1)}), bf16[8,16,1024]{2,1,0:T(8,128)(2,1)S(1)}, u32[]{:S(2)}, u32[]{:S(2)}) async-start(bf16[8,16,1024]{2,1,0:T(8,128)(2,1)} %bitcast.3), calls=%async_computation.1 | async-start | bytes 524288 | tf_op jit(solution)/shard_map/all_to_all | solution.py:254
  70.4 8.6 %collective-permute-start.2 = (f32[8,576]{1,0:T(8,128)S(1)}, f32[8,576]{1,0:T(8,128)S(1)}, u32[]{:S(2)}, u32[]{:S(2)}) collective-permute-start(f32[8,576]{1,0:T(8,128)S(1)} %get-tuple-element.30), channel_id=1, source_target_pairs={{32,0},{64,32},{96,64},{128,96},{160,128},{192,160},{224,192},{256... | collective-permute-start | bytes 55304 | tf_op jit(solution)/shard_map/ppermute | solution.py:36
